TPU v7x, 32 devices: a whole 2x2x4 slice. The times are simulated.
32 devices in a mesh: groups: 2 (over y), space: 4 (over z), batch: 4 (over x, core).
Axes of the slice: x: 2, y: 2, z: 4, core: 2. Of those that a mesh axis runs over, the one named last changes fastest.
Arguments:
- fields: bfloat16 [8, 32, 64, 128], P(('groups', 'batch'), 'space'), parts along dimension 0, may hold values from -36 to 36
- land: int32 [32, 64], P('space'), may hold values 0 or 1
- conv_in: bfloat16 [9, 128, 128], replicated, may hold values from -0.1875 to 0.1875
- conv_out: bfloat16 [9, 128, 128], replicated, may hold values from -0.1875 to 0.1875
- batchnorm_gain: float32 [128], replicated, may hold values from 0.25 to 1.75
- batchnorm_offset: float32 [128], replicated, may hold values from -3 to 3
- target_grad: bfloat16 [8, 32, 64, 128], P(('groups', 'batch'), 'space'), parts along dimension 0, may hold values from -6 to 6
Outputs:
- output: bfloat16 [8, 32, 64, 128], P(('groups', 'batch'), 'space'), parts along dimension 0
- grad_in: float32 [18, 128, 128], P('groups', None, 'batch'), parts along dimension 0
- grad_out: float32 [18, 128, 128], P('groups', None, 'batch'), parts along dimension 0
- gain_gradient: float32 [256], P('groups'), parts along dimension 0
- offset_gradient: float32 [256], P('groups'), parts along dimension 0
There are 2 independent parts, one for each index of `groups`. A program takes and returns all parts, laid end to end along the dimension named above; an argument that names none is the same for every part. Nothing has to cross between parts.
All inputs are finite; a program needn't handle non-finite values. No bound on the sum of `land` on one device may be relied on, other than what follows from the above.
Results may differ from a plain program's by a relative error of at most 0.025.
Values may be sent and summed in bfloat16 or wider, within the bound.
No kernel may reach another device: no remote copies, remote signals or barrier semaphores. Data moves between devices by JAX's collectives and lax.ppermute only.
A program may use at most 64 MiB of HBM per device.

v0:
```python
import functools

import jax
import jax.numpy as jnp
from jax import lax
from jax.experimental import pallas as pl
from jax.experimental.pallas import tpu as pltpu
from jax.sharding import PartitionSpec as P


F32 = jnp.float32
BF16 = jnp.bfloat16
VMEM = pl.BlockSpec(memory_space=pltpu.VMEM)


def run(body, outs, args, scratch=(), flops=0, space=VMEM, alias=None):
    nbytes = sum(a.size * a.dtype.itemsize for a in args)
    nbytes += sum(o.size * o.dtype.itemsize for o in outs)
    return pl.pallas_call(
        body,
        out_shape=list(outs),
        in_specs=[space] * len(args),
        out_specs=[VMEM] * len(outs),
        scratch_shapes=list(scratch),
        cost_estimate=pl.CostEstimate(flops=flops, bytes_accessed=nbytes, transcendentals=0),
        compiler_params=pltpu.CompilerParams(vmem_limit_bytes=24 << 20),
        input_output_aliases=alias or {},
    )(*args)


def sds(shape, dtype):
    return jax.ShapeDtypeStruct(shape, dtype)


def dot(a, b):
    return jnp.dot(a, b, preferred_element_type=F32)


def spread(line, lat, chans):
    rows = lax.broadcasted_iota(jnp.int32, (lat, lat), 0)
    cols = lax.broadcasted_iota(jnp.int32, (lat, lat), 1)
    col = jnp.sum(jnp.where(rows == cols, jnp.broadcast_to(line, (lat, lat)), 0.0), axis=1, keepdims=True)
    return jnp.broadcast_to(col, (lat, chans))


def pack_kernel(lon, lat, chans, join, f_hbm, t_hbm, land_hbm, e_ref, o_ref, p_ref, fc, fr, tc, tr, land, sems):
    copies = [
        pltpu.make_async_copy(f_hbm.at[0, 0:2], fc.at[0:2], sems.at[0]),
        pltpu.make_async_copy(f_hbm.at[0, lon - 2 : lon], fc.at[2:4], sems.at[1]),
        pltpu.make_async_copy(f_hbm.at[0, :, lat - 8 : lat], fr, sems.at[2]),
        pltpu.make_async_copy(t_hbm.at[0, 0:1], tc.at[0:1], sems.at[3]),
        pltpu.make_async_copy(t_hbm.at[0, lon - 1 : lon], tc.at[1:2], sems.at[4]),
        pltpu.make_async_copy(t_hbm.at[0, :, lat - 8 : lat], tr, sems.at[5]),
        pltpu.make_async_copy(land_hbm, land, sems.at[6]),
    ]
    for c in copies:
        c.start()
    even = lax.rem(lax.axis_index("space"), 2) == 0
    for c in copies:
        c.wait()
    lines = land[...].astype(F32)

    def edge(k, cols_f, side):
        masks = [spread(lines[i : i + 1], lat, chans) for i in cols_f]
        parts = [fc[k + n].astype(F32) * m for n, m in enumerate(masks)]
        col = cols_f[0] if side == 0 else cols_f[1]
        parts.append(tc[side].astype(F32) * masks[0 if side == 0 else 1])
        line = jnp.concatenate([lines[col : col + 1], jnp.zeros((1, chans - lat), F32)], axis=1)
        parts += [line, jnp.zeros((15, chans), F32)]
        return jnp.concatenate(parts, axis=0).astype(BF16)

    west = edge(0, (0, 1), 0)
    east = edge(2, (lon - 2, lon - 1), 1)
    n = west.shape[0]
    e_ref[...] = jnp.where(even, east, west)
    o_ref[0:n, :] = jnp.where(even, west, east)
    lane = lax.broadcasted_iota(jnp.int32, (lon, lat), 1)
    last = {}
    for j in (lat - 2, lat - 1):
        col = jnp.sum(jnp.where(lane == j, lines, 0.0), axis=1, keepdims=True)
        last[j] = jnp.broadcast_to(col, (lon, chans))
    rows = []
    for j, ref in ((lat - 2, fr), (lat - 1, fr), (lat - 1, tr)):
        k = j - (lat - 8)
        line = jnp.concatenate([ref[i].astype(F32)[k : k + 1] for i in range(lon)], axis=0)
        rows.append(line * last[j])
    rows.append(last[lat - 1])
    polar = jnp.concatenate(rows, axis=0).astype(BF16)
    p_ref[...] = polar
    if join:
        o_ref[n:, :] = polar


def shift_rows(x, step, fill):
    rows = lax.broadcasted_iota(jnp.int32, x.shape, 0)
    n = x.shape[0]
    moved = pltpu.roll(x, (-step) % n, 0)
    return jnp.where(rows == (n - 1 if step > 0 else 0), fill, moved)


def prep_kernel(
    lon, lat, chans,
    f_hbm, t_hbm, land_hbm, win_hbm, wout_hbm, gain_hbm, offset_hbm,
    ss_ref, tt_ref, mask_ref, win_ref, wout_ref, wt_ref, bn_ref,
    f_ref, t_ref, land_ref, sems,
):
    pairs = [
        (land_hbm, land_ref), (f_hbm, f_ref), (t_hbm, t_ref), (wout_hbm, wout_ref), (win_hbm, win_ref),
        (gain_hbm, bn_ref.at[0:1]), (offset_hbm, bn_ref.at[1:2]),
    ]
    copies = [pltpu.make_async_copy(src, dst, sems.at[i]) for i, (src, dst) in enumerate(pairs)]
    for c in copies:
        c.start()
    for c in copies[:3]:
        c.wait()
    lines = land_ref[...].astype(F32)
    zero = jnp.zeros((1, chans), F32)
    for i in range(lon):
        mask = spread(lines[i : i + 1], lat, chans)
        mask_ref[i * lat : (i + 1) * lat] = mask.astype(BF16)
        x = f_ref[0, i].astype(F32) * mask
        ss_ref[i + 2, :, 0:chans] = shift_rows(x, -1, zero).astype(BF16)
        ss_ref[i + 2, :, chans : 2 * chans] = x.astype(BF16)
        ss_ref[i + 2, :, 2 * chans :] = shift_rows(x, 1, zero).astype(BF16)
        x = t_ref[0, i].astype(F32) * mask
        tt_ref[i + 1, :, 0:chans] = shift_rows(x, 1, zero).astype(BF16)
        tt_ref[i + 1, :, chans : 2 * chans] = x.astype(BF16)
        tt_ref[i + 1, :, 2 * chans :] = shift_rows(x, -1, zero).astype(BF16)
    for c in copies[3:]:
        c.wait()
    for a in range(3):
        for b in range(3):
            wt_ref[a, b * chans : (b + 1) * chans] = wout_ref[3 * a + b].T


def conv_kernel(
    lon, lat, chans, moff,
    re_ref, ro_ref, rm_ref, r1_ref, r2_ref, own_ref, ss_in, tt_in, om_ref, w_ref,
    ss_ref, tt_ref, first_ref, mask_ref, stat_ref, tx_ref,
):
    even = lax.rem(lax.axis_index("space"), 2) == 0
    recv_e = re_ref[...].astype(F32)
    recv_o = ro_ref[0 : recv_e.shape[0], :].astype(F32)
    west = jnp.where(even, recv_o, recv_e)
    east = jnp.where(even, recv_e, recv_o)
    polar_m = rm_ref[moff : moff + 4 * lon, :].astype(F32)
    if r1_ref is r2_ref:
        other = r1_ref[...].astype(F32)
        own = own_ref[...].astype(F32)
        polar_1 = jnp.where(even, other, own)
        polar_2 = jnp.where(even, own, other)
    else:
        polar_1 = r1_ref[...].astype(F32)
        polar_2 = r2_ref[...].astype(F32)

    def ghost(kind, cols):
        line = jnp.concatenate([p[kind * lon : (kind + 1) * lon] for p in (polar_1, polar_m, polar_2)], axis=0)
        picks = [2 * lon - 1 - i for i in cols]
        return jnp.concatenate([line[k : k + 1] for k in picks], axis=0)

    zero = jnp.zeros((1, chans), F32)
    wide = list(range(-2, lon + 2))
    near = list(range(-1, lon + 1))
    g62, g63 = ghost(0, wide), ghost(1, wide)
    gt, gm = ghost(2, near), ghost(3, near)
    halo = {0: west[0:lat], 1: west[lat : 2 * lat], lon + 2: east[0:lat], lon + 3: east[lat : 2 * lat]}
    rows8 = lax.broadcasted_iota(jnp.int32, (8, chans), 0)
    top = []
    for k in range(lon + 4):
        fill = g63[k : k + 1]
        if k in halo:
            x = halo[k]
            ss_ref[k, :, 0:chans] = shift_rows(x, -1, zero).astype(BF16)
            ss_ref[k, :, chans : 2 * chans] = x.astype(BF16)
            ss_ref[k, :, 2 * chans :] = shift_rows(x, 1, fill).astype(BF16)
            top.append(x[lat - 1 : lat])
        else:
            tail = ss_ref[k, lat - 8 :, chans : 2 * chans].astype(F32)
            top.append(tail[7:8])
            ss_ref[k, lat - 8 :, 2 * chans :] = shift_rows(tail, 1, fill).astype(BF16)
    top = jnp.concatenate(top, axis=0)
    fold = jnp.concatenate([g62, g63, top], axis=1)
    total = None
    n = lon + 2
    pad = jnp.zeros((16 - n, 3 * chans), F32)
    for a in (-1, 0, 1):
        ghost_rows = jnp.concatenate([fold[1 - a : 1 - a + n], pad], axis=0).astype(BF16)
        piece = jnp.concatenate([ss_ref[a + 1 : a + 1 + n].reshape(n * lat, 3 * chans), ghost_rows], axis=0)
        part = dot(piece, w_ref[3 * (a + 1) : 3 * (a + 2)].reshape(3 * chans, chans))
        total = part if total is None else total + part
    first = total.astype(BF16)
    first_ref[...] = first
    own_first = first[lat : lat + lon * lat].astype(F32)
    own_mask = om_ref[...].astype(F32)
    kept = own_first * own_mask
    sums = jnp.sum(kept, axis=0, keepdims=True)
    squares = jnp.sum(kept * own_first, axis=0, keepdims=True)
    count = jnp.sum(own_mask, axis=0, keepdims=True)
    stat_ref[...] = jnp.concatenate([sums, squares, count, jnp.zeros((5, chans), F32)], axis=0)
    edges = [spread(x[3 * lat : 3 * lat + 1, 0:lat], lat, chans) for x in (west, east)]
    mask_ref[0:lat] = edges[0].astype(BF16)
    mask_ref[lat : lat + lon * lat] = om_ref[...]
    mask_ref[lat + lon * lat : n * lat] = edges[1].astype(BF16)
    mask_ref[n * lat :] = jnp.concatenate([gm, jnp.zeros((16 - n, chans), F32)], axis=0).astype(BF16)
    for k, x in ((0, west[2 * lat : 3 * lat]), (lon + 1, east[2 * lat : 3 * lat])):
        tt_ref[k, :, 0:chans] = shift_rows(x, 1, zero).astype(BF16)
        tt_ref[k, :, chans : 2 * chans] = x.astype(BF16)
        tt_ref[k, :, 2 * chans :] = shift_rows(x, -1, zero).astype(BF16)
    tx_ref[...] = jnp.concatenate([gt, jnp.zeros((16 - n, chans), F32)], axis=0)


def adjoint_kernel(lon, lat, chans, tt_ref, tx_ref, wt_ref, dact_ref):
    gt = tx_ref[...]
    total = None
    for a in (-1, 0, 1):
        extra = jnp.concatenate([gt[1 + a : 1 + a + lon], jnp.zeros((16 - lon, chans), F32)], axis=0)
        extra = jnp.concatenate([jnp.zeros((16, 2 * chans), F32), extra], axis=1).astype(BF16)
        piece = jnp.concatenate([tt_ref[1 - a : 1 - a + lon].reshape(lon * lat, 3 * chans), extra], axis=0)
        part = dot(piece, wt_ref[a + 1])
        total = part if total is None else total + part
    rows = lax.broadcasted_iota(jnp.int32, (lat, chans), 0)
    for i in range(lon):
        add = total[lon * lat + i : lon * lat + i + 1]
        dact_ref[i * lat : (i + 1) * lat, :] = total[i * lat : (i + 1) * lat] + jnp.where(rows == lat - 1, add, 0.0)


def moments(stat_ref):
    count = stat_ref[2:3, :]
    mean = stat_ref[0:1, :] / count
    var = stat_ref[1:2, :] / count - mean * mean
    return count, mean, lax.rsqrt(var + 1e-05)


def act_kernel(lon, lat, chans, first_ref, mask_ref, stat_ref, bn_ref, dact_ref, gsum_ref, dpre_ref, aa_ref):
    count, mean, rstd = moments(stat_ref)
    gain, offset = bn_ref[0:1, :], bn_ref[1:2, :]

    def forward(lo, hi):
        xhat = (first_ref[lo:hi].astype(F32) - mean) * rstd
        u = gain * xhat + offset
        hyper = jnp.tanh(0.7978845608 * (u + 0.044715 * u * u * u))
        m = mask_ref[lo:hi].astype(F32)
        return xhat, u, hyper, m, 0.5 * u * (1.0 + hyper) * m

    n = lon + 2
    zero = jnp.zeros((1, chans), F32)
    ghost = forward(n * lat, n * lat + 16)[4]
    scale = lax.rsqrt(count)
    goff = jnp.zeros((1, chans), F32)
    ggain = jnp.zeros((1, chans), F32)
    for k in range(n):
        xhat, u, hyper, m, act = forward(k * lat, (k + 1) * lat)
        aa_ref[k, :, 0:chans] = shift_rows(act, -1, zero).astype(BF16)
        aa_ref[k, :, chans : 2 * chans] = act.astype(BF16)
        aa_ref[k, :, 2 * chans :] = shift_rows(act, 1, ghost[k : k + 1]).astype(BF16)
        if 0 < k <= lon:
            slope = 0.5 * (1.0 + hyper) + 0.5 * u * (1.0 - hyper * hyper) * 0.7978845608 * (
                1.0 + 3.0 * 0.044715 * u * u
            )
            rows = slice((k - 1) * lat, k * lat)
            dpre = dact_ref[rows] * scale * m * slope
            dpre_ref[rows] = dpre
            goff = goff + jnp.sum(dpre, axis=0, keepdims=True)
            ggain = ggain + jnp.sum(dpre * xhat, axis=0, keepdims=True)
    gsum_ref[...] = jnp.concatenate([goff, ggain, jnp.zeros((6, chans), F32)], axis=0)


def put_taps(grad_ref, grad, shifted_ref, base, lon, lat, chans):
    chunks, width = grad_ref.shape[0], grad_ref.shape[2]
    turned = grad.T
    for a in (-1, 0, 1):
        piece = shifted_ref[base + a : base + a + lon].reshape(lon * lat, 3 * chans)
        part = dot(turned, piece).astype(BF16)
        for b in range(3):
            for c in range(chunks):
                grad_ref[c, 3 * (a + 1) + b] = part[c * width : (c + 1) * width, b * chans : (b + 1) * chans]


def out_kernel(lon, lat, chans, aa_ref, mask_ref, tt_ref, stat_ref, w_ref, out_ref, grad_ref):
    total = None
    for a in (-1, 0, 1):
        piece = aa_ref[a + 1 : a + 1 + lon].reshape(lon * lat, 3 * chans)
        part = dot(piece, w_ref[3 * (a + 1) : 3 * (a + 2)].reshape(3 * chans, chans))
        total = part if total is None else total + part
    own_mask = mask_ref[lat : lat + lon * lat].astype(F32)
    out_ref[...] = (total * own_mask).astype(BF16).reshape(1, lon, lat, chans)
    scale = lax.rsqrt(stat_ref[2:3, :])
    target = tt_ref[1 : 1 + lon, :, chans : 2 * chans].reshape(lon * lat, chans).astype(F32)
    dout = (target * scale).astype(BF16)
    put_taps(grad_ref, dout, aa_ref, 1, lon, lat, chans)


def in_kernel(lon, lat, chans, first_ref, mask_ref, stat_ref, bn_ref, dpre_ref, gsum_ref, ss_ref, grad_ref):
    count, mean, rstd = moments(stat_ref)
    goff, ggain = gsum_ref[0:1, :], gsum_ref[1:2, :]
    own = slice(lat, lat + lon * lat)
    xhat = (first_ref[own].astype(F32) - mean) * rstd
    dfirst = mask_ref[own].astype(F32) * (bn_ref[0:1, :] * rstd) * (dpre_ref[...] - (goff + xhat * ggain) / count)
    put_taps(grad_ref, dfirst.astype(BF16), ss_ref, 2, lon, lat, chans)


def xor_pairs(size, k):
    return [(i, i ^ k) for i in range(size)]


def all_sum(x, axis):
    size = lax.axis_size(axis)
    bit = 1
    while bit < size:
        other = lax.ppermute(x, axis, xor_pairs(size, bit))
        if 2 * bit < size:
            far = lax.ppermute(x, axis, xor_pairs(size, 2 * bit))
            both = lax.ppermute(x, axis, xor_pairs(size, 3 * bit))
            x = (x + other) + (far + both)
        else:
            x = x + other
        bit *= 4
    return x


def scatter_sum(x, axis, last=BF16):
    size = lax.axis_size(axis)
    me = lax.axis_index(axis)
    bit = 1
    while bit < size:
        mine = (me // bit) % 2
        split = x.reshape(x.shape[0] // 2, 2, *x.shape[1:])
        keep = lax.dynamic_index_in_dim(split, mine, 1, keepdims=False)
        send = lax.dynamic_index_in_dim(split, 1 - mine, 1, keepdims=False)
        got = lax.ppermute(send, axis, xor_pairs(size, bit))
        bit *= 2
        x = (keep.astype(F32) + got.astype(F32)).astype(BF16 if bit < size else last)
    return x[0]


def space_sum(x):
    size = lax.axis_size("space")
    bit = 1
    while bit < size:
        got = lax.ppermute(x, "space", xor_pairs(size, bit))
        x = x.astype(F32) + got.astype(F32)
        bit *= 2
        if bit < size:
            x = x.astype(BF16)
    return jnp.swapaxes(x, 1, 2)


def put_shifted(ref, k, x, step):
    chans = x.shape[1]
    zero = jnp.zeros((1, chans), F32)
    ref[k, :, 0:chans] = shift_rows(x, -step, zero).astype(BF16)
    ref[k, :, chans : 2 * chans] = x.astype(BF16)
    ref[k, :, 2 * chans :] = shift_rows(x, step, zero).astype(BF16)


def join_kernel(a_ref, b_ref, out_ref):
    rows = a_ref.shape[0]
    out_ref[0:rows] = a_ref[...]
    out_ref[rows:] = b_ref[...]


def sample_prep(
    lon, lat, chans, tiles,
    f_hbm, t_hbm, land_hbm, win_hbm, wout_hbm, gain_hbm, offset_hbm,
    ss_ref, tt_ref, mask_ref, target_ref, land_ref, win_ref, wout_ref, wt_ref, bn_ref,
    f_ref, t_ref, sems,
):
    pairs = [
        (land_hbm, land_ref), (f_hbm, f_ref), (t_hbm, t_ref), (wout_hbm, wout_ref), (win_hbm, win_ref),
        (gain_hbm, bn_ref.at[0:1]), (offset_hbm, bn_ref.at[1:2]),
    ]
    copies = [pltpu.make_async_copy(src, dst, sems.at[i]) for i, (src, dst) in enumerate(pairs)]
    for c in copies:
        c.start()
    first = lax.axis_index("space") * lon
    for c in copies[:3]:
        c.wait()
    lines = land_ref[...].astype(F32)
    for i in range(lon):
        mask = spread(lines[i : i + 1], lat, chans)
        mask_ref[first + i] = mask.astype(BF16)
        put_shifted(ss_ref, first + i + 1, f_ref[0, i].astype(F32) * mask, 1)
        target = t_ref[0, i].astype(F32) * mask
        target_ref[0, i] = target.astype(BF16)
        put_shifted(tt_ref, first + i + 1, target, -1)
    for c in copies[3:]:
        c.wait()
    for a in range(3):
        for b in range(3):
            wt_ref[a, b * chans : (b + 1) * chans] = wout_ref[3 * a + b].T


def sample_build(lon, lat, chans, f1_ref, f2_ref, l2_ref, l13_ref, ss_in, mask_in, ss_ref, mask_ref):
    me = lax.axis_index("space")
    for k, f_ref, land_ref in ((1, f1_ref, l13_ref), (2, f2_ref, l2_ref), (3, None, l13_ref)):
        first = jnp.bitwise_xor(me, k) * lon
        lines = land_ref[lon if k == 3 else 0 : 2 * lon if k == 3 else lon].astype(F32)
        for i in range(lon):
            mask = spread(lines[i : i + 1], lat, chans)
            mask_ref[first + i] = mask.astype(BF16)
            if f_ref is not None:
                put_shifted(ss_ref, first + i + 1, f_ref[0, i].astype(F32) * mask, 1)


def sample_conv(lon, lat, chans, f3_ref, ss_in, mask_ref, w_ref, ss_ref, first_ref, stat_ref):
    nx = mask_ref.shape[0]
    start = jnp.bitwise_xor(lax.axis_index("space"), 3) * lon
    for i in range(lon):
        put_shifted(ss_ref, start + i + 1, f3_ref[0, i].astype(F32) * mask_ref[start + i].astype(F32), 1)
    tails = [ss_ref[i + 1, lat - 8 :, chans : 2 * chans].astype(F32) for i in range(nx)]
    for i in range(nx):
        fill = tails[nx - 1 - i][7:8]
        ss_ref[i + 1, lat - 8 :, 2 * chans :] = shift_rows(tails[i], 1, fill).astype(BF16)
    ss_ref[0] = ss_ref[nx]
    ss_ref[nx + 1] = ss_ref[1]
    sums, squares, count = [jnp.zeros((8, chans), F32)] * 3
    step = 8
    for c in range(0, nx, step):
        total = None
        for a in (-1, 0, 1):
            piece = ss_ref[c + a + 1 : c + a + 1 + step].reshape(step * lat, 3 * chans)
            part = dot(piece, w_ref[3 * (a + 1) : 3 * (a + 2)].reshape(3 * chans, chans))
            total = part if total is None else total + part
        first = total.astype(BF16)
        first_ref[c : c + step] = first.reshape(step, lat, chans)
        x = first.astype(F32)
        m = mask_ref[c : c + step].reshape(step * lat, chans).astype(F32)
        kept = x * m
        fold = lambda v: jnp.sum(v.reshape(-1, 8, chans), axis=0)
        sums, squares, count = sums + fold(kept), squares + fold(kept * x), count + fold(m)
    rows = [jnp.sum(v, axis=0, keepdims=True) for v in (sums, squares, count)]
    stat_ref[...] = jnp.concatenate(rows + [jnp.zeros((5, chans), F32)], axis=0)


def sample_adjoint(lon, lat, chans, t1_ref, t2_ref, t3_ref, wt_ref, tt_in, tt_ref, dact_ref):
    nx = dact_ref.shape[0]
    me = lax.axis_index("space")
    for k, t_ref in ((1, t1_ref), (2, t2_ref), (3, t3_ref)):
        start = jnp.bitwise_xor(me, k) * lon
        for i in range(lon):
            put_shifted(tt_ref, start + i + 1, t_ref[0, i].astype(F32), -1)
    tt_ref[0] = tt_ref[nx]
    tt_ref[nx + 1] = tt_ref[1]
    top = [tt_ref[i + 1, lat - 8 :, chans : 2 * chans].astype(F32)[7:8] for i in range(nx)]
    extra = None
    for a in (-1, 0, 1):
        rows = jnp.concatenate([top[nx - 1 - (i + a) % nx] for i in range(nx)], axis=0).astype(BF16)
        part = dot(rows, wt_ref[a + 1, 2 * chans :])
        extra = part if extra is None else extra + part
    last = lax.broadcasted_iota(jnp.int32, (lat, chans), 0) == lat - 1
    step = 8
    for c in range(0, nx, step):
        total = None
        for a in (-1, 0, 1):
            piece = tt_ref[c + 1 - a : c + 1 - a + step].reshape(step * lat, 3 * chans)
            part = dot(piece, wt_ref[a + 1])
            total = part if total is None else total + part
        for i in range(step):
            add = jnp.where(last, extra[c + i : c + i + 1], 0.0)
            dact_ref[c + i] = total[i * lat : (i + 1) * lat] + add


def sample_act(lat, chans, first_ref, mask_ref, stat_ref, bn_ref, dact_ref, gsum_ref, dpre_ref, aa_ref):
    nx = mask_ref.shape[0]
    count, mean, rstd = moments(stat_ref)
    gain, offset = bn_ref[0:1, :], bn_ref[1:2, :]
    scale = lax.rsqrt(count)
    fold = lambda v: jnp.sum(v.reshape(-1, 8, chans), axis=0)
    goff, ggain = [jnp.zeros((8, chans), F32)] * 2
    for i in range(nx // 2):
        acts = []
        for k in (i, nx - 1 - i):
            xhat = (first_ref[k].astype(F32) - mean) * rstd
            u = gain * xhat + offset
            square = u * u
            hyper = jnp.tanh(0.7978845608 * (u + 0.044715 * square * u))
            m = mask_ref[k].astype(F32)
            half = 0.5 * (1.0 + hyper)
            acts.append(u * half * m)
            slope = half + 0.5 * u * (1.0 - hyper * hyper) * 0.7978845608 * (1.0 + 3.0 * 0.044715 * square)
            dpre = dact_ref[k] * scale * m * slope
            dpre_ref[k] = dpre
            goff, ggain = goff + fold(dpre), ggain + fold(dpre * xhat)
        for k, x, other in ((i, acts[0], acts[1]), (nx - 1 - i, acts[1], acts[0])):
            aa_ref[k + 1, :, 0:chans] = shift_rows(x, -1, jnp.zeros((1, chans), F32)).astype(BF16)
            aa_ref[k + 1, :, chans : 2 * chans] = x.astype(BF16)
            aa_ref[k + 1, :, 2 * chans :] = shift_rows(x, 1, other[lat - 1 : lat]).astype(BF16)
    aa_ref[0] = aa_ref[nx]
    aa_ref[nx + 1] = aa_ref[1]
    rows = [jnp.sum(v, axis=0, keepdims=True) for v in (goff, ggain)]
    gsum_ref[...] = jnp.concatenate(rows + [jnp.zeros((6, chans), F32)], axis=0)


def halve(get, keep_ref, send_ref, bit):
    mine = lax.rem(lax.div(lax.axis_index("batch"), bit), 2)
    for j in range(keep_ref.shape[0]):
        keep_ref[j] = get(2 * j + mine)
        send_ref[j] = get(2 * j + 1 - mine)


def fold_kernel(bit, a_ref, b_ref, keep_ref, send_ref):
    halve(lambda k: (a_ref[k].astype(F32) + b_ref[k].astype(F32)).astype(BF16), keep_ref, send_ref, bit)


def exchange_sum(keep, send, size):
    bit = 1
    while True:
        got = lax.ppermute(send, "batch", xor_pairs(size, bit))
        bit *= 2
        if bit == size:
            return jnp.swapaxes(keep[0].astype(F32) + got[0].astype(F32), 1, 2), keep
        half = sds((keep.shape[0] // 2,) + keep.shape[1:], BF16)
        keep, send = run(functools.partial(fold_kernel, bit), [half, half], [keep, got])


def sample_grad(lat, chans, aa_ref, tt_ref, stat_ref, keep_ref, send_ref, grad_ref):
    nx = aa_ref.shape[0] - 2
    scale = lax.rsqrt(stat_ref[2:3, :])
    target = tt_ref[1 : 1 + nx, :, chans : 2 * chans].reshape(nx * lat, chans).astype(F32)
    put_taps(grad_ref, (target * scale).astype(BF16), aa_ref, 1, nx, lat, chans)
    halve(lambda k: grad_ref[k], keep_ref, send_ref, 1)


def sample_out(lon, lat, chans, aa_ref, mask_ref, w_ref, after_ref, out_ref):
    start = lax.axis_index("space") * lon
    total = None
    for a in (-1, 0, 1):
        piece = aa_ref[pl.ds(start + a + 1, lon)].reshape(lon * lat, 3 * chans)
        part = dot(piece, w_ref[3 * (a + 1) : 3 * (a + 2)].reshape(3 * chans, chans))
        total = part if total is None else total + part
    own_mask = mask_ref[pl.ds(start, lon)].reshape(lon * lat, chans).astype(F32)
    out_ref[...] = (total * own_mask).astype(BF16).reshape(1, lon, lat, chans)


def sample_in(lat, chans, first_ref, mask_ref, stat_ref, bn_ref, dpre_ref, gsum_ref, ss_ref, keep_ref, send_ref, grad_ref):
    nx = mask_ref.shape[0]
    count, mean, rstd = moments(stat_ref)
    goff, ggain = gsum_ref[0:1, :] / count, gsum_ref[1:2, :] / count
    factor = bn_ref[0:1, :] * rstd
    rows = []
    for k in range(nx):
        xhat = (first_ref[k].astype(F32) - mean) * rstd
        rows.append((mask_ref[k].astype(F32) * factor * (dpre_ref[k] - (goff + xhat * ggain))).astype(BF16))
    put_taps(grad_ref, jnp.concatenate(rows, axis=0), ss_ref, 1, nx, lat, chans)
    halve(lambda k: grad_ref[k], keep_ref, send_ref, 1)


def tile_body(fields, land, conv_in, conv_out, batchnorm_gain, batchnorm_offset, target_grad):
    lon, lat, chans = fields.shape[1:]
    tiles = lax.axis_size("space")
    sizes = (lon, lat, chans)
    cells = lon * lat
    gain, offset = batchnorm_gain[None, :], batchnorm_offset[None, :]
    fields, land, conv_in, conv_out, target_grad, gain, offset = (
        pltpu.with_memory_space_constraint(x, pltpu.HBM)
        for x in (fields, land, conv_in, conv_out, target_grad, gain, offset)
    )
    n = lon + 2
    join = tiles == 4
    edge = 3 * lat + 16
    shares = lax.axis_size("batch")
    taps = sds((shares, 9, chans // shares, chans), BF16)
    pay_e, pay_o, polar = run(
        functools.partial(pack_kernel, *sizes, join),
        [sds((edge, chans), BF16), sds((edge + (4 * lon if join else 0), chans), BF16), sds((4 * lon, chans), BF16)],
        [fields, target_grad, land],
        scratch=[
            pltpu.VMEM((4, lat, chans), BF16), pltpu.VMEM((lon, 8, chans), BF16),
            pltpu.VMEM((2, lat, chans), BF16), pltpu.VMEM((lon, 8, chans), BF16),
            pltpu.VMEM((lon, lat), jnp.int32), pltpu.SemaphoreType.DMA((7,)),
        ],
        space=pl.BlockSpec(memory_space=pltpu.HBM),
    )
    mirror = [(i, tiles - 1 - i) for i in range(tiles)]
    got_o = lax.ppermute(pay_o, "space", [(i, (i - 1 if i % 2 == 0 else i + 1) % tiles) for i in range(tiles)])
    got_e = lax.ppermute(pay_e, "space", xor_pairs(tiles, 1))
    if join:
        got_x = lax.ppermute(polar, "space", xor_pairs(tiles, 2))
        poles = [got_o, got_x, got_x, polar]
    else:
        poles = [
            lax.ppermute(polar, "space", mirror),
            lax.ppermute(polar, "space", [(i, (tiles - 2 - i) % tiles) for i in range(tiles)]),
            lax.ppermute(polar, "space", [(i, (tiles - i) % tiles) for i in range(tiles)]),
            polar,
        ]
    wide = sds((lon + 4, lat, 3 * chans), BF16)
    near = sds((n, lat, 3 * chans), BF16)
    ss, tt, own_mask, win, wout, wt, bn = run(
        functools.partial(prep_kernel, *sizes),
        [
            wide, near, sds((cells, chans), BF16), sds(conv_in.shape, BF16), sds(conv_out.shape, BF16),
            sds((3, 3 * chans, chans), BF16), sds((8, chans), F32),
        ],
        [fields, target_grad, land, conv_in, conv_out, gain, offset],
        scratch=[
            pltpu.VMEM(fields.shape, BF16), pltpu.VMEM(fields.shape, BF16), pltpu.VMEM(land.shape, jnp.int32),
            pltpu.SemaphoreType.DMA((7,)),
        ],
        space=pl.BlockSpec(memory_space=pltpu.HBM),
    )

    def conv_body(*refs):
        refs = list(refs)
        if join:
            refs[4] = refs[3]
        conv_kernel(*sizes, edge if join else 0, *refs)

    rows = n * lat + 16
    ss, tt, first, mask, stat, tx = run(
        conv_body,
        [wide, near, sds((rows, chans), BF16), sds((rows, chans), BF16), sds((8, chans), F32), sds((16, chans), F32)],
        [got_e, got_o, *poles, ss, tt, own_mask, win],
        flops=2 * rows * 9 * chans * chans,
        alias={6: 0, 7: 1},
    )
    stat = all_sum(all_sum(stat, "batch"), "space")
    dact = run(
        functools.partial(adjoint_kernel, *sizes),
        [sds((cells, chans), F32)],
        [tt, tx, wt],
        flops=2 * cells * 9 * chans * chans,
    )[0]
    gsum, dpre, aa = run(
        functools.partial(act_kernel, *sizes),
        [sds((8, chans), F32), sds((cells, chans), F32), sds((n, lat, 3 * chans), BF16)],
        [first, mask, stat, bn, dact],
    )
    gsum = all_sum(all_sum(gsum, "batch"), "space")
    output, part_out = run(
        functools.partial(out_kernel, *sizes),
        [sds((1, lon, lat, chans), BF16), taps],
        [aa, mask, tt, stat, wout],
        flops=4 * cells * 9 * chans * chans,
    )
    grad_out = space_sum(scatter_sum(part_out, "batch"))
    part_in = run(
        functools.partial(in_kernel, *sizes),
        [taps],
        [first, mask, stat, bn, dpre, gsum, ss],
        flops=2 * cells * 9 * chans * chans,
    )[0]
    grad_in = space_sum(scatter_sum(part_in, "batch"))
    return (output, grad_in, grad_out, gsum[1], gsum[0])


def sample_body(fields, land, conv_in, conv_out, batchnorm_gain, batchnorm_offset, target_grad):
    lon, lat, chans = fields.shape[1:]
    tiles = lax.axis_size("space")
    sizes = (lon, lat, chans)
    nx = tiles * lon
    near, across = xor_pairs(tiles, 1), xor_pairs(tiles, 2)
    move = lambda x, pairs: lax.ppermute(x, "space", pairs)
    f2 = move(fields, across)
    l2 = move(land, across)
    f1 = move(fields, near)
    f3 = move(f2, near)
    gain, offset = batchnorm_gain[None, :], batchnorm_offset[None, :]
    params = [
        pltpu.with_memory_space_constraint(x, pltpu.HBM)
        for x in (fields, target_grad, land, conv_in, conv_out, gain, offset)
    ]
    shares = lax.axis_size("batch")
    half = sds((shares // 2, 9, chans // shares, chans), BF16)
    whole = [pltpu.VMEM((shares, 9, chans // shares, chans), BF16)]
    shifted = sds((nx + 2, lat, 3 * chans), BF16)
    cells = sds((nx, lat, chans), BF16)
    cells_f = sds((nx, lat, chans), F32)
    sums = sds((8, chans), F32)
    work = 2 * nx * lat * 9 * chans * chans
    ss, tt, mask, target, land_own, win, wout, wt, bn = run(
        functools.partial(sample_prep, *sizes, tiles),
        [shifted, shifted, cells, sds(target_grad.shape, BF16), sds(land.shape, jnp.int32), sds(conv_in.shape, BF16), sds(conv_out.shape, BF16), sds((3, 3 * chans, chans), BF16), sums],
        params,
        scratch=[
            pltpu.VMEM(fields.shape, BF16), pltpu.VMEM(fields.shape, BF16), pltpu.SemaphoreType.DMA((7,)),
        ],
        space=pl.BlockSpec(memory_space=pltpu.HBM),
    )
    (both,) = run(join_kernel, [sds((2 * lon, lat), jnp.int32)], [land_own, l2])
    l13 = move(both, near)
    ss, mask = run(
        functools.partial(sample_build, *sizes), [shifted, cells], [f1, f2, l2, l13, ss, mask], alias={4: 0, 5: 1}
    )
    t2 = move(target, across)
    t1 = move(target, near)
    t3 = move(t2, near)
    ss, first, stat = run(
        functools.partial(sample_conv, *sizes), [shifted, cells, sums], [f3, ss, mask, win], flops=work, alias={1: 0}
    )
    stat = all_sum(stat, "batch")
    tt, dact = run(
        functools.partial(sample_adjoint, *sizes), [shifted, cells_f], [t1, t2, t3, wt, tt], flops=work, alias={4: 0}
    )
    gsum, dpre, aa = run(
        functools.partial(sample_act, lat, chans), [sums, cells_f, shifted], [first, mask, stat, bn, dact]
    )
    gsum = all_sum(gsum, "batch")
    keep_o, send_o = run(
        functools.partial(sample_grad, lat, chans), [half, half], [aa, tt, stat], scratch=whole, flops=work
    )
    grad_out, _ = exchange_sum(keep_o, send_o, shares)
    keep_i, send_i = run(
        functools.partial(sample_in, lat, chans),
        [half, half], [first, mask, stat, bn, dpre, gsum, ss], scratch=whole, flops=work,
    )
    grad_in, folded = exchange_sum(keep_i, send_i, shares)
    (output,) = run(
        functools.partial(sample_out, *sizes), [sds(fields.shape, BF16)], [aa, mask, wout, folded], flops=work // tiles
    )
    return (output, grad_in, grad_out, gsum[1], gsum[0])


def body(*args):
    if lax.axis_size("space") != 4:
        return tile_body(*args)
    return sample_body(*args)


def solution(mesh):
    in_specs = (
        P(("groups", "batch"), "space", None, None),
        P("space", None),
        P(),
        P(),
        P(),
        P(),
        P(("groups", "batch"), "space", None, None),
    )
    out_specs = (
        P(("groups", "batch"), "space", None, None),
        P("groups", None, "batch"),
        P("groups", None, "batch"),
        P("groups"),
        P("groups"),
    )
    return jax.shard_map(body, mesh=mesh, in_specs=in_specs, out_specs=out_specs, check_vma=False)
```

profile of v0, /device:TPU:0, one launch (start us, length us, event | category | flops | bytes accessed | tf_op | source)
XLA Modules:
  0.0 49.4 jit_solution(2452694859483863664)
XLA Ops:
  0.6 4.1 %collective-permute-start = (bf16[1,8,64,128]{3,2,1,0:T(8,128)(2,1)}, bf16[1,8,64,128]{3,2,1,0:T(8,128)(2,1)S(1)}, u32[]{:S(2)}, u32[]{:S(2)}) collective-permute-start(bf16[1,8,64,128]{3,2,1,0:T(8,128)(2,1)} %f_hbm.1), channel_id=1, source_target_pairs={{0,8},{4,12},{8,0},{12,4},{1,9},{5,13},{9,1},{13,5},{2,10},{6,14},... | collective-permute-start | bytes 393224 | tf_op jit(solution)/shard_map/ppermute | solution.py:653
  4.8 1.4 %shard_map.110 = (bf16[34,64,384]{2,1,0:T(8,128)(2,1)S(1)}, bf16[34,64,384]{2,1,0:T(8,128)(2,1)S(1)}, bf16[32,64,128]{2,1,0:T(8,128)(2,1)S(1)}, bf16[1,8,64,128]...) custom-call(bf16[1,8,64,128]{3,2,1,0:T(8,128)(2,1)} %f_hbm.1, ...), custom_call_target="tpu_custom_call" | custom-call | bytes 5743616 | tf_op jit(solution)/shard_map/pallas_call | solution.py:19
  6.3 1.9 %collective-permute-start.2 = (bf16[1,8,64,128]{3,2,1,0:T(8,128)(2,1)}, bf16[1,8,64,128]{3,2,1,0:T(8,128)(2,1)S(1)}, u32[]{:S(2)}, u32[]{:S(2)}) collective-permute-start(bf16[1,8,64,128]{3,2,1,0:T(8,128)(2,1)} %f_hbm.1), channel_id=1, source_target_pairs={{0,4},{4,0},{8,12},{12,8},{1,5},{5,1},{9,13},{13,9},{2,6},{6,2},{1... | collective-permute-start | bytes 393224 | tf_op jit(solution)/shard_map/ppermute | solution.py:653
  8.2 6.7 %collective-permute-done.f2_ref = bf16[1,8,64,128]{3,2,1,0:T(8,128)(2,1)S(1)} collective-permute-done((bf16[1,8,64,128]{3,2,1,0:T(8,128)(2,1)}, bf16[1,8,64,128]{3,2,1,0:T(8,128)(2,1)S(1)}, u32[]{:S(2)}, u32[]{:S(2)}) %collective-permute-start) | collective-permute-done | bytes 131104 | tf_op jit(solution)/shard_map/ppermute | solution.py:653
  14.9 0.1 collective-permute-start.1
  15.1 1.9 %collective-permute-start.8 = (bf16[1,8,64,128]{3,2,1,0:T(8,128)(2,1)S(1)}, bf16[1,8,64,128]{3,2,1,0:T(8,128)(2,1)S(1)}, u32[]{:S(2)}, u32[]{:S(2)}) collective-permute-start(bf16[1,8,64,128]{3,2,1,0:T(8,128)(2,1)S(1)} %get-tuple-element.41), channel_id=1, source_target_pairs={{0,4},{4,0},{8,12},{12,8},{1,5},{5,1},{9,13},{13,9},{2,6},{6,2},{1... | collective-permute-start | bytes 393224 | tf_op jit(solution)/shard_map/ppermute | solution.py:653
  17.0 0.7 %collective-permute-start.10 = (bf16[1,8,64,128]{3,2,1,0:T(8,128)(2,1)S(1)}, bf16[1,8,64,128]{3,2,1,0:T(8,128)(2,1)S(1)}, u32[]{:S(2)}, u32[]{:S(2)}) collective-permute-start(bf16[1,8,64,128]{3,2,1,0:T(8,128)(2,1)S(1)} %collective-permute-done.9.t2_ref), channel_id=1, source_target_pairs={{0,4},{4,0},{8,12},{12,8},{1,5},{5,1},{9,13},{13,9},{2,6},{6,2},{1... | collective-permute-start | bytes 393224 | tf_op jit(solution)/shard_map/ppermute | solution.py:653
  17.7 3.4 %collective-permute-start.3 = (s32[8,64]{1,0:T(8,128)}, s32[8,64]{1,0:T(8,128)S(1)}, u32[]{:S(2)}, u32[]{:S(2)}) collective-permute-start(s32[8,64]{1,0:T(8,128)} %land_hbm.1), channel_id=1, source_target_pairs={{0,8},{4,12},{8,0},{12,4},{1,9},{5,13},{9,1},{13,5},{2,10},{6,14},... | collective-permute-start | bytes 6152 | tf_op jit(solution)/shard_map/ppermute | solution.py:653
  21.1 2.5 %collective-permute-done.3.b_ref.l2_ref = s32[8,64]{1,0:T(8,128)S(1)} collective-permute-done((s32[8,64]{1,0:T(8,128)}, s32[8,64]{1,0:T(8,128)S(1)}, u32[]{:S(2)}, u32[]{:S(2)}) %collective-permute-start.3) | collective-permute-done | bytes 2080 | tf_op jit(solution)/shard_map/ppermute | solution.py:653
  23.6 4.0 %collective-permute-start.4 = (s32[16,64]{1,0:T(8,128)S(1)}, s32[16,64]{1,0:T(8,128)S(1)}, u32[]{:S(2)}, u32[]{:S(2)}) collective-permute-start(s32[16,64]{1,0:T(8,128)S(1)} %shard_map.111), channel_id=1, source_target_pairs={{0,4},{4,0},{8,12},{12,8},{1,5},{5,1},{9,13},{13,9},{2,6},{6,2},{1... | collective-permute-start | bytes 12296 | tf_op jit(solution)/shard_map/ppermute | solution.py:653
  27.6 1.6 %collective-permute-done.4.l13_ref = s32[16,64]{1,0:T(8,128)S(1)} collective-permute-done((s32[16,64]{1,0:T(8,128)S(1)}, s32[16,64]{1,0:T(8,128)S(1)}, u32[]{:S(2)}, u32[]{:S(2)}) %collective-permute-start.4) | collective-permute-done | bytes 4128 | tf_op jit(solution)/shard_map/ppermute | solution.py:653
  29.3 0.3 shard_map.112
  29.6 1.5 %shard_map.113 = (bf16[34,64,384]{2,1,0:T(8,128)(2,1)S(1)}, bf16[32,64,128]{2,1,0:T(8,128)(2,1)S(1)}, f32[8,128]{1,0:T(8,128)S(1)}) custom-call(bf16[1,8,64,128]{3,2,1,0:T(8,128)(2,1)S(1)} %collective-permute-done.1.f3_ref, bf16[34,64,384]{2,1,0:T(8,128)(2,1)S(1)} %get-tuple-element.35.ss_in, ...), custom_call_target="tpu_custom_call", output_to_operand_aliasing={{0}: (1, {})} | custom-call | flops 603979776 | bytes 4820992 | tf_op jit(solution)/shard_map/pallas_call | solution.py:19
  31.2 1.6 %collective-permute-start.6 = (f32[8,128]{1,0:T(8,128)S(1)}, f32[8,128]{1,0:T(8,128)S(1)}, u32[]{:S(2)}, u32[]{:S(2)}) collective-permute-start(f32[8,128]{1,0:T(8,128)S(1)} %get-tuple-element.39), channel_id=1, source_target_pairs={{0,2},{1,3},{2,0},{3,1},{4,6},{5,7},{6,4},{7,5},{8,10},{9,11},{10,... | collective-permute-start | bytes 12296 | tf_op jit(solution)/shard_map/ppermute | solution.py:312
  32.8 0.3 collective-permute-start.5
  33.1 1.6 %shard_map.114 = (bf16[34,64,384]{2,1,0:T(8,128)(2,1)S(1)}, f32[32,64,128]{2,1,0:T(8,128)S(1)}) custom-call(bf16[1,8,64,128]{3,2,1,0:T(8,128)(2,1)S(1)} %collective-permute-done.8.t1_ref, bf16[1,8,64,128]{3,2,1,0:T(8,128)(2,1)S(1)} %collective-permute-done.9.t2_ref, ...), custom_call_target="tpu_custom_call", output_to_operand_aliasing={{0}: (4, {})} | custom-call | flops 603979776 | bytes 5079040 | tf_op jit(solution)/shard_map/pallas_call | solution.py:19
  34.7 0.2 collective-permute-done.6
  34.9 1.4 %shard_map.115 = (f32[8,128]{1,0:T(8,128)S(1)}, f32[32,64,128]{2,1,0:T(8,128)S(1)}, bf16[34,64,384]{2,1,0:T(8,128)(2,1)S(1)}) custom-call(bf16[32,64,128]{2,1,0:T(8,128)(2,1)S(1)} %get-tuple-element.38.first_ref, bf16[32,64,128]{2,1,0:T(8,128)(2,1)S(1)} %get-tuple-element.36.mask_ref, f32[8,128]{1,0:T(8,128)S(1)} %add_add_fusion.1.stat_ref, ...), custom_call_target="tpu_custom_call" | custom-call | bytes 4829184 | tf_op jit(solution)/shard_map/pallas_call | solution.py:19
  36.3 1.0 %collective-permute-start.13 = (f32[8,128]{1,0:T(8,128)S(1)}, f32[8,128]{1,0:T(8,128)S(1)}, u32[]{:S(2)}, u32[]{:S(2)}) collective-permute-start(f32[8,128]{1,0:T(8,128)S(1)} %get-tuple-element.48), channel_id=1, source_target_pairs={{0,3},{1,2},{2,1},{3,0},{4,7},{5,6},{6,5},{7,4},{8,11},{9,10},{10,... | collective-permute-start | bytes 12296 | tf_op jit(solution)/shard_map/ppermute | solution.py:313
  37.4 1.0 %collective-permute-start.12 = (f32[8,128]{1,0:T(8,128)S(1)}, f32[8,128]{1,0:T(8,128)S(1)}, u32[]{:S(2)}, u32[]{:S(2)}) collective-permute-start(f32[8,128]{1,0:T(8,128)S(1)} %get-tuple-element.48), channel_id=1, source_target_pairs={{0,2},{1,3},{2,0},{3,1},{4,6},{5,7},{6,4},{7,5},{8,10},{9,11},{10,... | collective-permute-start | bytes 12296 | tf_op jit(solution)/shard_map/ppermute | solution.py:312
  38.4 1.1 %shard_map.119 = (bf16[2,9,32,128]{3,2,1,0:T(8,128)(2,1)S(1)}, bf16[2,9,32,128]{3,2,1,0:T(8,128)(2,1)S(1)}) custom-call(bf16[34,64,384]{2,1,0:T(8,128)(2,1)S(1)} %get-tuple-element.45.aa_ref, bf16[34,64,384]{2,1,0:T(8,128)(2,1)S(1)} %get-tuple-element.54.tt_ref, f32[8,128]{1,0:T(8,128)S(1)} %add_add_fusion.1.stat_ref), custom_call_target="tpu_custom_call" | custom-call | flops 603979776 | bytes 3641344 | tf_op jit(solution)/shard_map/pallas_call | solution.py:19
  39.5 0.6 %collective-permute-start.16 = (bf16[2,9,32,128]{3,2,1,0:T(8,128)(2,1)S(1)}, bf16[2,9,32,128]{3,2,1,0:T(8,128)(2,1)S(1)}, u32[]{:S(2)}, u32[]{:S(2)}) collective-permute-start(bf16[2,9,32,128]{3,2,1,0:T(8,128)(2,1)S(1)} %get-tuple-element.56), channel_id=1, source_target_pairs={{0,1},{1,0},{2,3},{3,2},{4,5},{5,4},{6,7},{7,6},{8,9},{9,8},{10,11... | collective-permute-start | bytes 442376 | tf_op jit(solution)/shard_map/ppermute | solution.py:508
  40.1 0.9 %collective-permute-done.12 = f32[8,128]{1,0:T(8,128)S(1)} collective-permute-done((f32[8,128]{1,0:T(8,128)S(1)}, f32[8,128]{1,0:T(8,128)S(1)}, u32[]{:S(2)}, u32[]{:S(2)}) %collective-permute-start.12) | collective-permute-done | bytes 4128 | tf_op jit(solution)/shard_map/ppermute | solution.py:312
  41.0 1.3 %shard_map.116 = (bf16[2,9,32,128]{3,2,1,0:T(8,128)(2,1)S(1)}, bf16[2,9,32,128]{3,2,1,0:T(8,128)(2,1)S(1)}) custom-call(bf16[32,64,128]{2,1,0:T(8,128)(2,1)S(1)} %get-tuple-element.38.first_ref, bf16[32,64,128]{2,1,0:T(8,128)(2,1)S(1)} %get-tuple-element.36.mask_ref, f32[8,128]{1,0:T(8,128)S(1)} %add_add_fusion.1.stat_ref, ...), custom_call_target="tpu_custom_call" | custom-call | flops 603979776 | bytes 4075520 | tf_op jit(solution)/shard_map/pallas_call | solution.py:19
  42.4 1.1 %collective-permute-start.17 = (bf16[1,9,32,128]{3,2,1,0:T(8,128)(2,1)S(1)}, bf16[1,9,32,128]{3,2,1,0:T(8,128)(2,1)S(1)}, u32[]{:S(2)}, u32[]{:S(2)}) collective-permute-start(bf16[1,9,32,128]{3,2,1,0:T(8,128)(2,1)S(1)} %get-tuple-element.58), channel_id=1, source_target_pairs={{0,2},{1,3},{2,0},{3,1},{4,6},{5,7},{6,4},{7,5},{8,10},{9,11},{10,... | collective-permute-start | bytes 221192 | tf_op jit(solution)/shard_map/ppermute | solution.py:508
  43.5 0.5 %slice_bitcast_fusion = (f32[128]{0:T(128)}, f32[128]{0:T(128)}) fusion(f32[8,128]{1,0:T(8,128)S(1)} %add_add_fusion.gsum_ref), kind=kLoop, calls=%fused_computation.4 | loop fusion | bytes 2048 | tf_op jit(solution)/shard_map/squeeze | solution.py:711
  44.1 1.1 %collective-permute-start.15 = (bf16[1,9,32,128]{3,2,1,0:T(8,128)(2,1)S(1)}, bf16[1,9,32,128]{3,2,1,0:T(8,128)(2,1)S(1)}, u32[]{:S(2)}, u32[]{:S(2)}) collective-permute-start(bf16[1,9,32,128]{3,2,1,0:T(8,128)(2,1)S(1)} %get-tuple-element.53), channel_id=1, source_target_pairs={{0,2},{1,3},{2,0},{3,1},{4,6},{5,7},{6,4},{7,5},{8,10},{9,11},{10,... | collective-permute-start | bytes 221192 | tf_op jit(solution)/shard_map/ppermute | solution.py:508
  45.1 1.1 %shard_map.118 = bf16[1,8,64,128]{3,2,1,0:T(8,128)(2,1)} custom-call(bf16[34,64,384]{2,1,0:T(8,128)(2,1)S(1)} %get-tuple-element.45.aa_ref, bf16[32,64,128]{2,1,0:T(8,128)(2,1)S(1)} %get-tuple-element.36.mask_ref, bf16[9,128,128]{2,1,0:T(8,128)(2,1)S(1)} %get-tuple-element.46.w_ref, bf16[1,9,32,128]{3,2,1,0:T(8,128)(2,1)S(1)} %get-tuple-element.52.after_ref), custom_call_target="tpu_custom_call" | custom-call | flops 150994944 | bytes 2695168 | tf_op jit(solution)/shard_map/pallas_call | solution.py:19
  46.2 1.1 %collective-permute-done.17 = bf16[1,9,32,128]{3,2,1,0:T(8,128)(2,1)S(1)} collective-permute-done((bf16[1,9,32,128]{3,2,1,0:T(8,128)(2,1)S(1)}, bf16[1,9,32,128]{3,2,1,0:T(8,128)(2,1)S(1)}, u32[]{:S(2)}, u32[]{:S(2)}) %collective-permute-start.17) | collective-permute-done | bytes 73760 | tf_op jit(solution)/shard_map/ppermute | solution.py:508
  47.3 0.7 %add_bitcast_fusion = f32[9,128,32]{1,2,0:T(8,128)} fusion(bf16[1,9,32,128]{3,2,1,0:T(8,128)(2,1)S(1)} %collective-permute-done.17, bf16[1,9,32,128]{3,2,1,0:T(8,128)(2,1)S(1)} %get-tuple-element.57), kind=kLoop, calls=%fused_computation | loop fusion | flops 110592 | bytes 294912 | tf_op jit(solution)/shard_map/transpose | solution.py:511
  48.0 0.7 %collective-permute-done.15 = bf16[1,9,32,128]{3,2,1,0:T(8,128)(2,1)S(1)} collective-permute-done((bf16[1,9,32,128]{3,2,1,0:T(8,128)(2,1)S(1)}, bf16[1,9,32,128]{3,2,1,0:T(8,128)(2,1)S(1)}, u32[]{:S(2)}, u32[]{:S(2)}) %collective-permute-start.15) | collective-permute-done | bytes 73760 | tf_op jit(solution)/shard_map/ppermute | solution.py:508
  48.7 0.7 %add_bitcast_fusion.1 = f32[9,128,32]{1,2,0:T(8,128)} fusion(bf16[1,9,32,128]{3,2,1,0:T(8,128)(2,1)S(1)} %collective-permute-done.15, bf16[1,9,32,128]{3,2,1,0:T(8,128)(2,1)S(1)} %get-tuple-element.52.after_ref), kind=kLoop, calls=%fused_computation.1 | loop fusion | flops 110592 | bytes 294912 | tf_op jit(solution)/shard_map/transpose | solution.py:511
  (20 shorter events, 0.4 us)
Async XLA Ops:
  0.6 14.3 %collective-permute-start = (bf16[1,8,64,128]{3,2,1,0:T(8,128)(2,1)}, bf16[1,8,64,128]{3,2,1,0:T(8,128)(2,1)S(1)}, u32[]{:S(2)}, u32[]{:S(2)}) collective-permute-start(bf16[1,8,64,128]{3,2,1,0:T(8,128)(2,1)} %f_hbm.1), channel_id=1, source_target_pairs={{0,8},{4,12},{8,0},{12,4},{1,9},{5,13},{9,1},{13,5},{2,10},{6,14},... | collective-permute-start | bytes 393224 | tf_op jit(solution)/shard_map/ppermute | solution.py:653
  6.2 10.8 %collective-permute-start.9 = (bf16[1,8,64,128]{3,2,1,0:T(8,128)(2,1)S(1)}, bf16[1,8,64,128]{3,2,1,0:T(8,128)(2,1)S(1)}, u32[]{:S(2)}, u32[]{:S(2)}) collective-permute-start(bf16[1,8,64,128]{3,2,1,0:T(8,128)(2,1)S(1)} %get-tuple-element.41), channel_id=1, source_target_pairs={{0,8},{4,12},{8,0},{12,4},{1,9},{5,13},{9,1},{13,5},{2,10},{6,14},... | collective-permute-start | bytes 393224 | tf_op jit(solution)/shard_map/ppermute | solution.py:653
  6.3 23.0 %collective-permute-start.2 = (bf16[1,8,64,128]{3,2,1,0:T(8,128)(2,1)}, bf16[1,8,64,128]{3,2,1,0:T(8,128)(2,1)S(1)}, u32[]{:S(2)}, u32[]{:S(2)}) collective-permute-start(bf16[1,8,64,128]{3,2,1,0:T(8,128)(2,1)} %f_hbm.1), channel_id=1, source_target_pairs={{0,4},{4,0},{8,12},{12,8},{1,5},{5,1},{9,13},{13,9},{2,6},{6,2},{1... | collective-permute-start | bytes 393224 | tf_op jit(solution)/shard_map/ppermute | solution.py:653
  14.9 14.7 %collective-permute-start.1 = (bf16[1,8,64,128]{3,2,1,0:T(8,128)(2,1)S(1)}, bf16[1,8,64,128]{3,2,1,0:T(8,128)(2,1)S(1)}, u32[]{:S(2)}, u32[]{:S(2)}) collective-permute-start(bf16[1,8,64,128]{3,2,1,0:T(8,128)(2,1)S(1)} %collective-permute-done.f2_ref), channel_id=1, source_target_pairs={{0,4},{4,0},{8,12},{12,8},{1,5},{5,1},{9,13},{13,9},{2,6},{6,2},{1... | collective-permute-start | bytes 393224 | tf_op jit(solution)/shard_map/ppermute | solution.py:653
  15.1 18.0 %collective-permute-start.8 = (bf16[1,8,64,128]{3,2,1,0:T(8,128)(2,1)S(1)}, bf16[1,8,64,128]{3,2,1,0:T(8,128)(2,1)S(1)}, u32[]{:S(2)}, u32[]{:S(2)}) collective-permute-start(bf16[1,8,64,128]{3,2,1,0:T(8,128)(2,1)S(1)} %get-tuple-element.41), channel_id=1, source_target_pairs={{0,4},{4,0},{8,12},{12,8},{1,5},{5,1},{9,13},{13,9},{2,6},{6,2},{1... | collective-permute-start | bytes 393224 | tf_op jit(solution)/shard_map/ppermute | solution.py:653
  17.0 16.1 %collective-permute-start.10 = (bf16[1,8,64,128]{3,2,1,0:T(8,128)(2,1)S(1)}, bf16[1,8,64,128]{3,2,1,0:T(8,128)(2,1)S(1)}, u32[]{:S(2)}, u32[]{:S(2)}) collective-permute-start(bf16[1,8,64,128]{3,2,1,0:T(8,128)(2,1)S(1)} %collective-permute-done.9.t2_ref), channel_id=1, source_target_pairs={{0,4},{4,0},{8,12},{12,8},{1,5},{5,1},{9,13},{13,9},{2,6},{6,2},{1... | collective-permute-start | bytes 393224 | tf_op jit(solution)/shard_map/ppermute | solution.py:653
  17.7 5.9 %collective-permute-start.3 = (s32[8,64]{1,0:T(8,128)}, s32[8,64]{1,0:T(8,128)S(1)}, u32[]{:S(2)}, u32[]{:S(2)}) collective-permute-start(s32[8,64]{1,0:T(8,128)} %land_hbm.1), channel_id=1, source_target_pairs={{0,8},{4,12},{8,0},{12,4},{1,9},{5,13},{9,1},{13,5},{2,10},{6,14},... | collective-permute-start | bytes 6152 | tf_op jit(solution)/shard_map/ppermute | solution.py:653
  23.6 5.6 %collective-permute-start.4 = (s32[16,64]{1,0:T(8,128)S(1)}, s32[16,64]{1,0:T(8,128)S(1)}, u32[]{:S(2)}, u32[]{:S(2)}) collective-permute-start(s32[16,64]{1,0:T(8,128)S(1)} %shard_map.111), channel_id=1, source_target_pairs={{0,4},{4,0},{8,12},{12,8},{1,5},{5,1},{9,13},{13,9},{2,6},{6,2},{1... | collective-permute-start | bytes 12296 | tf_op jit(solution)/shard_map/ppermute | solution.py:653
  31.1 3.6 %collective-permute-start.7 = (f32[8,128]{1,0:T(8,128)S(1)}, f32[8,128]{1,0:T(8,128)S(1)}, u32[]{:S(2)}, u32[]{:S(2)}) collective-permute-start(f32[8,128]{1,0:T(8,128)S(1)} %get-tuple-element.39), channel_id=1, source_target_pairs={{0,3},{1,2},{2,1},{3,0},{4,7},{5,6},{6,5},{7,4},{8,11},{9,10},{10,... | collective-permute-start | bytes 12296 | tf_op jit(solution)/shard_map/ppermute | solution.py:313
  31.2 3.7 %collective-permute-start.6 = (f32[8,128]{1,0:T(8,128)S(1)}, f32[8,128]{1,0:T(8,128)S(1)}, u32[]{:S(2)}, u32[]{:S(2)}) collective-permute-start(f32[8,128]{1,0:T(8,128)S(1)} %get-tuple-element.39), channel_id=1, source_target_pairs={{0,2},{1,3},{2,0},{3,1},{4,6},{5,7},{6,4},{7,5},{8,10},{9,11},{10,... | collective-permute-start | bytes 12296 | tf_op jit(solution)/shard_map/ppermute | solution.py:312
  32.8 2.1 %collective-permute-start.5 = (f32[8,128]{1,0:T(8,128)S(1)}, f32[8,128]{1,0:T(8,128)S(1)}, u32[]{:S(2)}, u32[]{:S(2)}) collective-permute-start(f32[8,128]{1,0:T(8,128)S(1)} %get-tuple-element.39), channel_id=1, source_target_pairs={{0,1},{1,0},{2,3},{3,2},{4,5},{5,4},{6,7},{7,6},{8,9},{9,8},{10,11... | collective-permute-start | bytes 12296 | tf_op jit(solution)/shard_map/ppermute | solution.py:310
  36.3 3.8 %collective-permute-start.13 = (f32[8,128]{1,0:T(8,128)S(1)}, f32[8,128]{1,0:T(8,128)S(1)}, u32[]{:S(2)}, u32[]{:S(2)}) collective-permute-start(f32[8,128]{1,0:T(8,128)S(1)} %get-tuple-element.48), channel_id=1, source_target_pairs={{0,3},{1,2},{2,1},{3,0},{4,7},{5,6},{6,5},{7,4},{8,11},{9,10},{10,... | collective-permute-start | bytes 12296 | tf_op jit(solution)/shard_map/ppermute | solution.py:313
  37.4 3.6 %collective-permute-start.12 = (f32[8,128]{1,0:T(8,128)S(1)}, f32[8,128]{1,0:T(8,128)S(1)}, u32[]{:S(2)}, u32[]{:S(2)}) collective-permute-start(f32[8,128]{1,0:T(8,128)S(1)} %get-tuple-element.48), channel_id=1, source_target_pairs={{0,2},{1,3},{2,0},{3,1},{4,6},{5,7},{6,4},{7,5},{8,10},{9,11},{10,... | collective-permute-start | bytes 12296 | tf_op jit(solution)/shard_map/ppermute | solution.py:312
  38.4 2.6 %collective-permute-start.11 = (f32[8,128]{1,0:T(8,128)S(1)}, f32[8,128]{1,0:T(8,128)S(1)}, u32[]{:S(2)}, u32[]{:S(2)}) collective-permute-start(f32[8,128]{1,0:T(8,128)S(1)} %get-tuple-element.48), channel_id=1, source_target_pairs={{0,1},{1,0},{2,3},{3,2},{4,5},{5,4},{6,7},{7,6},{8,9},{9,8},{10,11... | collective-permute-start | bytes 12296 | tf_op jit(solution)/shard_map/ppermute | solution.py:310
  39.5 2.8 %collective-permute-start.16 = (bf16[2,9,32,128]{3,2,1,0:T(8,128)(2,1)S(1)}, bf16[2,9,32,128]{3,2,1,0:T(8,128)(2,1)S(1)}, u32[]{:S(2)}, u32[]{:S(2)}) collective-permute-start(bf16[2,9,32,128]{3,2,1,0:T(8,128)(2,1)S(1)} %get-tuple-element.56), channel_id=1, source_target_pairs={{0,1},{1,0},{2,3},{3,2},{4,5},{5,4},{6,7},{7,6},{8,9},{9,8},{10,11... | collective-permute-start | bytes 442376 | tf_op jit(solution)/shard_map/ppermute | solution.py:508
  42.3 1.8 %collective-permute-start.14 = (bf16[2,9,32,128]{3,2,1,0:T(8,128)(2,1)S(1)}, bf16[2,9,32,128]{3,2,1,0:T(8,128)(2,1)S(1)}, u32[]{:S(2)}, u32[]{:S(2)}) collective-permute-start(bf16[2,9,32,128]{3,2,1,0:T(8,128)(2,1)S(1)} %get-tuple-element.51), channel_id=1, source_target_pairs={{0,1},{1,0},{2,3},{3,2},{4,5},{5,4},{6,7},{7,6},{8,9},{9,8},{10,11... | collective-permute-start | bytes 442376 | tf_op jit(solution)/shard_map/ppermute | solution.py:508
  42.4 4.9 %collective-permute-start.17 = (bf16[1,9,32,128]{3,2,1,0:T(8,128)(2,1)S(1)}, bf16[1,9,32,128]{3,2,1,0:T(8,128)(2,1)S(1)}, u32[]{:S(2)}, u32[]{:S(2)}) collective-permute-start(bf16[1,9,32,128]{3,2,1,0:T(8,128)(2,1)S(1)} %get-tuple-element.58), channel_id=1, source_target_pairs={{0,2},{1,3},{2,0},{3,1},{4,6},{5,7},{6,4},{7,5},{8,10},{9,11},{10,... | collective-permute-start | bytes 221192 | tf_op jit(solution)/shard_map/ppermute | solution.py:508
  44.1 4.6 %collective-permute-start.15 = (bf16[1,9,32,128]{3,2,1,0:T(8,128)(2,1)S(1)}, bf16[1,9,32,128]{3,2,1,0:T(8,128)(2,1)S(1)}, u32[]{:S(2)}, u32[]{:S(2)}) collective-permute-start(bf16[1,9,32,128]{3,2,1,0:T(8,128)(2,1)S(1)} %get-tuple-element.53), channel_id=1, source_target_pairs={{0,2},{1,3},{2,0},{3,1},{4,6},{5,7},{6,4},{7,5},{8,10},{9,11},{10,... | collective-permute-start | bytes 221192 | tf_op jit(solution)/shard_map/ppermute | solution.py:508
where the time goes:
time: 49.6 us; the launch traced here: 49.4 us
  starting transfers between devices  23 us (46%)
  waiting for transfers between devices  13.7 us (28%)
  Pallas kernels  9.98 us (20%)
  other arithmetic  1.37 us (3%)
  between operations  0.73 us (1%)
  local copies, waits for them, and re-layouts  0.52 us (1%)
    ppermute x8, starting transfers between devices, sample_body(): move = lambda x, pairs: lax.ppermute(x, 'space', pairs)  16.2 us
    ppermute x8, waiting for transfers between devices, sample_body(): move = lambda x, pairs: lax.ppermute(x, 'space', pairs)  10.9 us
    pallas_call x11, Pallas kernels, run(): pl.pallas_call(body, out_shape=list(outs), in_specs=[space] * len(args),...  9.98 us
    ppermute x4, starting transfers between devices, exchange_sum(): got = lax.ppermute(send, 'batch', xor_pairs(size, bit))  2.8 us
    ppermute x2, starting transfers between devices, all_sum(): far = lax.ppermute(x, axis, xor_pairs(size, 2 * bit))  2.59 us
    ppermute x4, waiting for transfers between devices, exchange_sum(): got = lax.ppermute(send, 'batch', xor_pairs(size, bit))  1.78 us
    transpose x2, other arithmetic, exchange_sum(): return (jnp.swapaxes(keep[0].astype(F32) + got[0].astype(F32), 1, 2), keep)  1.36 us
    ppermute x2, starting transfers between devices, all_sum(): both = lax.ppermute(x, axis, xor_pairs(size, 3 * bit))  1.11 us
  transfers between devices with their start and end apart: 18, of which 7 were waited for; matrix products, arithmetic and copies ran while one was open for 2% of the time, Pallas kernels for 17%

commit v1 on v0

--- a/solution.py
+++ b/solution.py
@@ -267,13 +267,11 @@
 
 def put_taps(grad_ref, grad, shifted_ref, base, lon, lat, chans):
     chunks, width = grad_ref.shape[0], grad_ref.shape[2]
-    turned = grad.T
-    for a in (-1, 0, 1):
-        piece = shifted_ref[base + a : base + a + lon].reshape(lon * lat, 3 * chans)
-        part = dot(turned, piece).astype(BF16)
-        for b in range(3):
-            for c in range(chunks):
-                grad_ref[c, 3 * (a + 1) + b] = part[c * width : (c + 1) * width, b * chans : (b + 1) * chans]
+    pieces = [shifted_ref[base + a : base + a + lon].reshape(lon * lat, 3 * chans) for a in (-1, 0, 1)]
+    part = dot(grad.T, jnp.concatenate(pieces, axis=1)).astype(BF16)
+    for t in range(9):
+        for c in range(chunks):
+            grad_ref[c, t] = part[c * width : (c + 1) * width, t * chans : (t + 1) * chans]
 
 
 def out_kernel(lon, lat, chans, aa_ref, mask_ref, tt_ref, stat_ref, w_ref, out_ref, grad_ref):
@@ -353,20 +351,14 @@
     ref[k, :, 2 * chans :] = shift_rows(x, step, zero).astype(BF16)
 
 
-def join_kernel(a_ref, b_ref, out_ref):
-    rows = a_ref.shape[0]
-    out_ref[0:rows] = a_ref[...]
-    out_ref[rows:] = b_ref[...]
-
-
 def sample_prep(
     lon, lat, chans, tiles,
     f_hbm, t_hbm, land_hbm, win_hbm, wout_hbm, gain_hbm, offset_hbm,
-    ss_ref, tt_ref, mask_ref, target_ref, land_ref, win_ref, wout_ref, wt_ref, bn_ref,
-    f_ref, t_ref, sems,
+    ss_ref, tt_ref, mask_ref, target_ref, win_ref, wout_ref, wt_ref, bn_ref,
+    f_ref, t_ref, land_ref, wraw_ref, sems,
 ):
     pairs = [
-        (land_hbm, land_ref), (f_hbm, f_ref), (t_hbm, t_ref), (wout_hbm, wout_ref), (win_hbm, win_ref),
+        (land_hbm, land_ref), (f_hbm, f_ref), (t_hbm, t_ref), (wout_hbm, wout_ref), (win_hbm, wraw_ref),
         (gain_hbm, bn_ref.at[0:1]), (offset_hbm, bn_ref.at[1:2]),
     ]
     copies = [pltpu.make_async_copy(src, dst, sems.at[i]) for i, (src, dst) in enumerate(pairs)]
@@ -385,16 +377,29 @@
         put_shifted(tt_ref, first + i + 1, target, -1)
     for c in copies[3:]:
         c.wait()
-    for a in range(3):
-        for b in range(3):
-            wt_ref[a, b * chans : (b + 1) * chans] = wout_ref[3 * a + b].T
-
-
-def sample_build(lon, lat, chans, f1_ref, f2_ref, l2_ref, l13_ref, ss_in, mask_in, ss_ref, mask_ref):
+    deep = 3 * chans
+    zero = jnp.zeros((deep, chans), BF16)
+    for q in range(4):
+        rows = slice(q * deep, (q + 1) * deep)
+        for half in range(2):
+            lanes = slice(half * chans, (half + 1) * chans)
+            tap = q - half
+            inside = 0 <= tap < 3
+            win_ref[rows, lanes] = wraw_ref[3 * tap : 3 * tap + 3].reshape(deep, chans) if inside else zero
+            turned = [wout_ref[3 * (2 - tap) + b].T for b in range(3)] if inside else [zero]
+            wt_ref[rows, lanes] = jnp.concatenate(turned, axis=0)
+
+
+def paired(ref, start, pairs):
+    columns = [jnp.concatenate([ref[start + 2 * m + q] for m in range(pairs)], axis=0) for q in range(4)]
+    return jnp.concatenate(columns, axis=1)
+
+
+def sample_build(lon, lat, chans, f1_ref, f2_ref, l1_ref, l2_ref, l3_ref, ss_in, mask_in, ss_ref, mask_ref):
     me = lax.axis_index("space")
-    for k, f_ref, land_ref in ((1, f1_ref, l13_ref), (2, f2_ref, l2_ref), (3, None, l13_ref)):
+    for k, f_ref, land_ref in ((1, f1_ref, l1_ref), (2, f2_ref, l2_ref), (3, None, l3_ref)):
         first = jnp.bitwise_xor(me, k) * lon
-        lines = land_ref[lon if k == 3 else 0 : 2 * lon if k == 3 else lon].astype(F32)
+        lines = land_ref[...].astype(F32)
         for i in range(lon):
             mask = spread(lines[i : i + 1], lat, chans)
             mask_ref[first + i] = mask.astype(BF16)
@@ -414,20 +419,19 @@
     ss_ref[0] = ss_ref[nx]
     ss_ref[nx + 1] = ss_ref[1]
     sums, squares, count = [jnp.zeros((8, chans), F32)] * 3
-    step = 8
-    for c in range(0, nx, step):
-        total = None
-        for a in (-1, 0, 1):
-            piece = ss_ref[c + a + 1 : c + a + 1 + step].reshape(step * lat, 3 * chans)
-            part = dot(piece, w_ref[3 * (a + 1) : 3 * (a + 2)].reshape(3 * chans, chans))
-            total = part if total is None else total + part
-        first = total.astype(BF16)
-        first_ref[c : c + step] = first.reshape(step, lat, chans)
-        x = first.astype(F32)
-        m = mask_ref[c : c + step].reshape(step * lat, chans).astype(F32)
-        kept = x * m
-        fold = lambda v: jnp.sum(v.reshape(-1, 8, chans), axis=0)
-        sums, squares, count = sums + fold(kept), squares + fold(kept * x), count + fold(m)
+    fold = lambda v: jnp.sum(v.reshape(-1, 8, chans), axis=0)
+    pairs = lon
+    for c in range(0, nx, 2 * pairs):
+        total = dot(paired(ss_ref, c, pairs), w_ref[...])
+        for m in range(pairs):
+            for half in range(2):
+                k = c + 2 * m + half
+                first = total[m * lat : (m + 1) * lat, half * chans : (half + 1) * chans].astype(BF16)
+                first_ref[k] = first
+                x = first.astype(F32)
+                mask = mask_ref[k].astype(F32)
+                kept = x * mask
+                sums, squares, count = sums + fold(kept), squares + fold(kept * x), count + fold(mask)
     rows = [jnp.sum(v, axis=0, keepdims=True) for v in (sums, squares, count)]
     stat_ref[...] = jnp.concatenate(rows + [jnp.zeros((5, chans), F32)], axis=0)
 
@@ -445,19 +449,17 @@
     extra = None
     for a in (-1, 0, 1):
         rows = jnp.concatenate([top[nx - 1 - (i + a) % nx] for i in range(nx)], axis=0).astype(BF16)
-        part = dot(rows, wt_ref[a + 1, 2 * chans :])
+        part = dot(rows, wt_ref[(1 - a) * 3 * chans + 2 * chans : (2 - a) * 3 * chans, 0:chans])
         extra = part if extra is None else extra + part
     last = lax.broadcasted_iota(jnp.int32, (lat, chans), 0) == lat - 1
-    step = 8
-    for c in range(0, nx, step):
-        total = None
-        for a in (-1, 0, 1):
-            piece = tt_ref[c + 1 - a : c + 1 - a + step].reshape(step * lat, 3 * chans)
-            part = dot(piece, wt_ref[a + 1])
-            total = part if total is None else total + part
-        for i in range(step):
-            add = jnp.where(last, extra[c + i : c + i + 1], 0.0)
-            dact_ref[c + i] = total[i * lat : (i + 1) * lat] + add
+    pairs = lon
+    for c in range(0, nx, 2 * pairs):
+        total = dot(paired(tt_ref, c, pairs), wt_ref[...])
+        for m in range(pairs):
+            for half in range(2):
+                k = c + 2 * m + half
+                own = total[m * lat : (m + 1) * lat, half * chans : (half + 1) * chans]
+                dact_ref[k] = own + jnp.where(last, extra[k : k + 1], 0.0)
 
 
 def sample_act(lat, chans, first_ref, mask_ref, stat_ref, bn_ref, dact_ref, gsum_ref, dpre_ref, aa_ref):
@@ -521,7 +523,9 @@
     halve(lambda k: grad_ref[k], keep_ref, send_ref, 1)
 
 
-def sample_out(lon, lat, chans, aa_ref, mask_ref, w_ref, after_ref, out_ref):
+def sample_out(lon, lat, chans, aa_ref, mask_ref, w_ref, gsum_ref, after_ref, out_ref, gain_ref, offset_ref):
+    offset_ref[...] = gsum_ref[0:1, :]
+    gain_ref[...] = gsum_ref[1:2, :]
     start = lax.axis_index("space") * lon
     total = None
     for a in (-1, 0, 1):
@@ -654,6 +658,8 @@
     f2 = move(fields, across)
     l2 = move(land, across)
     f1 = move(fields, near)
+    l1 = move(land, near)
+    l3 = move(land, xor_pairs(tiles, 3))
     f3 = move(f2, near)
     gain, offset = batchnorm_gain[None, :], batchnorm_offset[None, :]
     params = [
@@ -668,19 +674,19 @@
     cells_f = sds((nx, lat, chans), F32)
     sums = sds((8, chans), F32)
     work = 2 * nx * lat * 9 * chans * chans
-    ss, tt, mask, target, land_own, win, wout, wt, bn = run(
+    double = sds((12 * chans, 2 * chans), BF16)
+    ss, tt, mask, target, win, wout, wt, bn = run(
         functools.partial(sample_prep, *sizes, tiles),
-        [shifted, shifted, cells, sds(target_grad.shape, BF16), sds(land.shape, jnp.int32), sds(conv_in.shape, BF16), sds(conv_out.shape, BF16), sds((3, 3 * chans, chans), BF16), sums],
+        [shifted, shifted, cells, sds(target_grad.shape, BF16), double, sds(conv_out.shape, BF16), double, sums],
         params,
         scratch=[
-            pltpu.VMEM(fields.shape, BF16), pltpu.VMEM(fields.shape, BF16), pltpu.SemaphoreType.DMA((7,)),
+            pltpu.VMEM(fields.shape, BF16), pltpu.VMEM(fields.shape, BF16), pltpu.VMEM(land.shape, jnp.int32),
+            pltpu.VMEM(conv_in.shape, BF16), pltpu.SemaphoreType.DMA((7,)),
         ],
         space=pl.BlockSpec(memory_space=pltpu.HBM),
     )
-    (both,) = run(join_kernel, [sds((2 * lon, lat), jnp.int32)], [land_own, l2])
-    l13 = move(both, near)
     ss, mask = run(
-        functools.partial(sample_build, *sizes), [shifted, cells], [f1, f2, l2, l13, ss, mask], alias={4: 0, 5: 1}
+        functools.partial(sample_build, *sizes), [shifted, cells], [f1, f2, l1, l2, l3, ss, mask], alias={5: 0, 6: 1}
     )
     t2 = move(target, across)
     t1 = move(target, near)
@@ -705,10 +711,12 @@
         [half, half], [first, mask, stat, bn, dpre, gsum, ss], scratch=whole, flops=work,
     )
     grad_in, folded = exchange_sum(keep_i, send_i, shares)
-    (output,) = run(
-        functools.partial(sample_out, *sizes), [sds(fields.shape, BF16)], [aa, mask, wout, folded], flops=work // tiles
-    )
-    return (output, grad_in, grad_out, gsum[1], gsum[0])
+    output, grad_gain, grad_offset = run(
+        functools.partial(sample_out, *sizes),
+        [sds(fields.shape, BF16), sds((1, chans), F32), sds((1, chans), F32)],
+        [aa, mask, wout, gsum, folded], flops=work // tiles,
+    )
+    return (output, grad_in, grad_out, grad_gain[0], grad_offset[0])
 
 
 def body(*args):

time: 49.6 us -> 54.4 us (1.097)
  waiting for transfers between devices: 13.7 us -> 18.4 us
  starting transfers between devices: 23 us -> 24.7 us
  Pallas kernels: 9.98 us -> 9.05 us
    ppermute x8 -> x9, waiting for transfers between devices: 10.9 us -> 15.5 us  [sample_body(): move = lambda x, pairs: lax.ppermute(x, 'space', pairs)]
    ppermute x8 -> x9, starting transfers between devices: 16.2 us -> 17.2 us  [sample_body(): move = lambda x, pairs: lax.ppermute(x, 'space', pairs)]
    pallas_call x11 -> x10, Pallas kernels: 9.98 us -> 9.05 us  [run(): pl.pallas_call(body, out_shape=list(outs), in_specs=[space] * len(args),...]
    ppermute x4, starting transfers between devices: 2.8 us -> 3.48 us  [exchange_sum(): got = lax.ppermute(send, 'batch', xor_pairs(size, bit))]
  transfers between devices with their start and end apart: 18 -> 19, of which waited for: 7 -> 8; matrix products, arithmetic and copies ran while one was open for 2% -> 1% of each run, Pallas kernels for 17% -> 14%
where the time goes in v1:
time: 54.4 us; the launch traced here: 54.2 us
  starting transfers between devices  24.7 us (45%)
  waiting for transfers between devices  18.4 us (34%)
  Pallas kernels  9.05 us (17%)
  other arithmetic  1.37 us (3%)
  between operations  0.72 us (1%)
    ppermute x9, starting transfers between devices, sample_body(): move = lambda x, pairs: lax.ppermute(x, 'space', pairs)  17.2 us
    ppermute x9, waiting for transfers between devices, sample_body(): move = lambda x, pairs: lax.ppermute(x, 'space', pairs)  15.5 us
    pallas_call x10, Pallas kernels, run(): pl.pallas_call(body, out_shape=list(outs), in_specs=[space] * len(args),...  9.05 us
    ppermute x4, starting transfers between devices, exchange_sum(): got = lax.ppermute(send, 'batch', xor_pairs(size, bit))  3.48 us
    ppermute x2, starting transfers between devices, all_sum(): far = lax.ppermute(x, axis, xor_pairs(size, 2 * bit))  3.01 us
    ppermute x4, waiting for transfers between devices, exchange_sum(): got = lax.ppermute(send, 'batch', xor_pairs(size, bit))  1.66 us
    transpose x2, other arithmetic, exchange_sum(): return (jnp.swapaxes(keep[0].astype(F32) + got[0].astype(F32), 1, 2), keep)  1.36 us
    ppermute x2, waiting for transfers between devices, all_sum(): far = lax.ppermute(x, axis, xor_pairs(size, 2 * bit))  1.18 us
  transfers between devices with their start and end apart: 19, of which 8 were waited for; matrix products, arithmetic and copies ran while one was open for 1% of the time, Pallas kernels for 14%

profile of v1, /device:TPU:0, one launch (start us, length us, event | category | flops | bytes accessed | tf_op | source)
XLA Modules:
  0.0 54.2 jit_solution(10375133675404811792)
XLA Ops:
  0.6 4.1 %collective-permute-start = (bf16[1,8,64,128]{3,2,1,0:T(8,128)(2,1)}, bf16[1,8,64,128]{3,2,1,0:T(8,128)(2,1)S(1)}, u32[]{:S(2)}, u32[]{:S(2)}) collective-permute-start(bf16[1,8,64,128]{3,2,1,0:T(8,128)(2,1)} %f_hbm.1), channel_id=1, source_target_pairs={{0,8},{4,12},{8,0},{12,4},{1,9},{5,13},{9,1},{13,5},{2,10},{6,14},... | collective-permute-start | bytes 393224 | tf_op jit(solution)/shard_map/ppermute | solution.py:657
  4.8 1.6 %shard_map.110 = (bf16[34,64,384]{2,1,0:T(8,128)(2,1)S(1)}, bf16[34,64,384]{2,1,0:T(8,128)(2,1)S(1)}, bf16[32,64,128]{2,1,0:T(8,128)(2,1)S(1)}, bf16[1,8,64,128]...) custom-call(bf16[1,8,64,128]{3,2,1,0:T(8,128)(2,1)} %f_hbm.1, ...), custom_call_target="tpu_custom_call" | custom-call | bytes 6724608 | tf_op jit(solution)/shard_map/pallas_call | solution.py:19
  6.5 1.9 %collective-permute-start.2 = (bf16[1,8,64,128]{3,2,1,0:T(8,128)(2,1)}, bf16[1,8,64,128]{3,2,1,0:T(8,128)(2,1)S(1)}, u32[]{:S(2)}, u32[]{:S(2)}) collective-permute-start(bf16[1,8,64,128]{3,2,1,0:T(8,128)(2,1)} %f_hbm.1), channel_id=1, source_target_pairs={{0,4},{4,0},{8,12},{12,8},{1,5},{5,1},{9,13},{13,9},{2,6},{6,2},{1... | collective-permute-start | bytes 393224 | tf_op jit(solution)/shard_map/ppermute | solution.py:657
  8.4 6.6 %collective-permute-done.f2_ref = bf16[1,8,64,128]{3,2,1,0:T(8,128)(2,1)S(1)} collective-permute-done((bf16[1,8,64,128]{3,2,1,0:T(8,128)(2,1)}, bf16[1,8,64,128]{3,2,1,0:T(8,128)(2,1)S(1)}, u32[]{:S(2)}, u32[]{:S(2)}) %collective-permute-start) | collective-permute-done | bytes 131104 | tf_op jit(solution)/shard_map/ppermute | solution.py:657
  15.1 1.9 %collective-permute-start.9 = (bf16[1,8,64,128]{3,2,1,0:T(8,128)(2,1)S(1)}, bf16[1,8,64,128]{3,2,1,0:T(8,128)(2,1)S(1)}, u32[]{:S(2)}, u32[]{:S(2)}) collective-permute-start(bf16[1,8,64,128]{3,2,1,0:T(8,128)(2,1)S(1)} %get-tuple-element.42), channel_id=1, source_target_pairs={{0,4},{4,0},{8,12},{12,8},{1,5},{5,1},{9,13},{13,9},{2,6},{6,2},{1... | collective-permute-start | bytes 393224 | tf_op jit(solution)/shard_map/ppermute | solution.py:657
  17.0 0.7 %collective-permute-start.11 = (bf16[1,8,64,128]{3,2,1,0:T(8,128)(2,1)S(1)}, bf16[1,8,64,128]{3,2,1,0:T(8,128)(2,1)S(1)}, u32[]{:S(2)}, u32[]{:S(2)}) collective-permute-start(bf16[1,8,64,128]{3,2,1,0:T(8,128)(2,1)S(1)} %collective-permute-done.10.t2_ref), channel_id=1, source_target_pairs={{0,4},{4,0},{8,12},{12,8},{1,5},{5,1},{9,13},{13,9},{2,6},{6,2},{1... | collective-permute-start | bytes 393224 | tf_op jit(solution)/shard_map/ppermute | solution.py:657
  17.7 3.4 %collective-permute-start.4 = (s32[8,64]{1,0:T(8,128)}, s32[8,64]{1,0:T(8,128)S(1)}, u32[]{:S(2)}, u32[]{:S(2)}) collective-permute-start(s32[8,64]{1,0:T(8,128)} %land_hbm.1), channel_id=1, source_target_pairs={{0,8},{4,12},{8,0},{12,4},{1,9},{5,13},{9,1},{13,5},{2,10},{6,14},... | collective-permute-start | bytes 6152 | tf_op jit(solution)/shard_map/ppermute | solution.py:657
  21.1 2.5 %collective-permute-done.4.l2_ref = s32[8,64]{1,0:T(8,128)S(1)} collective-permute-done((s32[8,64]{1,0:T(8,128)}, s32[8,64]{1,0:T(8,128)S(1)}, u32[]{:S(2)}, u32[]{:S(2)}) %collective-permute-start.4) | collective-permute-done | bytes 2080 | tf_op jit(solution)/shard_map/ppermute | solution.py:657
  23.6 4.0 %collective-permute-start.3 = (s32[8,64]{1,0:T(8,128)}, s32[8,64]{1,0:T(8,128)S(1)}, u32[]{:S(2)}, u32[]{:S(2)}) collective-permute-start(s32[8,64]{1,0:T(8,128)} %land_hbm.1), channel_id=1, source_target_pairs={{0,4},{4,0},{8,12},{12,8},{1,5},{5,1},{9,13},{13,9},{2,6},{6,2},{1... | collective-permute-start | bytes 6152 | tf_op jit(solution)/shard_map/ppermute | solution.py:657
  27.6 1.8 %collective-permute-done.3.l1_ref = s32[8,64]{1,0:T(8,128)S(1)} collective-permute-done((s32[8,64]{1,0:T(8,128)}, s32[8,64]{1,0:T(8,128)S(1)}, u32[]{:S(2)}, u32[]{:S(2)}) %collective-permute-start.3) | collective-permute-done | bytes 2080 | tf_op jit(solution)/shard_map/ppermute | solution.py:657
  29.4 1.0 %collective-permute-start.5 = (s32[8,64]{1,0:T(8,128)}, s32[8,64]{1,0:T(8,128)S(1)}, u32[]{:S(2)}, u32[]{:S(2)}) collective-permute-start(s32[8,64]{1,0:T(8,128)} %land_hbm.1), channel_id=1, source_target_pairs={{0,12},{4,8},{8,4},{12,0},{1,13},{5,9},{9,5},{13,1},{2,14},{6,10},... | collective-permute-start | bytes 6152 | tf_op jit(solution)/shard_map/ppermute | solution.py:657
  30.4 4.6 %collective-permute-done.5.l3_ref = s32[8,64]{1,0:T(8,128)S(1)} collective-permute-done((s32[8,64]{1,0:T(8,128)}, s32[8,64]{1,0:T(8,128)S(1)}, u32[]{:S(2)}, u32[]{:S(2)}) %collective-permute-start.5) | collective-permute-done | bytes 2080 | tf_op jit(solution)/shard_map/ppermute | solution.py:657
  35.0 0.3 shard_map.111
  35.4 1.2 %shard_map.112 = (bf16[34,64,384]{2,1,0:T(8,128)(2,1)S(1)}, bf16[32,64,128]{2,1,0:T(8,128)(2,1)S(1)}, f32[8,128]{1,0:T(8,128)S(1)}) custom-call(bf16[1,8,64,128]{3,2,1,0:T(8,128)(2,1)S(1)} %collective-permute-done.1.f3_ref, bf16[34,64,384]{2,1,0:T(8,128)(2,1)S(1)} %get-tuple-element.36.ss_in, ...), custom_call_target="tpu_custom_call", output_to_operand_aliasing={{0}: (1, {})} | custom-call | flops 603979776 | bytes 5312512 | tf_op jit(solution)/shard_map/pallas_call | solution.py:19
  36.7 1.6 %collective-permute-start.7 = (f32[8,128]{1,0:T(8,128)S(1)}, f32[8,128]{1,0:T(8,128)S(1)}, u32[]{:S(2)}, u32[]{:S(2)}) collective-permute-start(f32[8,128]{1,0:T(8,128)S(1)} %get-tuple-element.40), channel_id=1, source_target_pairs={{0,2},{1,3},{2,0},{3,1},{4,6},{5,7},{6,4},{7,5},{8,10},{9,11},{10,... | collective-permute-start | bytes 12296 | tf_op jit(solution)/shard_map/ppermute | solution.py:310
  38.2 0.3 collective-permute-start.6
  38.5 1.2 %shard_map.113 = (bf16[34,64,384]{2,1,0:T(8,128)(2,1)S(1)}, f32[32,64,128]{2,1,0:T(8,128)S(1)}) custom-call(bf16[1,8,64,128]{3,2,1,0:T(8,128)(2,1)S(1)} %collective-permute-done.9.t1_ref, bf16[1,8,64,128]{3,2,1,0:T(8,128)(2,1)S(1)} %collective-permute-done.10.t2_ref, ...), custom_call_target="tpu_custom_call", output_to_operand_aliasing={{0}: (4, {})} | custom-call | flops 603979776 | bytes 5570560 | tf_op jit(solution)/shard_map/pallas_call | solution.py:19
  39.8 0.6 %collective-permute-done.7 = f32[8,128]{1,0:T(8,128)S(1)} collective-permute-done((f32[8,128]{1,0:T(8,128)S(1)}, f32[8,128]{1,0:T(8,128)S(1)}, u32[]{:S(2)}, u32[]{:S(2)}) %collective-permute-start.7) | collective-permute-done | bytes 4128 | tf_op jit(solution)/shard_map/ppermute | solution.py:310
  40.4 1.4 %shard_map.114 = (f32[8,128]{1,0:T(8,128)S(1)}, f32[32,64,128]{2,1,0:T(8,128)S(1)}, bf16[34,64,384]{2,1,0:T(8,128)(2,1)S(1)}) custom-call(bf16[32,64,128]{2,1,0:T(8,128)(2,1)S(1)} %get-tuple-element.39.first_ref, bf16[32,64,128]{2,1,0:T(8,128)(2,1)S(1)} %get-tuple-element.37.mask_ref, f32[8,128]{1,0:T(8,128)S(1)} %add_add_fusion.1.stat_ref, ...), custom_call_target="tpu_custom_call" | custom-call | bytes 4829184 | tf_op jit(solution)/shard_map/pallas_call | solution.py:19
  41.8 0.6 %collective-permute-start.14 = (f32[8,128]{1,0:T(8,128)S(1)}, f32[8,128]{1,0:T(8,128)S(1)}, u32[]{:S(2)}, u32[]{:S(2)}) collective-permute-start(f32[8,128]{1,0:T(8,128)S(1)} %get-tuple-element.48), channel_id=1, source_target_pairs={{0,3},{1,2},{2,1},{3,0},{4,7},{5,6},{6,5},{7,4},{8,11},{9,10},{10,... | collective-permute-start | bytes 12296 | tf_op jit(solution)/shard_map/ppermute | solution.py:311
  42.4 1.5 %collective-permute-start.13 = (f32[8,128]{1,0:T(8,128)S(1)}, f32[8,128]{1,0:T(8,128)S(1)}, u32[]{:S(2)}, u32[]{:S(2)}) collective-permute-start(f32[8,128]{1,0:T(8,128)S(1)} %get-tuple-element.48), channel_id=1, source_target_pairs={{0,2},{1,3},{2,0},{3,1},{4,6},{5,7},{6,4},{7,5},{8,10},{9,11},{10,... | collective-permute-start | bytes 12296 | tf_op jit(solution)/shard_map/ppermute | solution.py:310
  43.9 1.0 %shard_map.118 = (bf16[2,9,32,128]{3,2,1,0:T(8,128)(2,1)S(1)}, bf16[2,9,32,128]{3,2,1,0:T(8,128)(2,1)S(1)}) custom-call(bf16[34,64,384]{2,1,0:T(8,128)(2,1)S(1)} %get-tuple-element.46.aa_ref, bf16[34,64,384]{2,1,0:T(8,128)(2,1)S(1)} %get-tuple-element.56.tt_ref, f32[8,128]{1,0:T(8,128)S(1)} %add_add_fusion.1.stat_ref), custom_call_target="tpu_custom_call" | custom-call | flops 603979776 | bytes 3641344 | tf_op jit(solution)/shard_map/pallas_call | solution.py:19
  44.8 0.6 %collective-permute-start.17 = (bf16[2,9,32,128]{3,2,1,0:T(8,128)(2,1)S(1)}, bf16[2,9,32,128]{3,2,1,0:T(8,128)(2,1)S(1)}, u32[]{:S(2)}, u32[]{:S(2)}) collective-permute-start(bf16[2,9,32,128]{3,2,1,0:T(8,128)(2,1)S(1)} %get-tuple-element.58), channel_id=1, source_target_pairs={{0,1},{1,0},{2,3},{3,2},{4,5},{5,4},{6,7},{7,6},{8,9},{9,8},{10,11... | collective-permute-start | bytes 442376 | tf_op jit(solution)/shard_map/ppermute | solution.py:510
  45.4 0.6 %collective-permute-done.13 = f32[8,128]{1,0:T(8,128)S(1)} collective-permute-done((f32[8,128]{1,0:T(8,128)S(1)}, f32[8,128]{1,0:T(8,128)S(1)}, u32[]{:S(2)}, u32[]{:S(2)}) %collective-permute-start.13) | collective-permute-done | bytes 4128 | tf_op jit(solution)/shard_map/ppermute | solution.py:310
  46.0 1.1 %shard_map.115 = (bf16[2,9,32,128]{3,2,1,0:T(8,128)(2,1)S(1)}, bf16[2,9,32,128]{3,2,1,0:T(8,128)(2,1)S(1)}) custom-call(bf16[32,64,128]{2,1,0:T(8,128)(2,1)S(1)} %get-tuple-element.39.first_ref, bf16[32,64,128]{2,1,0:T(8,128)(2,1)S(1)} %get-tuple-element.37.mask_ref, f32[8,128]{1,0:T(8,128)S(1)} %add_add_fusion.1.stat_ref, ...), custom_call_target="tpu_custom_call" | custom-call | flops 603979776 | bytes 4075520 | tf_op jit(solution)/shard_map/pallas_call | solution.py:19
  47.3 1.4 %collective-permute-start.18 = (bf16[1,9,32,128]{3,2,1,0:T(8,128)(2,1)S(1)}, bf16[1,9,32,128]{3,2,1,0:T(8,128)(2,1)S(1)}, u32[]{:S(2)}, u32[]{:S(2)}) collective-permute-start(bf16[1,9,32,128]{3,2,1,0:T(8,128)(2,1)S(1)} %get-tuple-element.60), channel_id=1, source_target_pairs={{0,2},{1,3},{2,0},{3,1},{4,6},{5,7},{6,4},{7,5},{8,10},{9,11},{10,... | collective-permute-start | bytes 221192 | tf_op jit(solution)/shard_map/ppermute | solution.py:510
  48.8 1.3 %collective-permute-start.16 = (bf16[1,9,32,128]{3,2,1,0:T(8,128)(2,1)S(1)}, bf16[1,9,32,128]{3,2,1,0:T(8,128)(2,1)S(1)}, u32[]{:S(2)}, u32[]{:S(2)}) collective-permute-start(bf16[1,9,32,128]{3,2,1,0:T(8,128)(2,1)S(1)} %get-tuple-element.55), channel_id=1, source_target_pairs={{0,2},{1,3},{2,0},{3,1},{4,6},{5,7},{6,4},{7,5},{8,10},{9,11},{10,... | collective-permute-start | bytes 221192 | tf_op jit(solution)/shard_map/ppermute | solution.py:510
  50.1 1.1 %shard_map.117 = (bf16[1,8,64,128]{3,2,1,0:T(8,128)(2,1)}, f32[1,128]{1,0:T(1,128)}, f32[1,128]{1,0:T(1,128)}) custom-call(bf16[34,64,384]{2,1,0:T(8,128)(2,1)S(1)} %get-tuple-element.46.aa_ref, bf16[32,64,128]{2,1,0:T(8,128)(2,1)S(1)} %get-tuple-element.37.mask_ref, bf16[9,128,128]{2,1,0:T(8,128)(2,1)S(1)} %get-tuple-element.47.w_ref, ...), custom_call_target="tpu_custom_call" | custom-call | flops 150994944 | bytes 2700288 | tf_op jit(solution)/shard_map/pallas_call | solution.py:19
  51.2 1.1 %collective-permute-done.18 = bf16[1,9,32,128]{3,2,1,0:T(8,128)(2,1)S(1)} collective-permute-done((bf16[1,9,32,128]{3,2,1,0:T(8,128)(2,1)S(1)}, bf16[1,9,32,128]{3,2,1,0:T(8,128)(2,1)S(1)}, u32[]{:S(2)}, u32[]{:S(2)}) %collective-permute-start.18) | collective-permute-done | bytes 73760 | tf_op jit(solution)/shard_map/ppermute | solution.py:510
  52.3 0.7 %add_bitcast_fusion = f32[9,128,32]{1,2,0:T(8,128)} fusion(bf16[1,9,32,128]{3,2,1,0:T(8,128)(2,1)S(1)} %collective-permute-done.18, bf16[1,9,32,128]{3,2,1,0:T(8,128)(2,1)S(1)} %get-tuple-element.59), kind=kLoop, calls=%fused_computation | loop fusion | flops 110592 | bytes 294912 | tf_op jit(solution)/shard_map/transpose | solution.py:513
  53.0 0.6 %collective-permute-done.16 = bf16[1,9,32,128]{3,2,1,0:T(8,128)(2,1)S(1)} collective-permute-done((bf16[1,9,32,128]{3,2,1,0:T(8,128)(2,1)S(1)}, bf16[1,9,32,128]{3,2,1,0:T(8,128)(2,1)S(1)}, u32[]{:S(2)}, u32[]{:S(2)}) %collective-permute-start.16) | collective-permute-done | bytes 73760 | tf_op jit(solution)/shard_map/ppermute | solution.py:510
  53.6 0.7 %add_bitcast_fusion.1 = f32[9,128,32]{1,2,0:T(8,128)} fusion(bf16[1,9,32,128]{3,2,1,0:T(8,128)(2,1)S(1)} %collective-permute-done.16, bf16[1,9,32,128]{3,2,1,0:T(8,128)(2,1)S(1)} %get-tuple-element.53.after_ref), kind=kLoop, calls=%fused_computation.1 | loop fusion | flops 110592 | bytes 294912 | tf_op jit(solution)/shard_map/transpose | solution.py:513
  (20 shorter events, 0.6 us)
Async XLA Ops:
  0.6 14.3 %collective-permute-start = (bf16[1,8,64,128]{3,2,1,0:T(8,128)(2,1)}, bf16[1,8,64,128]{3,2,1,0:T(8,128)(2,1)S(1)}, u32[]{:S(2)}, u32[]{:S(2)}) collective-permute-start(bf16[1,8,64,128]{3,2,1,0:T(8,128)(2,1)} %f_hbm.1), channel_id=1, source_target_pairs={{0,8},{4,12},{8,0},{12,4},{1,9},{5,13},{9,1},{13,5},{2,10},{6,14},... | collective-permute-start | bytes 393224 | tf_op jit(solution)/shard_map/ppermute | solution.py:657
  6.4 10.6 %collective-permute-start.10 = (bf16[1,8,64,128]{3,2,1,0:T(8,128)(2,1)S(1)}, bf16[1,8,64,128]{3,2,1,0:T(8,128)(2,1)S(1)}, u32[]{:S(2)}, u32[]{:S(2)}) collective-permute-start(bf16[1,8,64,128]{3,2,1,0:T(8,128)(2,1)S(1)} %get-tuple-element.42), channel_id=1, source_target_pairs={{0,8},{4,12},{8,0},{12,4},{1,9},{5,13},{9,1},{13,5},{2,10},{6,14},... | collective-permute-start | bytes 393224 | tf_op jit(solution)/shard_map/ppermute | solution.py:657
  6.5 28.6 %collective-permute-start.2 = (bf16[1,8,64,128]{3,2,1,0:T(8,128)(2,1)}, bf16[1,8,64,128]{3,2,1,0:T(8,128)(2,1)S(1)}, u32[]{:S(2)}, u32[]{:S(2)}) collective-permute-start(bf16[1,8,64,128]{3,2,1,0:T(8,128)(2,1)} %f_hbm.1), channel_id=1, source_target_pairs={{0,4},{4,0},{8,12},{12,8},{1,5},{5,1},{9,13},{13,9},{2,6},{6,2},{1... | collective-permute-start | bytes 393224 | tf_op jit(solution)/shard_map/ppermute | solution.py:657
  14.9 20.4 %collective-permute-start.1 = (bf16[1,8,64,128]{3,2,1,0:T(8,128)(2,1)S(1)}, bf16[1,8,64,128]{3,2,1,0:T(8,128)(2,1)S(1)}, u32[]{:S(2)}, u32[]{:S(2)}) collective-permute-start(bf16[1,8,64,128]{3,2,1,0:T(8,128)(2,1)S(1)} %collective-permute-done.f2_ref), channel_id=1, source_target_pairs={{0,4},{4,0},{8,12},{12,8},{1,5},{5,1},{9,13},{13,9},{2,6},{6,2},{1... | collective-permute-start | bytes 393224 | tf_op jit(solution)/shard_map/ppermute | solution.py:657
  15.1 23.5 %collective-permute-start.9 = (bf16[1,8,64,128]{3,2,1,0:T(8,128)(2,1)S(1)}, bf16[1,8,64,128]{3,2,1,0:T(8,128)(2,1)S(1)}, u32[]{:S(2)}, u32[]{:S(2)}) collective-permute-start(bf16[1,8,64,128]{3,2,1,0:T(8,128)(2,1)S(1)} %get-tuple-element.42), channel_id=1, source_target_pairs={{0,4},{4,0},{8,12},{12,8},{1,5},{5,1},{9,13},{13,9},{2,6},{6,2},{1... | collective-permute-start | bytes 393224 | tf_op jit(solution)/shard_map/ppermute | solution.py:657
  17.0 21.5 %collective-permute-start.11 = (bf16[1,8,64,128]{3,2,1,0:T(8,128)(2,1)S(1)}, bf16[1,8,64,128]{3,2,1,0:T(8,128)(2,1)S(1)}, u32[]{:S(2)}, u32[]{:S(2)}) collective-permute-start(bf16[1,8,64,128]{3,2,1,0:T(8,128)(2,1)S(1)} %collective-permute-done.10.t2_ref), channel_id=1, source_target_pairs={{0,4},{4,0},{8,12},{12,8},{1,5},{5,1},{9,13},{13,9},{2,6},{6,2},{1... | collective-permute-start | bytes 393224 | tf_op jit(solution)/shard_map/ppermute | solution.py:657
  17.7 5.9 %collective-permute-start.4 = (s32[8,64]{1,0:T(8,128)}, s32[8,64]{1,0:T(8,128)S(1)}, u32[]{:S(2)}, u32[]{:S(2)}) collective-permute-start(s32[8,64]{1,0:T(8,128)} %land_hbm.1), channel_id=1, source_target_pairs={{0,8},{4,12},{8,0},{12,4},{1,9},{5,13},{9,1},{13,5},{2,10},{6,14},... | collective-permute-start | bytes 6152 | tf_op jit(solution)/shard_map/ppermute | solution.py:657
  23.6 5.8 %collective-permute-start.3 = (s32[8,64]{1,0:T(8,128)}, s32[8,64]{1,0:T(8,128)S(1)}, u32[]{:S(2)}, u32[]{:S(2)}) collective-permute-start(s32[8,64]{1,0:T(8,128)} %land_hbm.1), channel_id=1, source_target_pairs={{0,4},{4,0},{8,12},{12,8},{1,5},{5,1},{9,13},{13,9},{2,6},{6,2},{1... | collective-permute-start | bytes 6152 | tf_op jit(solution)/shard_map/ppermute | solution.py:657
  29.4 5.6 %collective-permute-start.5 = (s32[8,64]{1,0:T(8,128)}, s32[8,64]{1,0:T(8,128)S(1)}, u32[]{:S(2)}, u32[]{:S(2)}) collective-permute-start(s32[8,64]{1,0:T(8,128)} %land_hbm.1), channel_id=1, source_target_pairs={{0,12},{4,8},{8,4},{12,0},{1,13},{5,9},{9,5},{13,1},{2,14},{6,10},... | collective-permute-start | bytes 6152 | tf_op jit(solution)/shard_map/ppermute | solution.py:657
  36.6 3.2 %collective-permute-start.8 = (f32[8,128]{1,0:T(8,128)S(1)}, f32[8,128]{1,0:T(8,128)S(1)}, u32[]{:S(2)}, u32[]{:S(2)}) collective-permute-start(f32[8,128]{1,0:T(8,128)S(1)} %get-tuple-element.40), channel_id=1, source_target_pairs={{0,3},{1,2},{2,1},{3,0},{4,7},{5,6},{6,5},{7,4},{8,11},{9,10},{10,... | collective-permute-start | bytes 12296 | tf_op jit(solution)/shard_map/ppermute | solution.py:311
  36.7 3.7 %collective-permute-start.7 = (f32[8,128]{1,0:T(8,128)S(1)}, f32[8,128]{1,0:T(8,128)S(1)}, u32[]{:S(2)}, u32[]{:S(2)}) collective-permute-start(f32[8,128]{1,0:T(8,128)S(1)} %get-tuple-element.40), channel_id=1, source_target_pairs={{0,2},{1,3},{2,0},{3,1},{4,6},{5,7},{6,4},{7,5},{8,10},{9,11},{10,... | collective-permute-start | bytes 12296 | tf_op jit(solution)/shard_map/ppermute | solution.py:310
  38.2 2.1 %collective-permute-start.6 = (f32[8,128]{1,0:T(8,128)S(1)}, f32[8,128]{1,0:T(8,128)S(1)}, u32[]{:S(2)}, u32[]{:S(2)}) collective-permute-start(f32[8,128]{1,0:T(8,128)S(1)} %get-tuple-element.40), channel_id=1, source_target_pairs={{0,1},{1,0},{2,3},{3,2},{4,5},{5,4},{6,7},{7,6},{8,9},{9,8},{10,11... | collective-permute-start | bytes 12296 | tf_op jit(solution)/shard_map/ppermute | solution.py:308
  41.8 3.6 %collective-permute-start.14 = (f32[8,128]{1,0:T(8,128)S(1)}, f32[8,128]{1,0:T(8,128)S(1)}, u32[]{:S(2)}, u32[]{:S(2)}) collective-permute-start(f32[8,128]{1,0:T(8,128)S(1)} %get-tuple-element.48), channel_id=1, source_target_pairs={{0,3},{1,2},{2,1},{3,0},{4,7},{5,6},{6,5},{7,4},{8,11},{9,10},{10,... | collective-permute-start | bytes 12296 | tf_op jit(solution)/shard_map/ppermute | solution.py:311
  42.4 3.6 %collective-permute-start.13 = (f32[8,128]{1,0:T(8,128)S(1)}, f32[8,128]{1,0:T(8,128)S(1)}, u32[]{:S(2)}, u32[]{:S(2)}) collective-permute-start(f32[8,128]{1,0:T(8,128)S(1)} %get-tuple-element.48), channel_id=1, source_target_pairs={{0,2},{1,3},{2,0},{3,1},{4,6},{5,7},{6,4},{7,5},{8,10},{9,11},{10,... | collective-permute-start | bytes 12296 | tf_op jit(solution)/shard_map/ppermute | solution.py:310
  43.9 2.2 %collective-permute-start.12 = (f32[8,128]{1,0:T(8,128)S(1)}, f32[8,128]{1,0:T(8,128)S(1)}, u32[]{:S(2)}, u32[]{:S(2)}) collective-permute-start(f32[8,128]{1,0:T(8,128)S(1)} %get-tuple-element.48), channel_id=1, source_target_pairs={{0,1},{1,0},{2,3},{3,2},{4,5},{5,4},{6,7},{7,6},{8,9},{9,8},{10,11... | collective-permute-start | bytes 12296 | tf_op jit(solution)/shard_map/ppermute | solution.py:308
  44.8 2.5 %collective-permute-start.17 = (bf16[2,9,32,128]{3,2,1,0:T(8,128)(2,1)S(1)}, bf16[2,9,32,128]{3,2,1,0:T(8,128)(2,1)S(1)}, u32[]{:S(2)}, u32[]{:S(2)}) collective-permute-start(bf16[2,9,32,128]{3,2,1,0:T(8,128)(2,1)S(1)} %get-tuple-element.58), channel_id=1, source_target_pairs={{0,1},{1,0},{2,3},{3,2},{4,5},{5,4},{6,7},{7,6},{8,9},{9,8},{10,11... | collective-permute-start | bytes 442376 | tf_op jit(solution)/shard_map/ppermute | solution.py:510
  47.1 1.7 %collective-permute-start.15 = (bf16[2,9,32,128]{3,2,1,0:T(8,128)(2,1)S(1)}, bf16[2,9,32,128]{3,2,1,0:T(8,128)(2,1)S(1)}, u32[]{:S(2)}, u32[]{:S(2)}) collective-permute-start(bf16[2,9,32,128]{3,2,1,0:T(8,128)(2,1)S(1)} %get-tuple-element.52), channel_id=1, source_target_pairs={{0,1},{1,0},{2,3},{3,2},{4,5},{5,4},{6,7},{7,6},{8,9},{9,8},{10,11... | collective-permute-start | bytes 442376 | tf_op jit(solution)/shard_map/ppermute | solution.py:510
  47.3 4.9 %collective-permute-start.18 = (bf16[1,9,32,128]{3,2,1,0:T(8,128)(2,1)S(1)}, bf16[1,9,32,128]{3,2,1,0:T(8,128)(2,1)S(1)}, u32[]{:S(2)}, u32[]{:S(2)}) collective-permute-start(bf16[1,9,32,128]{3,2,1,0:T(8,128)(2,1)S(1)} %get-tuple-element.60), channel_id=1, source_target_pairs={{0,2},{1,3},{2,0},{3,1},{4,6},{5,7},{6,4},{7,5},{8,10},{9,11},{10,... | collective-permute-start | bytes 221192 | tf_op jit(solution)/shard_map/ppermute | solution.py:510
  48.8 4.7 %collective-permute-start.16 = (bf16[1,9,32,128]{3,2,1,0:T(8,128)(2,1)S(1)}, bf16[1,9,32,128]{3,2,1,0:T(8,128)(2,1)S(1)}, u32[]{:S(2)}, u32[]{:S(2)}) collective-permute-start(bf16[1,9,32,128]{3,2,1,0:T(8,128)(2,1)S(1)} %get-tuple-element.55), channel_id=1, source_target_pairs={{0,2},{1,3},{2,0},{3,1},{4,6},{5,7},{6,4},{7,5},{8,10},{9,11},{10,... | collective-permute-start | bytes 221192 | tf_op jit(solution)/shard_map/ppermute | solution.py:510

commit v2 on v1

--- a/solution.py
+++ b/solution.py
@@ -351,11 +351,17 @@
     ref[k, :, 2 * chans :] = shift_rows(x, step, zero).astype(BF16)
 
 
+def join_kernel(a_ref, b_ref, out_ref):
+    rows = a_ref.shape[0]
+    out_ref[0:rows] = a_ref[...]
+    out_ref[rows:] = b_ref[...]
+
+
 def sample_prep(
     lon, lat, chans, tiles,
     f_hbm, t_hbm, land_hbm, win_hbm, wout_hbm, gain_hbm, offset_hbm,
-    ss_ref, tt_ref, mask_ref, target_ref, win_ref, wout_ref, wt_ref, bn_ref,
-    f_ref, t_ref, land_ref, wraw_ref, sems,
+    ss_ref, tt_ref, mask_ref, target_ref, land_ref, win_ref, wout_ref, wt_ref, bn_ref,
+    f_ref, t_ref, wraw_ref, sems,
 ):
     pairs = [
         (land_hbm, land_ref), (f_hbm, f_ref), (t_hbm, t_ref), (wout_hbm, wout_ref), (win_hbm, wraw_ref),
@@ -395,11 +401,11 @@
     return jnp.concatenate(columns, axis=1)
 
 
-def sample_build(lon, lat, chans, f1_ref, f2_ref, l1_ref, l2_ref, l3_ref, ss_in, mask_in, ss_ref, mask_ref):
+def sample_build(lon, lat, chans, f1_ref, f2_ref, l2_ref, l13_ref, ss_in, mask_in, ss_ref, mask_ref):
     me = lax.axis_index("space")
-    for k, f_ref, land_ref in ((1, f1_ref, l1_ref), (2, f2_ref, l2_ref), (3, None, l3_ref)):
+    for k, f_ref, land_ref in ((1, f1_ref, l13_ref), (2, f2_ref, l2_ref), (3, None, l13_ref)):
         first = jnp.bitwise_xor(me, k) * lon
-        lines = land_ref[...].astype(F32)
+        lines = land_ref[lon if k == 3 else 0 : 2 * lon if k == 3 else lon].astype(F32)
         for i in range(lon):
             mask = spread(lines[i : i + 1], lat, chans)
             mask_ref[first + i] = mask.astype(BF16)
@@ -481,7 +487,7 @@
             acts.append(u * half * m)
             slope = half + 0.5 * u * (1.0 - hyper * hyper) * 0.7978845608 * (1.0 + 3.0 * 0.044715 * square)
             dpre = dact_ref[k] * scale * m * slope
-            dpre_ref[k] = dpre
+            dpre_ref[k] = dpre.astype(BF16)
             goff, ggain = goff + fold(dpre), ggain + fold(dpre * xhat)
         for k, x, other in ((i, acts[0], acts[1]), (nx - 1 - i, acts[1], acts[0])):
             aa_ref[k + 1, :, 0:chans] = shift_rows(x, -1, jnp.zeros((1, chans), F32)).astype(BF16)
@@ -536,16 +542,38 @@
     out_ref[...] = (total * own_mask).astype(BF16).reshape(1, lon, lat, chans)
 
 
-def sample_in(lat, chans, first_ref, mask_ref, stat_ref, bn_ref, dpre_ref, gsum_ref, ss_ref, keep_ref, send_ref, grad_ref):
+def side_by_side(ref, nx, lat, chans):
+    return jnp.concatenate([ref[1 + a : 1 + a + nx].reshape(nx * lat, 3 * chans) for a in (-1, 0, 1)], axis=1)
+
+
+def sample_static(lat, chans, first_ref, mask_ref, ss_ref, d_ref):
     nx = mask_ref.shape[0]
+    mask = mask_ref[...].reshape(nx * lat, chans)
+    kept = first_ref[...].reshape(nx * lat, chans) * mask
+    d_ref[...] = dot(jnp.concatenate([kept.T, mask.T[0:16]], axis=0), side_by_side(ss_ref, nx, lat, chans))
+
+
+def sample_inner(lat, chans, dpre_ref, ss_ref, a_ref):
+    nx = dpre_ref.shape[0]
+    a_ref[...] = dot(dpre_ref[...].reshape(nx * lat, chans).T, side_by_side(ss_ref, nx, lat, chans))
+
+
+def sample_in(chans, a_ref, d_ref, stat_ref, bn_ref, gsum_ref, keep_ref, send_ref, grad_ref):
     count, mean, rstd = moments(stat_ref)
-    goff, ggain = gsum_ref[0:1, :] / count, gsum_ref[1:2, :] / count
     factor = bn_ref[0:1, :] * rstd
-    rows = []
-    for k in range(nx):
-        xhat = (first_ref[k].astype(F32) - mean) * rstd
-        rows.append((mask_ref[k].astype(F32) * factor * (dpre_ref[k] - (goff + xhat * ggain))).astype(BF16))
-    put_taps(grad_ref, jnp.concatenate(rows, axis=0), ss_ref, 1, nx, lat, chans)
+    slope = factor * rstd * gsum_ref[1:2, :] / count
+    shift = slope * mean - factor * gsum_ref[0:1, :] / count
+    diagonal = lax.broadcasted_iota(jnp.int32, (chans, chans), 0) == lax.broadcasted_iota(jnp.int32, (chans, chans), 1)
+    factor, slope, shift = (
+        jnp.sum(jnp.where(diagonal, jnp.broadcast_to(v, (chans, chans)), 0.0), axis=1, keepdims=True)
+        for v in (factor, slope, shift)
+    )
+    width = grad_ref.shape[2]
+    for t in range(9):
+        lanes = slice(t * chans, (t + 1) * chans)
+        part = factor * a_ref[:, lanes] + (shift * d_ref[chans : chans + 1, lanes] - slope * d_ref[0:chans, lanes])
+        for c in range(grad_ref.shape[0]):
+            grad_ref[c, t] = part[c * width : (c + 1) * width].astype(BF16)
     halve(lambda k: grad_ref[k], keep_ref, send_ref, 1)
 
 
@@ -658,8 +686,6 @@
     f2 = move(fields, across)
     l2 = move(land, across)
     f1 = move(fields, near)
-    l1 = move(land, near)
-    l3 = move(land, xor_pairs(tiles, 3))
     f3 = move(f2, near)
     gain, offset = batchnorm_gain[None, :], batchnorm_offset[None, :]
     params = [
@@ -675,18 +701,19 @@
     sums = sds((8, chans), F32)
     work = 2 * nx * lat * 9 * chans * chans
     double = sds((12 * chans, 2 * chans), BF16)
-    ss, tt, mask, target, win, wout, wt, bn = run(
+    ss, tt, mask, target, land_own, win, wout, wt, bn = run(
         functools.partial(sample_prep, *sizes, tiles),
-        [shifted, shifted, cells, sds(target_grad.shape, BF16), double, sds(conv_out.shape, BF16), double, sums],
+        [shifted, shifted, cells, sds(target_grad.shape, BF16), sds(land.shape, jnp.int32), double, sds(conv_out.shape, BF16), double, sums],
         params,
         scratch=[
-            pltpu.VMEM(fields.shape, BF16), pltpu.VMEM(fields.shape, BF16), pltpu.VMEM(land.shape, jnp.int32),
-            pltpu.VMEM(conv_in.shape, BF16), pltpu.SemaphoreType.DMA((7,)),
+            pltpu.VMEM(fields.shape, BF16), pltpu.VMEM(fields.shape, BF16), pltpu.VMEM(conv_in.shape, BF16), pltpu.SemaphoreType.DMA((7,)),
         ],
         space=pl.BlockSpec(memory_space=pltpu.HBM),
     )
+    (both,) = run(join_kernel, [sds((2 * lon, lat), jnp.int32)], [land_own, l2])
+    l13 = move(both, near)
     ss, mask = run(
-        functools.partial(sample_build, *sizes), [shifted, cells], [f1, f2, l1, l2, l3, ss, mask], alias={5: 0, 6: 1}
+        functools.partial(sample_build, *sizes), [shifted, cells], [f1, f2, l2, l13, ss, mask], alias={4: 0, 5: 1}
     )
     t2 = move(target, across)
     t1 = move(target, near)
@@ -698,17 +725,20 @@
     tt, dact = run(
         functools.partial(sample_adjoint, *sizes), [shifted, cells_f], [t1, t2, t3, wt, tt], flops=work, alias={4: 0}
     )
+    (static,) = run(
+        functools.partial(sample_static, lat, chans), [sds((chans + 16, 9 * chans), F32)], [first, mask, ss], flops=work
+    )
     gsum, dpre, aa = run(
-        functools.partial(sample_act, lat, chans), [sums, cells_f, shifted], [first, mask, stat, bn, dact]
+        functools.partial(sample_act, lat, chans), [sums, cells, shifted], [first, mask, stat, bn, dact]
     )
     gsum = all_sum(gsum, "batch")
+    (inner,) = run(functools.partial(sample_inner, lat, chans), [sds((chans, 9 * chans), F32)], [dpre, ss], flops=work)
     keep_o, send_o = run(
         functools.partial(sample_grad, lat, chans), [half, half], [aa, tt, stat], scratch=whole, flops=work
     )
     grad_out, _ = exchange_sum(keep_o, send_o, shares)
     keep_i, send_i = run(
-        functools.partial(sample_in, lat, chans),
-        [half, half], [first, mask, stat, bn, dpre, gsum, ss], scratch=whole, flops=work,
+        functools.partial(sample_in, chans), [half, half], [inner, static, stat, bn, gsum], scratch=whole
     )
     grad_in, folded = exchange_sum(keep_i, send_i, shares)
     output, grad_gain, grad_offset = run(

time: 54.4 us -> 49 us (0.901)
  waiting for transfers between devices: 18.4 us -> 13.5 us
  starting transfers between devices: 24.7 us -> 23.1 us
  Pallas kernels: 9.05 us -> 10.2 us
    ppermute x9 -> x8, waiting for transfers between devices: 15.5 us -> 10.8 us  [sample_body(): move = lambda x, pairs: lax.ppermute(x, 'space', pairs)]
    ppermute x2, waiting for transfers between devices: 1.18 us -> 0.01 us  [all_sum(): far = lax.ppermute(x, axis, xor_pairs(size, 2 * bit))]
    pallas_call x10 -> x13, Pallas kernels: 9.05 us -> 10.2 us  [run(): pl.pallas_call(body, out_shape=list(outs), in_specs=[space] * len(args),...]
    ppermute x9 -> x8, starting transfers between devices: 17.2 us -> 16.2 us  [sample_body(): move = lambda x, pairs: lax.ppermute(x, 'space', pairs)]
    ppermute x2, waiting for transfers between devices: 0.01 us -> 0.61 us  [all_sum(): both = lax.ppermute(x, axis, xor_pairs(size, 3 * bit))]
  transfers between devices with their start and end apart: 19 -> 18, of which waited for: 8 -> 8; matrix products, arithmetic and copies ran while one was open for 1% -> 1% of each run, Pallas kernels for 14% -> 18%
where the time goes in v2:
time: 49 us; the launch traced here: 48.8 us
  starting transfers between devices  23.1 us (47%)
  waiting for transfers between devices  13.5 us (28%)
  Pallas kernels  10.2 us (21%)
  other arithmetic  1.37 us (3%)
  between operations  0.77 us (2%)
    ppermute x8, starting transfers between devices, sample_body(): move = lambda x, pairs: lax.ppermute(x, 'space', pairs)  16.2 us
    ppermute x8, waiting for transfers between devices, sample_body(): move = lambda x, pairs: lax.ppermute(x, 'space', pairs)  10.8 us
    pallas_call x13, Pallas kernels, run(): pl.pallas_call(body, out_shape=list(outs), in_specs=[space] * len(args),...  10.2 us
    ppermute x4, starting transfers between devices, exchange_sum(): got = lax.ppermute(send, 'batch', xor_pairs(size, bit))  2.97 us
    ppermute x2, starting transfers between devices, all_sum(): far = lax.ppermute(x, axis, xor_pairs(size, 2 * bit))  2.79 us
    ppermute x4, waiting for transfers between devices, exchange_sum(): got = lax.ppermute(send, 'batch', xor_pairs(size, bit))  2.1 us
    transpose x2, other arithmetic, exchange_sum(): return (jnp.swapaxes(keep[0].astype(F32) + got[0].astype(F32), 1, 2), keep)  1.36 us
  transfers between devices with their start and end apart: 18, of which 8 were waited for; matrix products, arithmetic and copies ran while one was open for 1% of the time, Pallas kernels for 18%

profile of v2, /device:TPU:0, one launch (start us, length us, event | category | flops | bytes accessed | tf_op | source)
XLA Modules:
  0.0 48.8 jit_solution(9942658447079639943)
XLA Ops:
  0.6 4.1 %collective-permute-start = (bf16[1,8,64,128]{3,2,1,0:T(8,128)(2,1)}, bf16[1,8,64,128]{3,2,1,0:T(8,128)(2,1)S(1)}, u32[]{:S(2)}, u32[]{:S(2)}) collective-permute-start(bf16[1,8,64,128]{3,2,1,0:T(8,128)(2,1)} %f_hbm.1), channel_id=1, source_target_pairs={{0,8},{4,12},{8,0},{12,4},{1,9},{5,13},{9,1},{13,5},{2,10},{6,14},... | collective-permute-start | bytes 393224 | tf_op jit(solution)/shard_map/ppermute | solution.py:685
  4.8 1.6 %shard_map.110 = (bf16[34,64,384]{2,1,0:T(8,128)(2,1)S(1)}, bf16[34,64,384]{2,1,0:T(8,128)(2,1)S(1)}, bf16[32,64,128]{2,1,0:T(8,128)(2,1)S(1)}, bf16[1,8,64,128]...) custom-call(bf16[1,8,64,128]{3,2,1,0:T(8,128)(2,1)} %f_hbm.1, ...), custom_call_target="tpu_custom_call" | custom-call | bytes 6726656 | tf_op jit(solution)/shard_map/pallas_call | solution.py:19
  6.5 1.9 %collective-permute-start.2 = (bf16[1,8,64,128]{3,2,1,0:T(8,128)(2,1)}, bf16[1,8,64,128]{3,2,1,0:T(8,128)(2,1)S(1)}, u32[]{:S(2)}, u32[]{:S(2)}) collective-permute-start(bf16[1,8,64,128]{3,2,1,0:T(8,128)(2,1)} %f_hbm.1), channel_id=1, source_target_pairs={{0,4},{4,0},{8,12},{12,8},{1,5},{5,1},{9,13},{13,9},{2,6},{6,2},{1... | collective-permute-start | bytes 393224 | tf_op jit(solution)/shard_map/ppermute | solution.py:685
  8.4 6.6 %collective-permute-done.f2_ref = bf16[1,8,64,128]{3,2,1,0:T(8,128)(2,1)S(1)} collective-permute-done((bf16[1,8,64,128]{3,2,1,0:T(8,128)(2,1)}, bf16[1,8,64,128]{3,2,1,0:T(8,128)(2,1)S(1)}, u32[]{:S(2)}, u32[]{:S(2)}) %collective-permute-start) | collective-permute-done | bytes 131104 | tf_op jit(solution)/shard_map/ppermute | solution.py:685
  15.1 1.9 %collective-permute-start.8 = (bf16[1,8,64,128]{3,2,1,0:T(8,128)(2,1)S(1)}, bf16[1,8,64,128]{3,2,1,0:T(8,128)(2,1)S(1)}, u32[]{:S(2)}, u32[]{:S(2)}) collective-permute-start(bf16[1,8,64,128]{3,2,1,0:T(8,128)(2,1)S(1)} %get-tuple-element.44), channel_id=1, source_target_pairs={{0,4},{4,0},{8,12},{12,8},{1,5},{5,1},{9,13},{13,9},{2,6},{6,2},{1... | collective-permute-start | bytes 393224 | tf_op jit(solution)/shard_map/ppermute | solution.py:685
  17.0 0.7 %collective-permute-start.10 = (bf16[1,8,64,128]{3,2,1,0:T(8,128)(2,1)S(1)}, bf16[1,8,64,128]{3,2,1,0:T(8,128)(2,1)S(1)}, u32[]{:S(2)}, u32[]{:S(2)}) collective-permute-start(bf16[1,8,64,128]{3,2,1,0:T(8,128)(2,1)S(1)} %collective-permute-done.9.t2_ref), channel_id=1, source_target_pairs={{0,4},{4,0},{8,12},{12,8},{1,5},{5,1},{9,13},{13,9},{2,6},{6,2},{1... | collective-permute-start | bytes 393224 | tf_op jit(solution)/shard_map/ppermute | solution.py:685
  17.7 3.4 %collective-permute-start.3 = (s32[8,64]{1,0:T(8,128)}, s32[8,64]{1,0:T(8,128)S(1)}, u32[]{:S(2)}, u32[]{:S(2)}) collective-permute-start(s32[8,64]{1,0:T(8,128)} %land_hbm.1), channel_id=1, source_target_pairs={{0,8},{4,12},{8,0},{12,4},{1,9},{5,13},{9,1},{13,5},{2,10},{6,14},... | collective-permute-start | bytes 6152 | tf_op jit(solution)/shard_map/ppermute | solution.py:685
  21.1 2.5 %collective-permute-done.3.b_ref.l2_ref = s32[8,64]{1,0:T(8,128)S(1)} collective-permute-done((s32[8,64]{1,0:T(8,128)}, s32[8,64]{1,0:T(8,128)S(1)}, u32[]{:S(2)}, u32[]{:S(2)}) %collective-permute-start.3) | collective-permute-done | bytes 2080 | tf_op jit(solution)/shard_map/ppermute | solution.py:685
  23.6 4.0 %collective-permute-start.4 = (s32[16,64]{1,0:T(8,128)S(1)}, s32[16,64]{1,0:T(8,128)S(1)}, u32[]{:S(2)}, u32[]{:S(2)}) collective-permute-start(s32[16,64]{1,0:T(8,128)S(1)} %shard_map.111), channel_id=1, source_target_pairs={{0,4},{4,0},{8,12},{12,8},{1,5},{5,1},{9,13},{13,9},{2,6},{6,2},{1... | collective-permute-start | bytes 12296 | tf_op jit(solution)/shard_map/ppermute | solution.py:685
  27.6 1.6 %collective-permute-done.4.l13_ref = s32[16,64]{1,0:T(8,128)S(1)} collective-permute-done((s32[16,64]{1,0:T(8,128)S(1)}, s32[16,64]{1,0:T(8,128)S(1)}, u32[]{:S(2)}, u32[]{:S(2)}) %collective-permute-start.4) | collective-permute-done | bytes 4128 | tf_op jit(solution)/shard_map/ppermute | solution.py:685
  29.3 0.3 shard_map.112
  29.6 1.2 %shard_map.113 = (bf16[34,64,384]{2,1,0:T(8,128)(2,1)S(1)}, bf16[32,64,128]{2,1,0:T(8,128)(2,1)S(1)}, f32[8,128]{1,0:T(8,128)S(1)}) custom-call(bf16[1,8,64,128]{3,2,1,0:T(8,128)(2,1)S(1)} %collective-permute-done.1.f3_ref, bf16[34,64,384]{2,1,0:T(8,128)(2,1)S(1)} %get-tuple-element.38.ss_in, ...), custom_call_target="tpu_custom_call", output_to_operand_aliasing={{0}: (1, {})} | custom-call | flops 603979776 | bytes 5312512 | tf_op jit(solution)/shard_map/pallas_call | solution.py:19
  30.9 1.6 %collective-permute-start.6 = (f32[8,128]{1,0:T(8,128)S(1)}, f32[8,128]{1,0:T(8,128)S(1)}, u32[]{:S(2)}, u32[]{:S(2)}) collective-permute-start(f32[8,128]{1,0:T(8,128)S(1)} %get-tuple-element.42), channel_id=1, source_target_pairs={{0,2},{1,3},{2,0},{3,1},{4,6},{5,7},{6,4},{7,5},{8,10},{9,11},{10,... | collective-permute-start | bytes 12296 | tf_op jit(solution)/shard_map/ppermute | solution.py:310
  32.5 0.3 collective-permute-start.7
  32.8 1.0 %shard_map.117.d_ref = f32[144,1152]{1,0:T(8,128)S(1)} custom-call(bf16[32,64,128]{2,1,0:T(8,128)(2,1)S(1)} %get-tuple-element.41.first_ref, bf16[32,64,128]{2,1,0:T(8,128)(2,1)S(1)} %get-tuple-element.39.mask_ref, bf16[34,64,384]{2,1,0:T(8,128)(2,1)S(1)} %get-tuple-element.52.ss_ref), custom_call_target="tpu_custom_call" | custom-call | flops 603979776 | bytes 3383296 | tf_op jit(solution)/shard_map/pallas_call | solution.py:19
  33.8 1.2 %shard_map.114 = (bf16[34,64,384]{2,1,0:T(8,128)(2,1)S(1)}, f32[32,64,128]{2,1,0:T(8,128)S(1)}) custom-call(bf16[1,8,64,128]{3,2,1,0:T(8,128)(2,1)S(1)} %collective-permute-done.8.t1_ref, bf16[1,8,64,128]{3,2,1,0:T(8,128)(2,1)S(1)} %collective-permute-done.9.t2_ref, ...), custom_call_target="tpu_custom_call", output_to_operand_aliasing={{0}: (4, {})} | custom-call | flops 603979776 | bytes 5570560 | tf_op jit(solution)/shard_map/pallas_call | solution.py:19
  35.0 0.5 collective-permute-done.7
  35.5 1.4 %shard_map.115 = (f32[8,128]{1,0:T(8,128)S(1)}, bf16[32,64,128]{2,1,0:T(8,128)(2,1)S(1)}, bf16[34,64,384]{2,1,0:T(8,128)(2,1)S(1)}) custom-call(bf16[32,64,128]{2,1,0:T(8,128)(2,1)S(1)} %get-tuple-element.41.first_ref, bf16[32,64,128]{2,1,0:T(8,128)(2,1)S(1)} %get-tuple-element.39.mask_ref, f32[8,128]{1,0:T(8,128)S(1)} %add_add_fusion.1.stat_ref, ...), custom_call_target="tpu_custom_call" | custom-call | bytes 4304896 | tf_op jit(solution)/shard_map/pallas_call | solution.py:19
  36.9 0.2 collective-permute-start.11
  37.2 1.2 %collective-permute-start.12 = (f32[8,128]{1,0:T(8,128)S(1)}, f32[8,128]{1,0:T(8,128)S(1)}, u32[]{:S(2)}, u32[]{:S(2)}) collective-permute-start(f32[8,128]{1,0:T(8,128)S(1)} %get-tuple-element.50), channel_id=1, source_target_pairs={{0,2},{1,3},{2,0},{3,1},{4,6},{5,7},{6,4},{7,5},{8,10},{9,11},{10,... | collective-permute-start | bytes 12296 | tf_op jit(solution)/shard_map/ppermute | solution.py:310
  38.4 0.5 collective-permute-start.13
  38.9 1.0 %shard_map.121 = (bf16[2,9,32,128]{3,2,1,0:T(8,128)(2,1)S(1)}, bf16[2,9,32,128]{3,2,1,0:T(8,128)(2,1)S(1)}) custom-call(bf16[34,64,384]{2,1,0:T(8,128)(2,1)S(1)} %get-tuple-element.48.aa_ref, bf16[34,64,384]{2,1,0:T(8,128)(2,1)S(1)} %get-tuple-element.58.tt_ref, f32[8,128]{1,0:T(8,128)S(1)} %add_add_fusion.1.stat_ref), custom_call_target="tpu_custom_call" | custom-call | flops 603979776 | bytes 3641344 | tf_op jit(solution)/shard_map/pallas_call | solution.py:19
  39.8 0.5 %collective-permute-start.16 = (bf16[2,9,32,128]{3,2,1,0:T(8,128)(2,1)S(1)}, bf16[2,9,32,128]{3,2,1,0:T(8,128)(2,1)S(1)}, u32[]{:S(2)}, u32[]{:S(2)}) collective-permute-start(bf16[2,9,32,128]{3,2,1,0:T(8,128)(2,1)S(1)} %get-tuple-element.60), channel_id=1, source_target_pairs={{0,1},{1,0},{2,3},{3,2},{4,5},{5,4},{6,7},{7,6},{8,9},{9,8},{10,11... | collective-permute-start | bytes 442376 | tf_op jit(solution)/shard_map/ppermute | solution.py:516
  40.3 0.9 %shard_map.116.a_ref = f32[128,1152]{1,0:T(8,128)S(1)} custom-call(bf16[32,64,128]{2,1,0:T(8,128)(2,1)S(1)} %get-tuple-element.51.dpre_ref, bf16[34,64,384]{2,1,0:T(8,128)(2,1)S(1)} %get-tuple-element.52.ss_ref), custom_call_target="tpu_custom_call" | custom-call | flops 603979776 | bytes 2785280 | tf_op jit(solution)/shard_map/pallas_call | solution.py:19
  41.4 0.3 shard_map.118
  41.9 1.1 %collective-permute-start.17 = (bf16[1,9,32,128]{3,2,1,0:T(8,128)(2,1)S(1)}, bf16[1,9,32,128]{3,2,1,0:T(8,128)(2,1)S(1)}, u32[]{:S(2)}, u32[]{:S(2)}) collective-permute-start(bf16[1,9,32,128]{3,2,1,0:T(8,128)(2,1)S(1)} %get-tuple-element.62), channel_id=1, source_target_pairs={{0,2},{1,3},{2,0},{3,1},{4,6},{5,7},{6,4},{7,5},{8,10},{9,11},{10,... | collective-permute-start | bytes 221192 | tf_op jit(solution)/shard_map/ppermute | solution.py:516
  43.2 1.2 %collective-permute-start.15 = (bf16[1,9,32,128]{3,2,1,0:T(8,128)(2,1)S(1)}, bf16[1,9,32,128]{3,2,1,0:T(8,128)(2,1)S(1)}, u32[]{:S(2)}, u32[]{:S(2)}) collective-permute-start(bf16[1,9,32,128]{3,2,1,0:T(8,128)(2,1)S(1)} %get-tuple-element.57), channel_id=1, source_target_pairs={{0,2},{1,3},{2,0},{3,1},{4,6},{5,7},{6,4},{7,5},{8,10},{9,11},{10,... | collective-permute-start | bytes 221192 | tf_op jit(solution)/shard_map/ppermute | solution.py:516
  44.4 1.1 %shard_map.120 = (bf16[1,8,64,128]{3,2,1,0:T(8,128)(2,1)}, f32[1,128]{1,0:T(1,128)}, f32[1,128]{1,0:T(1,128)}) custom-call(bf16[34,64,384]{2,1,0:T(8,128)(2,1)S(1)} %get-tuple-element.48.aa_ref, bf16[32,64,128]{2,1,0:T(8,128)(2,1)S(1)} %get-tuple-element.39.mask_ref, bf16[9,128,128]{2,1,0:T(8,128)(2,1)S(1)} %get-tuple-element.49.w_ref, ...), custom_call_target="tpu_custom_call" | custom-call | flops 150994944 | bytes 2700288 | tf_op jit(solution)/shard_map/pallas_call | solution.py:19
  45.5 1.7 %collective-permute-done.17 = bf16[1,9,32,128]{3,2,1,0:T(8,128)(2,1)S(1)} collective-permute-done((bf16[1,9,32,128]{3,2,1,0:T(8,128)(2,1)S(1)}, bf16[1,9,32,128]{3,2,1,0:T(8,128)(2,1)S(1)}, u32[]{:S(2)}, u32[]{:S(2)}) %collective-permute-start.17) | collective-permute-done | bytes 73760 | tf_op jit(solution)/shard_map/ppermute | solution.py:516
  47.1 0.7 %add_bitcast_fusion = f32[9,128,32]{1,2,0:T(8,128)} fusion(bf16[1,9,32,128]{3,2,1,0:T(8,128)(2,1)S(1)} %collective-permute-done.17, bf16[1,9,32,128]{3,2,1,0:T(8,128)(2,1)S(1)} %get-tuple-element.61), kind=kLoop, calls=%fused_computation | loop fusion | flops 110592 | bytes 294912 | tf_op jit(solution)/shard_map/transpose | solution.py:519
  47.8 0.3 collective-permute-done.15
  48.2 0.7 %add_bitcast_fusion.1 = f32[9,128,32]{1,2,0:T(8,128)} fusion(bf16[1,9,32,128]{3,2,1,0:T(8,128)(2,1)S(1)} %collective-permute-done.15, bf16[1,9,32,128]{3,2,1,0:T(8,128)(2,1)S(1)} %get-tuple-element.55.after_ref), kind=kLoop, calls=%fused_computation.1 | loop fusion | flops 110592 | bytes 294912 | tf_op jit(solution)/shard_map/transpose | solution.py:519
  (21 shorter events, 0.8 us)
Async XLA Ops:
  0.6 14.3 %collective-permute-start = (bf16[1,8,64,128]{3,2,1,0:T(8,128)(2,1)}, bf16[1,8,64,128]{3,2,1,0:T(8,128)(2,1)S(1)}, u32[]{:S(2)}, u32[]{:S(2)}) collective-permute-start(bf16[1,8,64,128]{3,2,1,0:T(8,128)(2,1)} %f_hbm.1), channel_id=1, source_target_pairs={{0,8},{4,12},{8,0},{12,4},{1,9},{5,13},{9,1},{13,5},{2,10},{6,14},... | collective-permute-start | bytes 393224 | tf_op jit(solution)/shard_map/ppermute | solution.py:685
  6.4 10.6 %collective-permute-start.9 = (bf16[1,8,64,128]{3,2,1,0:T(8,128)(2,1)S(1)}, bf16[1,8,64,128]{3,2,1,0:T(8,128)(2,1)S(1)}, u32[]{:S(2)}, u32[]{:S(2)}) collective-permute-start(bf16[1,8,64,128]{3,2,1,0:T(8,128)(2,1)S(1)} %get-tuple-element.44), channel_id=1, source_target_pairs={{0,8},{4,12},{8,0},{12,4},{1,9},{5,13},{9,1},{13,5},{2,10},{6,14},... | collective-permute-start | bytes 393224 | tf_op jit(solution)/shard_map/ppermute | solution.py:685
  6.5 22.8 %collective-permute-start.2 = (bf16[1,8,64,128]{3,2,1,0:T(8,128)(2,1)}, bf16[1,8,64,128]{3,2,1,0:T(8,128)(2,1)S(1)}, u32[]{:S(2)}, u32[]{:S(2)}) collective-permute-start(bf16[1,8,64,128]{3,2,1,0:T(8,128)(2,1)} %f_hbm.1), channel_id=1, source_target_pairs={{0,4},{4,0},{8,12},{12,8},{1,5},{5,1},{9,13},{13,9},{2,6},{6,2},{1... | collective-permute-start | bytes 393224 | tf_op jit(solution)/shard_map/ppermute | solution.py:685
  14.9 14.7 %collective-permute-start.1 = (bf16[1,8,64,128]{3,2,1,0:T(8,128)(2,1)S(1)}, bf16[1,8,64,128]{3,2,1,0:T(8,128)(2,1)S(1)}, u32[]{:S(2)}, u32[]{:S(2)}) collective-permute-start(bf16[1,8,64,128]{3,2,1,0:T(8,128)(2,1)S(1)} %collective-permute-done.f2_ref), channel_id=1, source_target_pairs={{0,4},{4,0},{8,12},{12,8},{1,5},{5,1},{9,13},{13,9},{2,6},{6,2},{1... | collective-permute-start | bytes 393224 | tf_op jit(solution)/shard_map/ppermute | solution.py:685
  15.1 18.7 %collective-permute-start.8 = (bf16[1,8,64,128]{3,2,1,0:T(8,128)(2,1)S(1)}, bf16[1,8,64,128]{3,2,1,0:T(8,128)(2,1)S(1)}, u32[]{:S(2)}, u32[]{:S(2)}) collective-permute-start(bf16[1,8,64,128]{3,2,1,0:T(8,128)(2,1)S(1)} %get-tuple-element.44), channel_id=1, source_target_pairs={{0,4},{4,0},{8,12},{12,8},{1,5},{5,1},{9,13},{13,9},{2,6},{6,2},{1... | collective-permute-start | bytes 393224 | tf_op jit(solution)/shard_map/ppermute | solution.py:685
  17.0 16.8 %collective-permute-start.10 = (bf16[1,8,64,128]{3,2,1,0:T(8,128)(2,1)S(1)}, bf16[1,8,64,128]{3,2,1,0:T(8,128)(2,1)S(1)}, u32[]{:S(2)}, u32[]{:S(2)}) collective-permute-start(bf16[1,8,64,128]{3,2,1,0:T(8,128)(2,1)S(1)} %collective-permute-done.9.t2_ref), channel_id=1, source_target_pairs={{0,4},{4,0},{8,12},{12,8},{1,5},{5,1},{9,13},{13,9},{2,6},{6,2},{1... | collective-permute-start | bytes 393224 | tf_op jit(solution)/shard_map/ppermute | solution.py:685
  17.7 5.9 %collective-permute-start.3 = (s32[8,64]{1,0:T(8,128)}, s32[8,64]{1,0:T(8,128)S(1)}, u32[]{:S(2)}, u32[]{:S(2)}) collective-permute-start(s32[8,64]{1,0:T(8,128)} %land_hbm.1), channel_id=1, source_target_pairs={{0,8},{4,12},{8,0},{12,4},{1,9},{5,13},{9,1},{13,5},{2,10},{6,14},... | collective-permute-start | bytes 6152 | tf_op jit(solution)/shard_map/ppermute | solution.py:685
  23.6 5.6 %collective-permute-start.4 = (s32[16,64]{1,0:T(8,128)S(1)}, s32[16,64]{1,0:T(8,128)S(1)}, u32[]{:S(2)}, u32[]{:S(2)}) collective-permute-start(s32[16,64]{1,0:T(8,128)S(1)} %shard_map.111), channel_id=1, source_target_pairs={{0,4},{4,0},{8,12},{12,8},{1,5},{5,1},{9,13},{13,9},{2,6},{6,2},{1... | collective-permute-start | bytes 12296 | tf_op jit(solution)/shard_map/ppermute | solution.py:685
  30.8 4.2 %collective-permute-start.5 = (f32[8,128]{1,0:T(8,128)S(1)}, f32[8,128]{1,0:T(8,128)S(1)}, u32[]{:S(2)}, u32[]{:S(2)}) collective-permute-start(f32[8,128]{1,0:T(8,128)S(1)} %get-tuple-element.42), channel_id=1, source_target_pairs={{0,1},{1,0},{2,3},{3,2},{4,5},{5,4},{6,7},{7,6},{8,9},{9,8},{10,11... | collective-permute-start | bytes 12296 | tf_op jit(solution)/shard_map/ppermute | solution.py:308
  30.9 4.1 %collective-permute-start.6 = (f32[8,128]{1,0:T(8,128)S(1)}, f32[8,128]{1,0:T(8,128)S(1)}, u32[]{:S(2)}, u32[]{:S(2)}) collective-permute-start(f32[8,128]{1,0:T(8,128)S(1)} %get-tuple-element.42), channel_id=1, source_target_pairs={{0,2},{1,3},{2,0},{3,1},{4,6},{5,7},{6,4},{7,5},{8,10},{9,11},{10,... | collective-permute-start | bytes 12296 | tf_op jit(solution)/shard_map/ppermute | solution.py:310
  32.5 3.0 %collective-permute-start.7 = (f32[8,128]{1,0:T(8,128)S(1)}, f32[8,128]{1,0:T(8,128)S(1)}, u32[]{:S(2)}, u32[]{:S(2)}) collective-permute-start(f32[8,128]{1,0:T(8,128)S(1)} %get-tuple-element.42), channel_id=1, source_target_pairs={{0,3},{1,2},{2,1},{3,0},{4,7},{5,6},{6,5},{7,4},{8,11},{9,10},{10,... | collective-permute-start | bytes 12296 | tf_op jit(solution)/shard_map/ppermute | solution.py:311
  36.9 4.3 %collective-permute-start.11 = (f32[8,128]{1,0:T(8,128)S(1)}, f32[8,128]{1,0:T(8,128)S(1)}, u32[]{:S(2)}, u32[]{:S(2)}) collective-permute-start(f32[8,128]{1,0:T(8,128)S(1)} %get-tuple-element.50), channel_id=1, source_target_pairs={{0,1},{1,0},{2,3},{3,2},{4,5},{5,4},{6,7},{7,6},{8,9},{9,8},{10,11... | collective-permute-start | bytes 12296 | tf_op jit(solution)/shard_map/ppermute | solution.py:308
  37.2 4.1 %collective-permute-start.12 = (f32[8,128]{1,0:T(8,128)S(1)}, f32[8,128]{1,0:T(8,128)S(1)}, u32[]{:S(2)}, u32[]{:S(2)}) collective-permute-start(f32[8,128]{1,0:T(8,128)S(1)} %get-tuple-element.50), channel_id=1, source_target_pairs={{0,2},{1,3},{2,0},{3,1},{4,6},{5,7},{6,4},{7,5},{8,10},{9,11},{10,... | collective-permute-start | bytes 12296 | tf_op jit(solution)/shard_map/ppermute | solution.py:310
  38.4 3.0 %collective-permute-start.13 = (f32[8,128]{1,0:T(8,128)S(1)}, f32[8,128]{1,0:T(8,128)S(1)}, u32[]{:S(2)}, u32[]{:S(2)}) collective-permute-start(f32[8,128]{1,0:T(8,128)S(1)} %get-tuple-element.50), channel_id=1, source_target_pairs={{0,3},{1,2},{2,1},{3,0},{4,7},{5,6},{6,5},{7,4},{8,11},{9,10},{10,... | collective-permute-start | bytes 12296 | tf_op jit(solution)/shard_map/ppermute | solution.py:311
  39.8 2.1 %collective-permute-start.16 = (bf16[2,9,32,128]{3,2,1,0:T(8,128)(2,1)S(1)}, bf16[2,9,32,128]{3,2,1,0:T(8,128)(2,1)S(1)}, u32[]{:S(2)}, u32[]{:S(2)}) collective-permute-start(bf16[2,9,32,128]{3,2,1,0:T(8,128)(2,1)S(1)} %get-tuple-element.60), channel_id=1, source_target_pairs={{0,1},{1,0},{2,3},{3,2},{4,5},{5,4},{6,7},{7,6},{8,9},{9,8},{10,11... | collective-permute-start | bytes 442376 | tf_op jit(solution)/shard_map/ppermute | solution.py:516
  41.7 1.4 %collective-permute-start.14 = (bf16[2,9,32,128]{3,2,1,0:T(8,128)(2,1)S(1)}, bf16[2,9,32,128]{3,2,1,0:T(8,128)(2,1)S(1)}, u32[]{:S(2)}, u32[]{:S(2)}) collective-permute-start(bf16[2,9,32,128]{3,2,1,0:T(8,128)(2,1)S(1)} %get-tuple-element.54), channel_id=1, source_target_pairs={{0,1},{1,0},{2,3},{3,2},{4,5},{5,4},{6,7},{7,6},{8,9},{9,8},{10,11... | collective-permute-start | bytes 442376 | tf_op jit(solution)/shard_map/ppermute | solution.py:516
  41.9 5.2 %collective-permute-start.17 = (bf16[1,9,32,128]{3,2,1,0:T(8,128)(2,1)S(1)}, bf16[1,9,32,128]{3,2,1,0:T(8,128)(2,1)S(1)}, u32[]{:S(2)}, u32[]{:S(2)}) collective-permute-start(bf16[1,9,32,128]{3,2,1,0:T(8,128)(2,1)S(1)} %get-tuple-element.62), channel_id=1, source_target_pairs={{0,2},{1,3},{2,0},{3,1},{4,6},{5,7},{6,4},{7,5},{8,10},{9,11},{10,... | collective-permute-start | bytes 221192 | tf_op jit(solution)/shard_map/ppermute | solution.py:516
  43.2 5.0 %collective-permute-start.15 = (bf16[1,9,32,128]{3,2,1,0:T(8,128)(2,1)S(1)}, bf16[1,9,32,128]{3,2,1,0:T(8,128)(2,1)S(1)}, u32[]{:S(2)}, u32[]{:S(2)}) collective-permute-start(bf16[1,9,32,128]{3,2,1,0:T(8,128)(2,1)S(1)} %get-tuple-element.57), channel_id=1, source_target_pairs={{0,2},{1,3},{2,0},{3,1},{4,6},{5,7},{6,4},{7,5},{8,10},{9,11},{10,... | collective-permute-start | bytes 221192 | tf_op jit(solution)/shard_map/ppermute | solution.py:516

commit v3 on v2

--- a/solution.py
+++ b/solution.py
@@ -442,10 +442,18 @@
     stat_ref[...] = jnp.concatenate(rows + [jnp.zeros((5, chans), F32)], axis=0)
 
 
-def sample_adjoint(lon, lat, chans, t1_ref, t2_ref, t3_ref, wt_ref, tt_in, tt_ref, dact_ref):
+def sample_place(lon, t1_ref, t2_ref, tt_in, tt_ref):
+    me = lax.axis_index("space")
+    for k, t_ref in ((1, t1_ref), (2, t2_ref)):
+        start = jnp.bitwise_xor(me, k) * lon
+        for i in range(lon):
+            put_shifted(tt_ref, start + i + 1, t_ref[0, i].astype(F32), -1)
+
+
+def sample_adjoint(lon, lat, chans, t3_ref, wt_ref, tt_in, tt_ref, dact_ref):
     nx = dact_ref.shape[0]
     me = lax.axis_index("space")
-    for k, t_ref in ((1, t1_ref), (2, t2_ref), (3, t3_ref)):
+    for k, t_ref in ((3, t3_ref),):
         start = jnp.bitwise_xor(me, k) * lon
         for i in range(lon):
             put_shifted(tt_ref, start + i + 1, t_ref[0, i].astype(F32), -1)
@@ -722,8 +730,9 @@
         functools.partial(sample_conv, *sizes), [shifted, cells, sums], [f3, ss, mask, win], flops=work, alias={1: 0}
     )
     stat = all_sum(stat, "batch")
+    (tt,) = run(functools.partial(sample_place, lon), [shifted], [t1, t2, tt], alias={2: 0})
     tt, dact = run(
-        functools.partial(sample_adjoint, *sizes), [shifted, cells_f], [t1, t2, t3, wt, tt], flops=work, alias={4: 0}
+        functools.partial(sample_adjoint, *sizes), [shifted, cells_f], [t3, wt, tt], flops=work, alias={2: 0}
     )
     (static,) = run(
         functools.partial(sample_static, lat, chans), [sds((chans + 16, 9 * chans), F32)], [first, mask, ss], flops=work

time: 49 us -> 46.5 us (0.949)
  starting transfers between devices: 23.1 us -> 19.4 us
  waiting for transfers between devices: 13.5 us -> 14.5 us
    ppermute x8, starting transfers between devices: 16.2 us -> 12.7 us  [sample_body(): move = lambda x, pairs: lax.ppermute(x, 'space', pairs)]
    ppermute x8, waiting for transfers between devices: 10.8 us -> 11.8 us  [sample_body(): move = lambda x, pairs: lax.ppermute(x, 'space', pairs)]
    pallas_call x13 -> x14, Pallas kernels: 10.2 us -> 10.2 us  [run(): pl.pallas_call(body, out_shape=list(outs), in_specs=[space] * len(args),...]
  transfers between devices with their start and end apart: 18 -> 18, of which waited for: 8 -> 8; matrix products, arithmetic and copies ran while one was open for 1% -> 1% of each run, Pallas kernels for 18% -> 19%
where the time goes in v3:
time: 46.5 us; the launch traced here: 46.3 us
  starting transfers between devices  19.4 us (42%)
  waiting for transfers between devices  14.5 us (31%)
  Pallas kernels  10.2 us (22%)
  other arithmetic  1.37 us (3%)
  between operations  0.78 us (2%)
    ppermute x8, starting transfers between devices, sample_body(): move = lambda x, pairs: lax.ppermute(x, 'space', pairs)  12.7 us
    ppermute x8, waiting for transfers between devices, sample_body(): move = lambda x, pairs: lax.ppermute(x, 'space', pairs)  11.8 us
    pallas_call x14, Pallas kernels, run(): pl.pallas_call(body, out_shape=list(outs), in_specs=[space] * len(args),...  10.2 us
    ppermute x4, starting transfers between devices, exchange_sum(): got = lax.ppermute(send, 'batch', xor_pairs(size, bit))  2.94 us
    ppermute x2, starting transfers between devices, all_sum(): far = lax.ppermute(x, axis, xor_pairs(size, 2 * bit))  2.65 us
    ppermute x4, waiting for transfers between devices, exchange_sum(): got = lax.ppermute(send, 'batch', xor_pairs(size, bit))  2.12 us
    transpose x2, other arithmetic, exchange_sum(): return (jnp.swapaxes(keep[0].astype(F32) + got[0].astype(F32), 1, 2), keep)  1.36 us
  transfers between devices with their start and end apart: 18, of which 8 were waited for; matrix products, arithmetic and copies ran while one was open for 1% of the time, Pallas kernels for 19%

profile of v3, /device:TPU:0, one launch (start us, length us, event | category | flops | bytes accessed | tf_op | source)
XLA Modules:
  0.0 46.3 jit_solution(5790062725551910620)
XLA Ops:
  0.6 4.1 %collective-permute-start = (bf16[1,8,64,128]{3,2,1,0:T(8,128)(2,1)}, bf16[1,8,64,128]{3,2,1,0:T(8,128)(2,1)S(1)}, u32[]{:S(2)}, u32[]{:S(2)}) collective-permute-start(bf16[1,8,64,128]{3,2,1,0:T(8,128)(2,1)} %f_hbm.1), channel_id=1, source_target_pairs={{0,8},{4,12},{8,0},{12,4},{1,9},{5,13},{9,1},{13,5},{2,10},{6,14},... | collective-permute-start | bytes 393224 | tf_op jit(solution)/shard_map/ppermute | solution.py:693
  4.8 1.6 %shard_map.110 = (bf16[34,64,384]{2,1,0:T(8,128)(2,1)S(1)}, bf16[34,64,384]{2,1,0:T(8,128)(2,1)S(1)}, bf16[32,64,128]{2,1,0:T(8,128)(2,1)S(1)}, bf16[1,8,64,128]...) custom-call(bf16[1,8,64,128]{3,2,1,0:T(8,128)(2,1)} %f_hbm.1, ...), custom_call_target="tpu_custom_call" | custom-call | bytes 6726656 | tf_op jit(solution)/shard_map/pallas_call | solution.py:19
  6.5 1.9 %collective-permute-start.10 = (bf16[1,8,64,128]{3,2,1,0:T(8,128)(2,1)S(1)}, bf16[1,8,64,128]{3,2,1,0:T(8,128)(2,1)S(1)}, u32[]{:S(2)}, u32[]{:S(2)}) collective-permute-start(bf16[1,8,64,128]{3,2,1,0:T(8,128)(2,1)S(1)} %get-tuple-element.44), channel_id=1, source_target_pairs={{0,4},{4,0},{8,12},{12,8},{1,5},{5,1},{9,13},{13,9},{2,6},{6,2},{1... | collective-permute-start | bytes 393224 | tf_op jit(solution)/shard_map/ppermute | solution.py:693
  8.5 6.5 %collective-permute-done.f2_ref = bf16[1,8,64,128]{3,2,1,0:T(8,128)(2,1)S(1)} collective-permute-done((bf16[1,8,64,128]{3,2,1,0:T(8,128)(2,1)}, bf16[1,8,64,128]{3,2,1,0:T(8,128)(2,1)S(1)}, u32[]{:S(2)}, u32[]{:S(2)}) %collective-permute-start) | collective-permute-done | bytes 131104 | tf_op jit(solution)/shard_map/ppermute | solution.py:693
  15.1 1.9 %collective-permute-done.8.t2_ref = bf16[1,8,64,128]{3,2,1,0:T(8,128)(2,1)S(1)} collective-permute-done((bf16[1,8,64,128]{3,2,1,0:T(8,128)(2,1)S(1)}, bf16[1,8,64,128]{3,2,1,0:T(8,128)(2,1)S(1)}, u32[]{:S(2)}, u32[]{:S(2)}) %collective-permute-start.8) | collective-permute-done | bytes 131104 | tf_op jit(solution)/shard_map/ppermute | solution.py:693
  17.0 0.7 %collective-permute-start.9 = (bf16[1,8,64,128]{3,2,1,0:T(8,128)(2,1)S(1)}, bf16[1,8,64,128]{3,2,1,0:T(8,128)(2,1)S(1)}, u32[]{:S(2)}, u32[]{:S(2)}) collective-permute-start(bf16[1,8,64,128]{3,2,1,0:T(8,128)(2,1)S(1)} %collective-permute-done.8.t2_ref), channel_id=1, source_target_pairs={{0,4},{4,0},{8,12},{12,8},{1,5},{5,1},{9,13},{13,9},{2,6},{6,2},{1... | collective-permute-start | bytes 393224 | tf_op jit(solution)/shard_map/ppermute | solution.py:693
  17.7 3.4 %collective-permute-start.3 = (s32[8,64]{1,0:T(8,128)}, s32[8,64]{1,0:T(8,128)S(1)}, u32[]{:S(2)}, u32[]{:S(2)}) collective-permute-start(s32[8,64]{1,0:T(8,128)} %land_hbm.1), channel_id=1, source_target_pairs={{0,8},{4,12},{8,0},{12,4},{1,9},{5,13},{9,1},{13,5},{2,10},{6,14},... | collective-permute-start | bytes 6152 | tf_op jit(solution)/shard_map/ppermute | solution.py:693
  21.1 1.9 %collective-permute-done.3.b_ref.l2_ref = s32[8,64]{1,0:T(8,128)S(1)} collective-permute-done((s32[8,64]{1,0:T(8,128)}, s32[8,64]{1,0:T(8,128)S(1)}, u32[]{:S(2)}, u32[]{:S(2)}) %collective-permute-start.3) | collective-permute-done | bytes 2080 | tf_op jit(solution)/shard_map/ppermute | solution.py:693
  23.0 2.2 %collective-permute-start.4 = (s32[16,64]{1,0:T(8,128)S(1)}, s32[16,64]{1,0:T(8,128)S(1)}, u32[]{:S(2)}, u32[]{:S(2)}) collective-permute-start(s32[16,64]{1,0:T(8,128)S(1)} %shard_map.111), channel_id=1, source_target_pairs={{0,4},{4,0},{8,12},{12,8},{1,5},{5,1},{9,13},{13,9},{2,6},{6,2},{1... | collective-permute-start | bytes 12296 | tf_op jit(solution)/shard_map/ppermute | solution.py:693
  25.4 1.4 %collective-permute-done.4.l13_ref = s32[16,64]{1,0:T(8,128)S(1)} collective-permute-done((s32[16,64]{1,0:T(8,128)S(1)}, s32[16,64]{1,0:T(8,128)S(1)}, u32[]{:S(2)}, u32[]{:S(2)}) %collective-permute-start.4) | collective-permute-done | bytes 4128 | tf_op jit(solution)/shard_map/ppermute | solution.py:693
  26.9 0.3 shard_map.112
  27.2 1.2 %shard_map.113 = (bf16[34,64,384]{2,1,0:T(8,128)(2,1)S(1)}, bf16[32,64,128]{2,1,0:T(8,128)(2,1)S(1)}, f32[8,128]{1,0:T(8,128)S(1)}) custom-call(bf16[1,8,64,128]{3,2,1,0:T(8,128)(2,1)S(1)} %collective-permute-done.1.f3_ref, bf16[34,64,384]{2,1,0:T(8,128)(2,1)S(1)} %get-tuple-element.38.ss_in, ...), custom_call_target="tpu_custom_call", output_to_operand_aliasing={{0}: (1, {})} | custom-call | flops 603979776 | bytes 5312512 | tf_op jit(solution)/shard_map/pallas_call | solution.py:19
  28.5 1.6 %collective-permute-start.6 = (f32[8,128]{1,0:T(8,128)S(1)}, f32[8,128]{1,0:T(8,128)S(1)}, u32[]{:S(2)}, u32[]{:S(2)}) collective-permute-start(f32[8,128]{1,0:T(8,128)S(1)} %get-tuple-element.42), channel_id=1, source_target_pairs={{0,2},{1,3},{2,0},{3,1},{4,6},{5,7},{6,4},{7,5},{8,10},{9,11},{10,... | collective-permute-start | bytes 12296 | tf_op jit(solution)/shard_map/ppermute | solution.py:310
  30.1 0.3 collective-permute-start.7
  30.4 1.0 %shard_map.118.d_ref = f32[144,1152]{1,0:T(8,128)S(1)} custom-call(bf16[32,64,128]{2,1,0:T(8,128)(2,1)S(1)} %get-tuple-element.41.first_ref, bf16[32,64,128]{2,1,0:T(8,128)(2,1)S(1)} %get-tuple-element.39.mask_ref, bf16[34,64,384]{2,1,0:T(8,128)(2,1)S(1)} %get-tuple-element.52.ss_ref), custom_call_target="tpu_custom_call" | custom-call | flops 603979776 | bytes 3383296 | tf_op jit(solution)/shard_map/pallas_call | solution.py:19
  31.4 1.1 %shard_map.115 = (bf16[34,64,384]{2,1,0:T(8,128)(2,1)S(1)}, f32[32,64,128]{2,1,0:T(8,128)S(1)}) custom-call(bf16[1,8,64,128]{3,2,1,0:T(8,128)(2,1)S(1)} %collective-permute-done.9.t3_ref, bf16[1536,256]{1,0:T(8,128)(2,1)S(1)} %get-tuple-element.45.wt_ref, bf16[34,64,384]{2,1,0:T(8,128)(2,1)S(1)} %shard_map.114.tt_in), custom_call_target="tpu_custom_call", output_to_operand_aliasing={{0}: (2, {})} | custom-call | flops 603979776 | bytes 5308416 | tf_op jit(solution)/shard_map/pallas_call | solution.py:19
  32.5 0.6 %collective-permute-done.7 = f32[8,128]{1,0:T(8,128)S(1)} collective-permute-done((f32[8,128]{1,0:T(8,128)S(1)}, f32[8,128]{1,0:T(8,128)S(1)}, u32[]{:S(2)}, u32[]{:S(2)}) %collective-permute-start.7) | collective-permute-done | bytes 4128 | tf_op jit(solution)/shard_map/ppermute | solution.py:311
  33.1 1.4 %shard_map.116 = (f32[8,128]{1,0:T(8,128)S(1)}, bf16[32,64,128]{2,1,0:T(8,128)(2,1)S(1)}, bf16[34,64,384]{2,1,0:T(8,128)(2,1)S(1)}) custom-call(bf16[32,64,128]{2,1,0:T(8,128)(2,1)S(1)} %get-tuple-element.41.first_ref, bf16[32,64,128]{2,1,0:T(8,128)(2,1)S(1)} %get-tuple-element.39.mask_ref, f32[8,128]{1,0:T(8,128)S(1)} %add_add_fusion.1.stat_ref, ...), custom_call_target="tpu_custom_call" | custom-call | bytes 4304896 | tf_op jit(solution)/shard_map/pallas_call | solution.py:19
  34.6 0.2 collective-permute-start.11
  34.8 1.1 %collective-permute-start.12 = (f32[8,128]{1,0:T(8,128)S(1)}, f32[8,128]{1,0:T(8,128)S(1)}, u32[]{:S(2)}, u32[]{:S(2)}) collective-permute-start(f32[8,128]{1,0:T(8,128)S(1)} %get-tuple-element.50), channel_id=1, source_target_pairs={{0,2},{1,3},{2,0},{3,1},{4,6},{5,7},{6,4},{7,5},{8,10},{9,11},{10,... | collective-permute-start | bytes 12296 | tf_op jit(solution)/shard_map/ppermute | solution.py:310
  35.9 0.6 %collective-permute-start.13 = (f32[8,128]{1,0:T(8,128)S(1)}, f32[8,128]{1,0:T(8,128)S(1)}, u32[]{:S(2)}, u32[]{:S(2)}) collective-permute-start(f32[8,128]{1,0:T(8,128)S(1)} %get-tuple-element.50), channel_id=1, source_target_pairs={{0,3},{1,2},{2,1},{3,0},{4,7},{5,6},{6,5},{7,4},{8,11},{9,10},{10,... | collective-permute-start | bytes 12296 | tf_op jit(solution)/shard_map/ppermute | solution.py:311
  36.5 1.0 %shard_map.122 = (bf16[2,9,32,128]{3,2,1,0:T(8,128)(2,1)S(1)}, bf16[2,9,32,128]{3,2,1,0:T(8,128)(2,1)S(1)}) custom-call(bf16[34,64,384]{2,1,0:T(8,128)(2,1)S(1)} %get-tuple-element.48.aa_ref, bf16[34,64,384]{2,1,0:T(8,128)(2,1)S(1)} %get-tuple-element.58.tt_ref, f32[8,128]{1,0:T(8,128)S(1)} %add_add_fusion.1.stat_ref), custom_call_target="tpu_custom_call" | custom-call | flops 603979776 | bytes 3641344 | tf_op jit(solution)/shard_map/pallas_call | solution.py:19
  37.5 0.5 %collective-permute-start.16 = (bf16[2,9,32,128]{3,2,1,0:T(8,128)(2,1)S(1)}, bf16[2,9,32,128]{3,2,1,0:T(8,128)(2,1)S(1)}, u32[]{:S(2)}, u32[]{:S(2)}) collective-permute-start(bf16[2,9,32,128]{3,2,1,0:T(8,128)(2,1)S(1)} %get-tuple-element.60), channel_id=1, source_target_pairs={{0,1},{1,0},{2,3},{3,2},{4,5},{5,4},{6,7},{7,6},{8,9},{9,8},{10,11... | collective-permute-start | bytes 442376 | tf_op jit(solution)/shard_map/ppermute | solution.py:524
  38.0 0.9 %shard_map.117.a_ref = f32[128,1152]{1,0:T(8,128)S(1)} custom-call(bf16[32,64,128]{2,1,0:T(8,128)(2,1)S(1)} %get-tuple-element.51.dpre_ref, bf16[34,64,384]{2,1,0:T(8,128)(2,1)S(1)} %get-tuple-element.52.ss_ref), custom_call_target="tpu_custom_call" | custom-call | flops 603979776 | bytes 2785280 | tf_op jit(solution)/shard_map/pallas_call | solution.py:19
  39.0 0.3 shard_map.119
  39.4 1.1 %collective-permute-start.17 = (bf16[1,9,32,128]{3,2,1,0:T(8,128)(2,1)S(1)}, bf16[1,9,32,128]{3,2,1,0:T(8,128)(2,1)S(1)}, u32[]{:S(2)}, u32[]{:S(2)}) collective-permute-start(bf16[1,9,32,128]{3,2,1,0:T(8,128)(2,1)S(1)} %get-tuple-element.62), channel_id=1, source_target_pairs={{0,2},{1,3},{2,0},{3,1},{4,6},{5,7},{6,4},{7,5},{8,10},{9,11},{10,... | collective-permute-start | bytes 221192 | tf_op jit(solution)/shard_map/ppermute | solution.py:524
  40.7 1.2 %collective-permute-start.15 = (bf16[1,9,32,128]{3,2,1,0:T(8,128)(2,1)S(1)}, bf16[1,9,32,128]{3,2,1,0:T(8,128)(2,1)S(1)}, u32[]{:S(2)}, u32[]{:S(2)}) collective-permute-start(bf16[1,9,32,128]{3,2,1,0:T(8,128)(2,1)S(1)} %get-tuple-element.57), channel_id=1, source_target_pairs={{0,2},{1,3},{2,0},{3,1},{4,6},{5,7},{6,4},{7,5},{8,10},{9,11},{10,... | collective-permute-start | bytes 221192 | tf_op jit(solution)/shard_map/ppermute | solution.py:524
  41.9 1.1 %shard_map.121 = (bf16[1,8,64,128]{3,2,1,0:T(8,128)(2,1)}, f32[1,128]{1,0:T(1,128)}, f32[1,128]{1,0:T(1,128)}) custom-call(bf16[34,64,384]{2,1,0:T(8,128)(2,1)S(1)} %get-tuple-element.48.aa_ref, bf16[32,64,128]{2,1,0:T(8,128)(2,1)S(1)} %get-tuple-element.39.mask_ref, bf16[9,128,128]{2,1,0:T(8,128)(2,1)S(1)} %get-tuple-element.49.w_ref, ...), custom_call_target="tpu_custom_call" | custom-call | flops 150994944 | bytes 2700288 | tf_op jit(solution)/shard_map/pallas_call | solution.py:19
  43.0 1.6 %collective-permute-done.17 = bf16[1,9,32,128]{3,2,1,0:T(8,128)(2,1)S(1)} collective-permute-done((bf16[1,9,32,128]{3,2,1,0:T(8,128)(2,1)S(1)}, bf16[1,9,32,128]{3,2,1,0:T(8,128)(2,1)S(1)}, u32[]{:S(2)}, u32[]{:S(2)}) %collective-permute-start.17) | collective-permute-done | bytes 73760 | tf_op jit(solution)/shard_map/ppermute | solution.py:524
  44.6 0.7 %add_bitcast_fusion = f32[9,128,32]{1,2,0:T(8,128)} fusion(bf16[1,9,32,128]{3,2,1,0:T(8,128)(2,1)S(1)} %collective-permute-done.17, bf16[1,9,32,128]{3,2,1,0:T(8,128)(2,1)S(1)} %get-tuple-element.61), kind=kLoop, calls=%fused_computation | loop fusion | flops 110592 | bytes 294912 | tf_op jit(solution)/shard_map/transpose | solution.py:527
  45.3 0.4 collective-permute-done.15
  45.7 0.7 %add_bitcast_fusion.1 = f32[9,128,32]{1,2,0:T(8,128)} fusion(bf16[1,9,32,128]{3,2,1,0:T(8,128)(2,1)S(1)} %collective-permute-done.15, bf16[1,9,32,128]{3,2,1,0:T(8,128)(2,1)S(1)} %get-tuple-element.55.after_ref), kind=kLoop, calls=%fused_computation.1 | loop fusion | flops 110592 | bytes 294912 | tf_op jit(solution)/shard_map/transpose | solution.py:527
  (22 shorter events, 0.9 us)
Async XLA Ops:
  0.6 14.4 %collective-permute-start = (bf16[1,8,64,128]{3,2,1,0:T(8,128)(2,1)}, bf16[1,8,64,128]{3,2,1,0:T(8,128)(2,1)S(1)}, u32[]{:S(2)}, u32[]{:S(2)}) collective-permute-start(bf16[1,8,64,128]{3,2,1,0:T(8,128)(2,1)} %f_hbm.1), channel_id=1, source_target_pairs={{0,8},{4,12},{8,0},{12,4},{1,9},{5,13},{9,1},{13,5},{2,10},{6,14},... | collective-permute-start | bytes 393224 | tf_op jit(solution)/shard_map/ppermute | solution.py:693
  6.4 10.6 %collective-permute-start.8 = (bf16[1,8,64,128]{3,2,1,0:T(8,128)(2,1)S(1)}, bf16[1,8,64,128]{3,2,1,0:T(8,128)(2,1)S(1)}, u32[]{:S(2)}, u32[]{:S(2)}) collective-permute-start(bf16[1,8,64,128]{3,2,1,0:T(8,128)(2,1)S(1)} %get-tuple-element.44), channel_id=1, source_target_pairs={{0,8},{4,12},{8,0},{12,4},{1,9},{5,13},{9,1},{13,5},{2,10},{6,14},... | collective-permute-start | bytes 393224 | tf_op jit(solution)/shard_map/ppermute | solution.py:693
  6.5 18.8 %collective-permute-start.10 = (bf16[1,8,64,128]{3,2,1,0:T(8,128)(2,1)S(1)}, bf16[1,8,64,128]{3,2,1,0:T(8,128)(2,1)S(1)}, u32[]{:S(2)}, u32[]{:S(2)}) collective-permute-start(bf16[1,8,64,128]{3,2,1,0:T(8,128)(2,1)S(1)} %get-tuple-element.44), channel_id=1, source_target_pairs={{0,4},{4,0},{8,12},{12,8},{1,5},{5,1},{9,13},{13,9},{2,6},{6,2},{1... | collective-permute-start | bytes 393224 | tf_op jit(solution)/shard_map/ppermute | solution.py:693
  8.4 18.5 %collective-permute-start.2 = (bf16[1,8,64,128]{3,2,1,0:T(8,128)(2,1)}, bf16[1,8,64,128]{3,2,1,0:T(8,128)(2,1)S(1)}, u32[]{:S(2)}, u32[]{:S(2)}) collective-permute-start(bf16[1,8,64,128]{3,2,1,0:T(8,128)(2,1)} %f_hbm.1), channel_id=1, source_target_pairs={{0,4},{4,0},{8,12},{12,8},{1,5},{5,1},{9,13},{13,9},{2,6},{6,2},{1... | collective-permute-start | bytes 393224 | tf_op jit(solution)/shard_map/ppermute | solution.py:693
  15.0 12.2 %collective-permute-start.1 = (bf16[1,8,64,128]{3,2,1,0:T(8,128)(2,1)S(1)}, bf16[1,8,64,128]{3,2,1,0:T(8,128)(2,1)S(1)}, u32[]{:S(2)}, u32[]{:S(2)}) collective-permute-start(bf16[1,8,64,128]{3,2,1,0:T(8,128)(2,1)S(1)} %collective-permute-done.f2_ref), channel_id=1, source_target_pairs={{0,4},{4,0},{8,12},{12,8},{1,5},{5,1},{9,13},{13,9},{2,6},{6,2},{1... | collective-permute-start | bytes 393224 | tf_op jit(solution)/shard_map/ppermute | solution.py:693
  17.0 14.4 %collective-permute-start.9 = (bf16[1,8,64,128]{3,2,1,0:T(8,128)(2,1)S(1)}, bf16[1,8,64,128]{3,2,1,0:T(8,128)(2,1)S(1)}, u32[]{:S(2)}, u32[]{:S(2)}) collective-permute-start(bf16[1,8,64,128]{3,2,1,0:T(8,128)(2,1)S(1)} %collective-permute-done.8.t2_ref), channel_id=1, source_target_pairs={{0,4},{4,0},{8,12},{12,8},{1,5},{5,1},{9,13},{13,9},{2,6},{6,2},{1... | collective-permute-start | bytes 393224 | tf_op jit(solution)/shard_map/ppermute | solution.py:693
  17.7 5.3 %collective-permute-start.3 = (s32[8,64]{1,0:T(8,128)}, s32[8,64]{1,0:T(8,128)S(1)}, u32[]{:S(2)}, u32[]{:S(2)}) collective-permute-start(s32[8,64]{1,0:T(8,128)} %land_hbm.1), channel_id=1, source_target_pairs={{0,8},{4,12},{8,0},{12,4},{1,9},{5,13},{9,1},{13,5},{2,10},{6,14},... | collective-permute-start | bytes 6152 | tf_op jit(solution)/shard_map/ppermute | solution.py:693
  23.0 3.9 %collective-permute-start.4 = (s32[16,64]{1,0:T(8,128)S(1)}, s32[16,64]{1,0:T(8,128)S(1)}, u32[]{:S(2)}, u32[]{:S(2)}) collective-permute-start(s32[16,64]{1,0:T(8,128)S(1)} %shard_map.111), channel_id=1, source_target_pairs={{0,4},{4,0},{8,12},{12,8},{1,5},{5,1},{9,13},{13,9},{2,6},{6,2},{1... | collective-permute-start | bytes 12296 | tf_op jit(solution)/shard_map/ppermute | solution.py:693
  28.5 4.0 %collective-permute-start.5 = (f32[8,128]{1,0:T(8,128)S(1)}, f32[8,128]{1,0:T(8,128)S(1)}, u32[]{:S(2)}, u32[]{:S(2)}) collective-permute-start(f32[8,128]{1,0:T(8,128)S(1)} %get-tuple-element.42), channel_id=1, source_target_pairs={{0,1},{1,0},{2,3},{3,2},{4,5},{5,4},{6,7},{7,6},{8,9},{9,8},{10,11... | collective-permute-start | bytes 12296 | tf_op jit(solution)/shard_map/ppermute | solution.py:308
  28.5 4.0 %collective-permute-start.6 = (f32[8,128]{1,0:T(8,128)S(1)}, f32[8,128]{1,0:T(8,128)S(1)}, u32[]{:S(2)}, u32[]{:S(2)}) collective-permute-start(f32[8,128]{1,0:T(8,128)S(1)} %get-tuple-element.42), channel_id=1, source_target_pairs={{0,2},{1,3},{2,0},{3,1},{4,6},{5,7},{6,4},{7,5},{8,10},{9,11},{10,... | collective-permute-start | bytes 12296 | tf_op jit(solution)/shard_map/ppermute | solution.py:310
  30.1 3.0 %collective-permute-start.7 = (f32[8,128]{1,0:T(8,128)S(1)}, f32[8,128]{1,0:T(8,128)S(1)}, u32[]{:S(2)}, u32[]{:S(2)}) collective-permute-start(f32[8,128]{1,0:T(8,128)S(1)} %get-tuple-element.42), channel_id=1, source_target_pairs={{0,3},{1,2},{2,1},{3,0},{4,7},{5,6},{6,5},{7,4},{8,11},{9,10},{10,... | collective-permute-start | bytes 12296 | tf_op jit(solution)/shard_map/ppermute | solution.py:311
  34.6 4.3 %collective-permute-start.11 = (f32[8,128]{1,0:T(8,128)S(1)}, f32[8,128]{1,0:T(8,128)S(1)}, u32[]{:S(2)}, u32[]{:S(2)}) collective-permute-start(f32[8,128]{1,0:T(8,128)S(1)} %get-tuple-element.50), channel_id=1, source_target_pairs={{0,1},{1,0},{2,3},{3,2},{4,5},{5,4},{6,7},{7,6},{8,9},{9,8},{10,11... | collective-permute-start | bytes 12296 | tf_op jit(solution)/shard_map/ppermute | solution.py:308
  34.8 4.1 %collective-permute-start.12 = (f32[8,128]{1,0:T(8,128)S(1)}, f32[8,128]{1,0:T(8,128)S(1)}, u32[]{:S(2)}, u32[]{:S(2)}) collective-permute-start(f32[8,128]{1,0:T(8,128)S(1)} %get-tuple-element.50), channel_id=1, source_target_pairs={{0,2},{1,3},{2,0},{3,1},{4,6},{5,7},{6,4},{7,5},{8,10},{9,11},{10,... | collective-permute-start | bytes 12296 | tf_op jit(solution)/shard_map/ppermute | solution.py:310
  35.9 3.0 %collective-permute-start.13 = (f32[8,128]{1,0:T(8,128)S(1)}, f32[8,128]{1,0:T(8,128)S(1)}, u32[]{:S(2)}, u32[]{:S(2)}) collective-permute-start(f32[8,128]{1,0:T(8,128)S(1)} %get-tuple-element.50), channel_id=1, source_target_pairs={{0,3},{1,2},{2,1},{3,0},{4,7},{5,6},{6,5},{7,4},{8,11},{9,10},{10,... | collective-permute-start | bytes 12296 | tf_op jit(solution)/shard_map/ppermute | solution.py:311
  37.5 1.9 %collective-permute-start.16 = (bf16[2,9,32,128]{3,2,1,0:T(8,128)(2,1)S(1)}, bf16[2,9,32,128]{3,2,1,0:T(8,128)(2,1)S(1)}, u32[]{:S(2)}, u32[]{:S(2)}) collective-permute-start(bf16[2,9,32,128]{3,2,1,0:T(8,128)(2,1)S(1)} %get-tuple-element.60), channel_id=1, source_target_pairs={{0,1},{1,0},{2,3},{3,2},{4,5},{5,4},{6,7},{7,6},{8,9},{9,8},{10,11... | collective-permute-start | bytes 442376 | tf_op jit(solution)/shard_map/ppermute | solution.py:524
  39.2 1.4 %collective-permute-start.14 = (bf16[2,9,32,128]{3,2,1,0:T(8,128)(2,1)S(1)}, bf16[2,9,32,128]{3,2,1,0:T(8,128)(2,1)S(1)}, u32[]{:S(2)}, u32[]{:S(2)}) collective-permute-start(bf16[2,9,32,128]{3,2,1,0:T(8,128)(2,1)S(1)} %get-tuple-element.54), channel_id=1, source_target_pairs={{0,1},{1,0},{2,3},{3,2},{4,5},{5,4},{6,7},{7,6},{8,9},{9,8},{10,11... | collective-permute-start | bytes 442376 | tf_op jit(solution)/shard_map/ppermute | solution.py:524
  39.4 5.2 %collective-permute-start.17 = (bf16[1,9,32,128]{3,2,1,0:T(8,128)(2,1)S(1)}, bf16[1,9,32,128]{3,2,1,0:T(8,128)(2,1)S(1)}, u32[]{:S(2)}, u32[]{:S(2)}) collective-permute-start(bf16[1,9,32,128]{3,2,1,0:T(8,128)(2,1)S(1)} %get-tuple-element.62), channel_id=1, source_target_pairs={{0,2},{1,3},{2,0},{3,1},{4,6},{5,7},{6,4},{7,5},{8,10},{9,11},{10,... | collective-permute-start | bytes 221192 | tf_op jit(solution)/shard_map/ppermute | solution.py:524
  40.7 5.0 %collective-permute-start.15 = (bf16[1,9,32,128]{3,2,1,0:T(8,128)(2,1)S(1)}, bf16[1,9,32,128]{3,2,1,0:T(8,128)(2,1)S(1)}, u32[]{:S(2)}, u32[]{:S(2)}) collective-permute-start(bf16[1,9,32,128]{3,2,1,0:T(8,128)(2,1)S(1)} %get-tuple-element.57), channel_id=1, source_target_pairs={{0,2},{1,3},{2,0},{3,1},{4,6},{5,7},{6,4},{7,5},{8,10},{9,11},{10,... | collective-permute-start | bytes 221192 | tf_op jit(solution)/shard_map/ppermute | solution.py:524

commit v4 on v1

--- a/solution.py
+++ b/solution.py
@@ -351,11 +351,17 @@
     ref[k, :, 2 * chans :] = shift_rows(x, step, zero).astype(BF16)
 
 
+def join_kernel(a_ref, b_ref, out_ref):
+    rows = a_ref.shape[0]
+    out_ref[0:rows] = a_ref[...]
+    out_ref[rows:] = b_ref[...]
+
+
 def sample_prep(
     lon, lat, chans, tiles,
     f_hbm, t_hbm, land_hbm, win_hbm, wout_hbm, gain_hbm, offset_hbm,
-    ss_ref, tt_ref, mask_ref, target_ref, win_ref, wout_ref, wt_ref, bn_ref,
-    f_ref, t_ref, land_ref, wraw_ref, sems,
+    ss_ref, tt_ref, mask_ref, target_ref, land_ref, win_ref, wout_ref, wt_ref, bn_ref,
+    f_ref, t_ref, wraw_ref, sems,
 ):
     pairs = [
         (land_hbm, land_ref), (f_hbm, f_ref), (t_hbm, t_ref), (wout_hbm, wout_ref), (win_hbm, wraw_ref),
@@ -395,11 +401,11 @@
     return jnp.concatenate(columns, axis=1)
 
 
-def sample_build(lon, lat, chans, f1_ref, f2_ref, l1_ref, l2_ref, l3_ref, ss_in, mask_in, ss_ref, mask_ref):
+def sample_build(lon, lat, chans, f1_ref, f2_ref, l2_ref, l13_ref, ss_in, mask_in, ss_ref, mask_ref):
     me = lax.axis_index("space")
-    for k, f_ref, land_ref in ((1, f1_ref, l1_ref), (2, f2_ref, l2_ref), (3, None, l3_ref)):
+    for k, f_ref, land_ref in ((1, f1_ref, l13_ref), (2, f2_ref, l2_ref), (3, None, l13_ref)):
         first = jnp.bitwise_xor(me, k) * lon
-        lines = land_ref[...].astype(F32)
+        lines = land_ref[lon if k == 3 else 0 : 2 * lon if k == 3 else lon].astype(F32)
         for i in range(lon):
             mask = spread(lines[i : i + 1], lat, chans)
             mask_ref[first + i] = mask.astype(BF16)
@@ -436,10 +442,18 @@
     stat_ref[...] = jnp.concatenate(rows + [jnp.zeros((5, chans), F32)], axis=0)
 
 
-def sample_adjoint(lon, lat, chans, t1_ref, t2_ref, t3_ref, wt_ref, tt_in, tt_ref, dact_ref):
+def sample_place(lon, t1_ref, t2_ref, tt_in, tt_ref):
+    me = lax.axis_index("space")
+    for k, t_ref in ((1, t1_ref), (2, t2_ref)):
+        start = jnp.bitwise_xor(me, k) * lon
+        for i in range(lon):
+            put_shifted(tt_ref, start + i + 1, t_ref[0, i].astype(F32), -1)
+
+
+def sample_adjoint(lon, lat, chans, t3_ref, mask_ref, wt_ref, tt_in, tt_ref, dact_ref):
     nx = dact_ref.shape[0]
     me = lax.axis_index("space")
-    for k, t_ref in ((1, t1_ref), (2, t2_ref), (3, t3_ref)):
+    for k, t_ref in ((3, t3_ref),):
         start = jnp.bitwise_xor(me, k) * lon
         for i in range(lon):
             put_shifted(tt_ref, start + i + 1, t_ref[0, i].astype(F32), -1)
@@ -459,37 +473,36 @@
             for half in range(2):
                 k = c + 2 * m + half
                 own = total[m * lat : (m + 1) * lat, half * chans : (half + 1) * chans]
-                dact_ref[k] = own + jnp.where(last, extra[k : k + 1], 0.0)
+                dact_ref[k] = (own + jnp.where(last, extra[k : k + 1], 0.0)) * mask_ref[k].astype(F32)
 
 
 def sample_act(lat, chans, first_ref, mask_ref, stat_ref, bn_ref, dact_ref, gsum_ref, dpre_ref, aa_ref):
     nx = mask_ref.shape[0]
     count, mean, rstd = moments(stat_ref)
-    gain, offset = bn_ref[0:1, :], bn_ref[1:2, :]
+    gain, offset = bn_ref[0:1, :] * rstd, bn_ref[1:2, :]
     scale = lax.rsqrt(count)
     fold = lambda v: jnp.sum(v.reshape(-1, 8, chans), axis=0)
     goff, ggain = [jnp.zeros((8, chans), F32)] * 2
     for i in range(nx // 2):
         acts = []
         for k in (i, nx - 1 - i):
-            xhat = (first_ref[k].astype(F32) - mean) * rstd
-            u = gain * xhat + offset
+            centred = first_ref[k].astype(F32) - mean
+            u = centred * gain + offset
             square = u * u
-            hyper = jnp.tanh(0.7978845608 * (u + 0.044715 * square * u))
-            m = mask_ref[k].astype(F32)
-            half = 0.5 * (1.0 + hyper)
-            acts.append(u * half * m)
-            slope = half + 0.5 * u * (1.0 - hyper * hyper) * 0.7978845608 * (1.0 + 3.0 * 0.044715 * square)
-            dpre = dact_ref[k] * scale * m * slope
+            half = 0.5 * jnp.tanh(u * (square * (0.7978845608 * 0.044715) + 0.7978845608)) + 0.5
+            acts.append(u * half * mask_ref[k].astype(F32))
+            bend = square * (6.0 * 0.7978845608 * 0.044715) + 2.0 * 0.7978845608
+            slope = half + (half - half * half) * u * bend
+            dpre = dact_ref[k] * scale * slope
             dpre_ref[k] = dpre
-            goff, ggain = goff + fold(dpre), ggain + fold(dpre * xhat)
+            goff, ggain = goff + fold(dpre), ggain + fold(dpre * centred)
         for k, x, other in ((i, acts[0], acts[1]), (nx - 1 - i, acts[1], acts[0])):
             aa_ref[k + 1, :, 0:chans] = shift_rows(x, -1, jnp.zeros((1, chans), F32)).astype(BF16)
             aa_ref[k + 1, :, chans : 2 * chans] = x.astype(BF16)
             aa_ref[k + 1, :, 2 * chans :] = shift_rows(x, 1, other[lat - 1 : lat]).astype(BF16)
     aa_ref[0] = aa_ref[nx]
     aa_ref[nx + 1] = aa_ref[1]
-    rows = [jnp.sum(v, axis=0, keepdims=True) for v in (goff, ggain)]
+    rows = [jnp.sum(v, axis=0, keepdims=True) for v in (goff, ggain * rstd)]
     gsum_ref[...] = jnp.concatenate(rows + [jnp.zeros((6, chans), F32)], axis=0)
 
 
@@ -658,8 +671,6 @@
     f2 = move(fields, across)
     l2 = move(land, across)
     f1 = move(fields, near)
-    l1 = move(land, near)
-    l3 = move(land, xor_pairs(tiles, 3))
     f3 = move(f2, near)
     gain, offset = batchnorm_gain[None, :], batchnorm_offset[None, :]
     params = [
@@ -675,18 +686,19 @@
     sums = sds((8, chans), F32)
     work = 2 * nx * lat * 9 * chans * chans
     double = sds((12 * chans, 2 * chans), BF16)
-    ss, tt, mask, target, win, wout, wt, bn = run(
+    ss, tt, mask, target, land_own, win, wout, wt, bn = run(
         functools.partial(sample_prep, *sizes, tiles),
-        [shifted, shifted, cells, sds(target_grad.shape, BF16), double, sds(conv_out.shape, BF16), double, sums],
+        [shifted, shifted, cells, sds(target_grad.shape, BF16), sds(land.shape, jnp.int32), double, sds(conv_out.shape, BF16), double, sums],
         params,
         scratch=[
-            pltpu.VMEM(fields.shape, BF16), pltpu.VMEM(fields.shape, BF16), pltpu.VMEM(land.shape, jnp.int32),
-            pltpu.VMEM(conv_in.shape, BF16), pltpu.SemaphoreType.DMA((7,)),
+            pltpu.VMEM(fields.shape, BF16), pltpu.VMEM(fields.shape, BF16), pltpu.VMEM(conv_in.shape, BF16), pltpu.SemaphoreType.DMA((7,)),
         ],
         space=pl.BlockSpec(memory_space=pltpu.HBM),
     )
+    (both,) = run(join_kernel, [sds((2 * lon, lat), jnp.int32)], [land_own, l2])
+    l13 = move(both, near)
     ss, mask = run(
-        functools.partial(sample_build, *sizes), [shifted, cells], [f1, f2, l1, l2, l3, ss, mask], alias={5: 0, 6: 1}
+        functools.partial(sample_build, *sizes), [shifted, cells], [f1, f2, l2, l13, ss, mask], alias={4: 0, 5: 1}
     )
     t2 = move(target, across)
     t1 = move(target, near)
@@ -695,8 +707,9 @@
         functools.partial(sample_conv, *sizes), [shifted, cells, sums], [f3, ss, mask, win], flops=work, alias={1: 0}
     )
     stat = all_sum(stat, "batch")
+    (tt,) = run(functools.partial(sample_place, lon), [shifted], [t1, t2, tt], alias={2: 0})
     tt, dact = run(
-        functools.partial(sample_adjoint, *sizes), [shifted, cells_f], [t1, t2, t3, wt, tt], flops=work, alias={4: 0}
+        functools.partial(sample_adjoint, *sizes), [shifted, cells_f], [t3, mask, wt, tt], flops=work, alias={3: 0}
     )
     gsum, dpre, aa = run(
         functools.partial(sample_act, lat, chans), [sums, cells_f, shifted], [first, mask, stat, bn, dact]

time: 54.4 us -> 46.6 us (0.86)
  starting transfers between devices: 24.7 us -> 19.9 us
  waiting for transfers between devices: 18.4 us -> 15.5 us
    ppermute x9 -> x8, starting transfers between devices: 17.2 us -> 12.7 us  [sample_body(): move = lambda x, pairs: lax.ppermute(x, 'space', pairs)]
    ppermute x9 -> x8, waiting for transfers between devices: 15.5 us -> 11.8 us  [sample_body(): move = lambda x, pairs: lax.ppermute(x, 'space', pairs)]
    ppermute x2, waiting for transfers between devices: 0.01 us -> 0.92 us  [all_sum(): both = lax.ppermute(x, axis, xor_pairs(size, 3 * bit))]
    ppermute x2, starting transfers between devices: 3.01 us -> 2.1 us  [all_sum(): far = lax.ppermute(x, axis, xor_pairs(size, 2 * bit))]
    ppermute x2, starting transfers between devices: 0.69 us -> 1.46 us  [all_sum(): both = lax.ppermute(x, axis, xor_pairs(size, 3 * bit))]
    pallas_call x10 -> x12, Pallas kernels: 9.05 us -> 8.9 us  [run(): pl.pallas_call(body, out_shape=list(outs), in_specs=[space] * len(args),...]
  transfers between devices with their start and end apart: 19 -> 18, of which waited for: 8 -> 9; matrix products, arithmetic and copies ran while one was open for 1% -> 1% of each run, Pallas kernels for 14% -> 17%
where the time goes in v4:
time: 46.6 us; the launch traced here: 46.4 us
  starting transfers between devices  19.9 us (43%)
  waiting for transfers between devices  15.5 us (33%)
  Pallas kernels  8.9 us (19%)
  other arithmetic  1.37 us (3%)
  between operations  0.71 us (2%)
    ppermute x8, starting transfers between devices, sample_body(): move = lambda x, pairs: lax.ppermute(x, 'space', pairs)  12.7 us
    ppermute x8, waiting for transfers between devices, sample_body(): move = lambda x, pairs: lax.ppermute(x, 'space', pairs)  11.8 us
    pallas_call x12, Pallas kernels, run(): pl.pallas_call(body, out_shape=list(outs), in_specs=[space] * len(args),...  8.9 us
    ppermute x4, starting transfers between devices, exchange_sum(): got = lax.ppermute(send, 'batch', xor_pairs(size, bit))  3.38 us
    ppermute x2, starting transfers between devices, all_sum(): far = lax.ppermute(x, axis, xor_pairs(size, 2 * bit))  2.1 us
    ppermute x4, waiting for transfers between devices, exchange_sum(): got = lax.ppermute(send, 'batch', xor_pairs(size, bit))  1.66 us
    ppermute x2, starting transfers between devices, all_sum(): both = lax.ppermute(x, axis, xor_pairs(size, 3 * bit))  1.46 us
    transpose x2, other arithmetic, exchange_sum(): return (jnp.swapaxes(keep[0].astype(F32) + got[0].astype(F32), 1, 2), keep)  1.36 us
  transfers between devices with their start and end apart: 18, of which 9 were waited for; matrix products, arithmetic and copies ran while one was open for 1% of the time, Pallas kernels for 17%

profile of v4, /device:TPU:0, one launch (start us, length us, event | category | flops | bytes accessed | tf_op | source)
XLA Modules:
  0.0 46.4 jit_solution(16644888963066384943)
XLA Ops:
  0.6 4.1 %collective-permute-start = (bf16[1,8,64,128]{3,2,1,0:T(8,128)(2,1)}, bf16[1,8,64,128]{3,2,1,0:T(8,128)(2,1)S(1)}, u32[]{:S(2)}, u32[]{:S(2)}) collective-permute-start(bf16[1,8,64,128]{3,2,1,0:T(8,128)(2,1)} %f_hbm.1), channel_id=1, source_target_pairs={{0,8},{4,12},{8,0},{12,4},{1,9},{5,13},{9,1},{13,5},{2,10},{6,14},... | collective-permute-start | bytes 393224 | tf_op jit(solution)/shard_map/ppermute | solution.py:670
  4.8 1.6 %shard_map.110 = (bf16[34,64,384]{2,1,0:T(8,128)(2,1)S(1)}, bf16[34,64,384]{2,1,0:T(8,128)(2,1)S(1)}, bf16[32,64,128]{2,1,0:T(8,128)(2,1)S(1)}, bf16[1,8,64,128]...) custom-call(bf16[1,8,64,128]{3,2,1,0:T(8,128)(2,1)} %f_hbm.1, ...), custom_call_target="tpu_custom_call" | custom-call | bytes 6726656 | tf_op jit(solution)/shard_map/pallas_call | solution.py:19
  6.5 1.9 %collective-permute-start.10 = (bf16[1,8,64,128]{3,2,1,0:T(8,128)(2,1)S(1)}, bf16[1,8,64,128]{3,2,1,0:T(8,128)(2,1)S(1)}, u32[]{:S(2)}, u32[]{:S(2)}) collective-permute-start(bf16[1,8,64,128]{3,2,1,0:T(8,128)(2,1)S(1)} %get-tuple-element.44), channel_id=1, source_target_pairs={{0,4},{4,0},{8,12},{12,8},{1,5},{5,1},{9,13},{13,9},{2,6},{6,2},{1... | collective-permute-start | bytes 393224 | tf_op jit(solution)/shard_map/ppermute | solution.py:670
  8.5 6.5 %collective-permute-done.f2_ref = bf16[1,8,64,128]{3,2,1,0:T(8,128)(2,1)S(1)} collective-permute-done((bf16[1,8,64,128]{3,2,1,0:T(8,128)(2,1)}, bf16[1,8,64,128]{3,2,1,0:T(8,128)(2,1)S(1)}, u32[]{:S(2)}, u32[]{:S(2)}) %collective-permute-start) | collective-permute-done | bytes 131104 | tf_op jit(solution)/shard_map/ppermute | solution.py:670
  15.1 1.9 %collective-permute-done.8.t2_ref = bf16[1,8,64,128]{3,2,1,0:T(8,128)(2,1)S(1)} collective-permute-done((bf16[1,8,64,128]{3,2,1,0:T(8,128)(2,1)S(1)}, bf16[1,8,64,128]{3,2,1,0:T(8,128)(2,1)S(1)}, u32[]{:S(2)}, u32[]{:S(2)}) %collective-permute-start.8) | collective-permute-done | bytes 131104 | tf_op jit(solution)/shard_map/ppermute | solution.py:670
  17.0 0.7 %collective-permute-start.9 = (bf16[1,8,64,128]{3,2,1,0:T(8,128)(2,1)S(1)}, bf16[1,8,64,128]{3,2,1,0:T(8,128)(2,1)S(1)}, u32[]{:S(2)}, u32[]{:S(2)}) collective-permute-start(bf16[1,8,64,128]{3,2,1,0:T(8,128)(2,1)S(1)} %collective-permute-done.8.t2_ref), channel_id=1, source_target_pairs={{0,4},{4,0},{8,12},{12,8},{1,5},{5,1},{9,13},{13,9},{2,6},{6,2},{1... | collective-permute-start | bytes 393224 | tf_op jit(solution)/shard_map/ppermute | solution.py:670
  17.7 3.4 %collective-permute-start.3 = (s32[8,64]{1,0:T(8,128)}, s32[8,64]{1,0:T(8,128)S(1)}, u32[]{:S(2)}, u32[]{:S(2)}) collective-permute-start(s32[8,64]{1,0:T(8,128)} %land_hbm.1), channel_id=1, source_target_pairs={{0,8},{4,12},{8,0},{12,4},{1,9},{5,13},{9,1},{13,5},{2,10},{6,14},... | collective-permute-start | bytes 6152 | tf_op jit(solution)/shard_map/ppermute | solution.py:670
  21.1 1.9 %collective-permute-done.3.b_ref.l2_ref = s32[8,64]{1,0:T(8,128)S(1)} collective-permute-done((s32[8,64]{1,0:T(8,128)}, s32[8,64]{1,0:T(8,128)S(1)}, u32[]{:S(2)}, u32[]{:S(2)}) %collective-permute-start.3) | collective-permute-done | bytes 2080 | tf_op jit(solution)/shard_map/ppermute | solution.py:670
  23.0 2.2 %collective-permute-start.4 = (s32[16,64]{1,0:T(8,128)S(1)}, s32[16,64]{1,0:T(8,128)S(1)}, u32[]{:S(2)}, u32[]{:S(2)}) collective-permute-start(s32[16,64]{1,0:T(8,128)S(1)} %shard_map.111), channel_id=1, source_target_pairs={{0,4},{4,0},{8,12},{12,8},{1,5},{5,1},{9,13},{13,9},{2,6},{6,2},{1... | collective-permute-start | bytes 12296 | tf_op jit(solution)/shard_map/ppermute | solution.py:670
  25.4 1.4 %collective-permute-done.4.l13_ref = s32[16,64]{1,0:T(8,128)S(1)} collective-permute-done((s32[16,64]{1,0:T(8,128)S(1)}, s32[16,64]{1,0:T(8,128)S(1)}, u32[]{:S(2)}, u32[]{:S(2)}) %collective-permute-start.4) | collective-permute-done | bytes 4128 | tf_op jit(solution)/shard_map/ppermute | solution.py:670
  26.9 0.3 shard_map.112
  27.2 1.2 %shard_map.113 = (bf16[34,64,384]{2,1,0:T(8,128)(2,1)S(1)}, bf16[32,64,128]{2,1,0:T(8,128)(2,1)S(1)}, f32[8,128]{1,0:T(8,128)S(1)}) custom-call(bf16[1,8,64,128]{3,2,1,0:T(8,128)(2,1)S(1)} %collective-permute-done.1.f3_ref, bf16[34,64,384]{2,1,0:T(8,128)(2,1)S(1)} %get-tuple-element.38.ss_in, ...), custom_call_target="tpu_custom_call", output_to_operand_aliasing={{0}: (1, {})} | custom-call | flops 603979776 | bytes 5312512 | tf_op jit(solution)/shard_map/pallas_call | solution.py:19
  28.5 1.6 %collective-permute-start.6 = (f32[8,128]{1,0:T(8,128)S(1)}, f32[8,128]{1,0:T(8,128)S(1)}, u32[]{:S(2)}, u32[]{:S(2)}) collective-permute-start(f32[8,128]{1,0:T(8,128)S(1)} %get-tuple-element.42), channel_id=1, source_target_pairs={{0,2},{1,3},{2,0},{3,1},{4,6},{5,7},{6,4},{7,5},{8,10},{9,11},{10,... | collective-permute-start | bytes 12296 | tf_op jit(solution)/shard_map/ppermute | solution.py:310
  30.1 0.3 collective-permute-start.7
  30.4 1.1 %shard_map.115 = (bf16[34,64,384]{2,1,0:T(8,128)(2,1)S(1)}, f32[32,64,128]{2,1,0:T(8,128)S(1)}) custom-call(bf16[1,8,64,128]{3,2,1,0:T(8,128)(2,1)S(1)} %collective-permute-done.9.t3_ref, bf16[32,64,128]{2,1,0:T(8,128)(2,1)S(1)} %get-tuple-element.39.mask_ref, bf16[1536,256]{1,0:T(8,128)(2,1)S(1)} %get-tuple-element.45.wt_ref, ...), custom_call_target="tpu_custom_call", output_to_operand_aliasing={{0}: (3, {})} | custom-call | flops 603979776 | bytes 5832704 | tf_op jit(solution)/shard_map/pallas_call | solution.py:19
  31.5 0.7 %collective-permute-done.6 = f32[8,128]{1,0:T(8,128)S(1)} collective-permute-done((f32[8,128]{1,0:T(8,128)S(1)}, f32[8,128]{1,0:T(8,128)S(1)}, u32[]{:S(2)}, u32[]{:S(2)}) %collective-permute-start.6) | collective-permute-done | bytes 4128 | tf_op jit(solution)/shard_map/ppermute | solution.py:310
  32.2 0.9 %collective-permute-done.7 = f32[8,128]{1,0:T(8,128)S(1)} collective-permute-done((f32[8,128]{1,0:T(8,128)S(1)}, f32[8,128]{1,0:T(8,128)S(1)}, u32[]{:S(2)}, u32[]{:S(2)}) %collective-permute-start.7) | collective-permute-done | bytes 4128 | tf_op jit(solution)/shard_map/ppermute | solution.py:311
  33.1 1.2 %shard_map.116 = (f32[8,128]{1,0:T(8,128)S(1)}, f32[32,64,128]{2,1,0:T(8,128)S(1)}, bf16[34,64,384]{2,1,0:T(8,128)(2,1)S(1)}) custom-call(bf16[32,64,128]{2,1,0:T(8,128)(2,1)S(1)} %get-tuple-element.41.first_ref, bf16[32,64,128]{2,1,0:T(8,128)(2,1)S(1)} %get-tuple-element.39.mask_ref, f32[8,128]{1,0:T(8,128)S(1)} %add_add_fusion.1.stat_ref, ...), custom_call_target="tpu_custom_call" | custom-call | bytes 4829184 | tf_op jit(solution)/shard_map/pallas_call | solution.py:19
  34.4 0.2 collective-permute-start.11
  34.6 0.5 %collective-permute-start.12 = (f32[8,128]{1,0:T(8,128)S(1)}, f32[8,128]{1,0:T(8,128)S(1)}, u32[]{:S(2)}, u32[]{:S(2)}) collective-permute-start(f32[8,128]{1,0:T(8,128)S(1)} %get-tuple-element.50), channel_id=1, source_target_pairs={{0,2},{1,3},{2,0},{3,1},{4,6},{5,7},{6,4},{7,5},{8,10},{9,11},{10,... | collective-permute-start | bytes 12296 | tf_op jit(solution)/shard_map/ppermute | solution.py:310
  35.1 1.2 %collective-permute-start.13 = (f32[8,128]{1,0:T(8,128)S(1)}, f32[8,128]{1,0:T(8,128)S(1)}, u32[]{:S(2)}, u32[]{:S(2)}) collective-permute-start(f32[8,128]{1,0:T(8,128)S(1)} %get-tuple-element.50), channel_id=1, source_target_pairs={{0,3},{1,2},{2,1},{3,0},{4,7},{5,6},{6,5},{7,4},{8,11},{9,10},{10,... | collective-permute-start | bytes 12296 | tf_op jit(solution)/shard_map/ppermute | solution.py:311
  36.3 1.0 %shard_map.120 = (bf16[2,9,32,128]{3,2,1,0:T(8,128)(2,1)S(1)}, bf16[2,9,32,128]{3,2,1,0:T(8,128)(2,1)S(1)}) custom-call(bf16[34,64,384]{2,1,0:T(8,128)(2,1)S(1)} %get-tuple-element.48.aa_ref, bf16[34,64,384]{2,1,0:T(8,128)(2,1)S(1)} %get-tuple-element.58.tt_ref, f32[8,128]{1,0:T(8,128)S(1)} %add_add_fusion.1.stat_ref), custom_call_target="tpu_custom_call" | custom-call | flops 603979776 | bytes 3641344 | tf_op jit(solution)/shard_map/pallas_call | solution.py:19
  37.3 0.5 %collective-permute-start.16 = (bf16[2,9,32,128]{3,2,1,0:T(8,128)(2,1)S(1)}, bf16[2,9,32,128]{3,2,1,0:T(8,128)(2,1)S(1)}, u32[]{:S(2)}, u32[]{:S(2)}) collective-permute-start(bf16[2,9,32,128]{3,2,1,0:T(8,128)(2,1)S(1)} %get-tuple-element.60), channel_id=1, source_target_pairs={{0,1},{1,0},{2,3},{3,2},{4,5},{5,4},{6,7},{7,6},{8,9},{9,8},{10,11... | collective-permute-start | bytes 442376 | tf_op jit(solution)/shard_map/ppermute | solution.py:523
  37.8 0.4 collective-permute-done.12
  38.2 1.1 %shard_map.117 = (bf16[2,9,32,128]{3,2,1,0:T(8,128)(2,1)S(1)}, bf16[2,9,32,128]{3,2,1,0:T(8,128)(2,1)S(1)}) custom-call(bf16[32,64,128]{2,1,0:T(8,128)(2,1)S(1)} %get-tuple-element.41.first_ref, bf16[32,64,128]{2,1,0:T(8,128)(2,1)S(1)} %get-tuple-element.39.mask_ref, f32[8,128]{1,0:T(8,128)S(1)} %add_add_fusion.1.stat_ref, ...), custom_call_target="tpu_custom_call" | custom-call | flops 603979776 | bytes 4075520 | tf_op jit(solution)/shard_map/pallas_call | solution.py:19
  39.5 1.5 %collective-permute-start.17 = (bf16[1,9,32,128]{3,2,1,0:T(8,128)(2,1)S(1)}, bf16[1,9,32,128]{3,2,1,0:T(8,128)(2,1)S(1)}, u32[]{:S(2)}, u32[]{:S(2)}) collective-permute-start(bf16[1,9,32,128]{3,2,1,0:T(8,128)(2,1)S(1)} %get-tuple-element.62), channel_id=1, source_target_pairs={{0,2},{1,3},{2,0},{3,1},{4,6},{5,7},{6,4},{7,5},{8,10},{9,11},{10,... | collective-permute-start | bytes 221192 | tf_op jit(solution)/shard_map/ppermute | solution.py:523
  41.1 1.2 %collective-permute-start.15 = (bf16[1,9,32,128]{3,2,1,0:T(8,128)(2,1)S(1)}, bf16[1,9,32,128]{3,2,1,0:T(8,128)(2,1)S(1)}, u32[]{:S(2)}, u32[]{:S(2)}) collective-permute-start(bf16[1,9,32,128]{3,2,1,0:T(8,128)(2,1)S(1)} %get-tuple-element.57), channel_id=1, source_target_pairs={{0,2},{1,3},{2,0},{3,1},{4,6},{5,7},{6,4},{7,5},{8,10},{9,11},{10,... | collective-permute-start | bytes 221192 | tf_op jit(solution)/shard_map/ppermute | solution.py:523
  42.3 1.1 %shard_map.119 = (bf16[1,8,64,128]{3,2,1,0:T(8,128)(2,1)}, f32[1,128]{1,0:T(1,128)}, f32[1,128]{1,0:T(1,128)}) custom-call(bf16[34,64,384]{2,1,0:T(8,128)(2,1)S(1)} %get-tuple-element.48.aa_ref, bf16[32,64,128]{2,1,0:T(8,128)(2,1)S(1)} %get-tuple-element.39.mask_ref, bf16[9,128,128]{2,1,0:T(8,128)(2,1)S(1)} %get-tuple-element.49.w_ref, ...), custom_call_target="tpu_custom_call" | custom-call | flops 150994944 | bytes 2700288 | tf_op jit(solution)/shard_map/pallas_call | solution.py:19
  43.4 1.1 %collective-permute-done.17 = bf16[1,9,32,128]{3,2,1,0:T(8,128)(2,1)S(1)} collective-permute-done((bf16[1,9,32,128]{3,2,1,0:T(8,128)(2,1)S(1)}, bf16[1,9,32,128]{3,2,1,0:T(8,128)(2,1)S(1)}, u32[]{:S(2)}, u32[]{:S(2)}) %collective-permute-start.17) | collective-permute-done | bytes 73760 | tf_op jit(solution)/shard_map/ppermute | solution.py:523
  44.4 0.7 %add_bitcast_fusion = f32[9,128,32]{1,2,0:T(8,128)} fusion(bf16[1,9,32,128]{3,2,1,0:T(8,128)(2,1)S(1)} %collective-permute-done.17, bf16[1,9,32,128]{3,2,1,0:T(8,128)(2,1)S(1)} %get-tuple-element.61), kind=kLoop, calls=%fused_computation | loop fusion | flops 110592 | bytes 294912 | tf_op jit(solution)/shard_map/transpose | solution.py:526
  45.1 0.6 %collective-permute-done.15 = bf16[1,9,32,128]{3,2,1,0:T(8,128)(2,1)S(1)} collective-permute-done((bf16[1,9,32,128]{3,2,1,0:T(8,128)(2,1)S(1)}, bf16[1,9,32,128]{3,2,1,0:T(8,128)(2,1)S(1)}, u32[]{:S(2)}, u32[]{:S(2)}) %collective-permute-start.15) | collective-permute-done | bytes 73760 | tf_op jit(solution)/shard_map/ppermute | solution.py:523
  45.7 0.7 %add_bitcast_fusion.1 = f32[9,128,32]{1,2,0:T(8,128)} fusion(bf16[1,9,32,128]{3,2,1,0:T(8,128)(2,1)S(1)} %collective-permute-done.15, bf16[1,9,32,128]{3,2,1,0:T(8,128)(2,1)S(1)} %get-tuple-element.55.after_ref), kind=kLoop, calls=%fused_computation.1 | loop fusion | flops 110592 | bytes 294912 | tf_op jit(solution)/shard_map/transpose | solution.py:526
  (20 shorter events, 0.8 us)
Async XLA Ops:
  0.6 14.4 %collective-permute-start = (bf16[1,8,64,128]{3,2,1,0:T(8,128)(2,1)}, bf16[1,8,64,128]{3,2,1,0:T(8,128)(2,1)S(1)}, u32[]{:S(2)}, u32[]{:S(2)}) collective-permute-start(bf16[1,8,64,128]{3,2,1,0:T(8,128)(2,1)} %f_hbm.1), channel_id=1, source_target_pairs={{0,8},{4,12},{8,0},{12,4},{1,9},{5,13},{9,1},{13,5},{2,10},{6,14},... | collective-permute-start | bytes 393224 | tf_op jit(solution)/shard_map/ppermute | solution.py:670
  6.4 10.6 %collective-permute-start.8 = (bf16[1,8,64,128]{3,2,1,0:T(8,128)(2,1)S(1)}, bf16[1,8,64,128]{3,2,1,0:T(8,128)(2,1)S(1)}, u32[]{:S(2)}, u32[]{:S(2)}) collective-permute-start(bf16[1,8,64,128]{3,2,1,0:T(8,128)(2,1)S(1)} %get-tuple-element.44), channel_id=1, source_target_pairs={{0,8},{4,12},{8,0},{12,4},{1,9},{5,13},{9,1},{13,5},{2,10},{6,14},... | collective-permute-start | bytes 393224 | tf_op jit(solution)/shard_map/ppermute | solution.py:670
  6.5 18.8 %collective-permute-start.10 = (bf16[1,8,64,128]{3,2,1,0:T(8,128)(2,1)S(1)}, bf16[1,8,64,128]{3,2,1,0:T(8,128)(2,1)S(1)}, u32[]{:S(2)}, u32[]{:S(2)}) collective-permute-start(bf16[1,8,64,128]{3,2,1,0:T(8,128)(2,1)S(1)} %get-tuple-element.44), channel_id=1, source_target_pairs={{0,4},{4,0},{8,12},{12,8},{1,5},{5,1},{9,13},{13,9},{2,6},{6,2},{1... | collective-permute-start | bytes 393224 | tf_op jit(solution)/shard_map/ppermute | solution.py:670
  8.4 18.5 %collective-permute-start.2 = (bf16[1,8,64,128]{3,2,1,0:T(8,128)(2,1)}, bf16[1,8,64,128]{3,2,1,0:T(8,128)(2,1)S(1)}, u32[]{:S(2)}, u32[]{:S(2)}) collective-permute-start(bf16[1,8,64,128]{3,2,1,0:T(8,128)(2,1)} %f_hbm.1), channel_id=1, source_target_pairs={{0,4},{4,0},{8,12},{12,8},{1,5},{5,1},{9,13},{13,9},{2,6},{6,2},{1... | collective-permute-start | bytes 393224 | tf_op jit(solution)/shard_map/ppermute | solution.py:670
  15.0 12.2 %collective-permute-start.1 = (bf16[1,8,64,128]{3,2,1,0:T(8,128)(2,1)S(1)}, bf16[1,8,64,128]{3,2,1,0:T(8,128)(2,1)S(1)}, u32[]{:S(2)}, u32[]{:S(2)}) collective-permute-start(bf16[1,8,64,128]{3,2,1,0:T(8,128)(2,1)S(1)} %collective-permute-done.f2_ref), channel_id=1, source_target_pairs={{0,4},{4,0},{8,12},{12,8},{1,5},{5,1},{9,13},{13,9},{2,6},{6,2},{1... | collective-permute-start | bytes 393224 | tf_op jit(solution)/shard_map/ppermute | solution.py:670
  17.0 13.4 %collective-permute-start.9 = (bf16[1,8,64,128]{3,2,1,0:T(8,128)(2,1)S(1)}, bf16[1,8,64,128]{3,2,1,0:T(8,128)(2,1)S(1)}, u32[]{:S(2)}, u32[]{:S(2)}) collective-permute-start(bf16[1,8,64,128]{3,2,1,0:T(8,128)(2,1)S(1)} %collective-permute-done.8.t2_ref), channel_id=1, source_target_pairs={{0,4},{4,0},{8,12},{12,8},{1,5},{5,1},{9,13},{13,9},{2,6},{6,2},{1... | collective-permute-start | bytes 393224 | tf_op jit(solution)/shard_map/ppermute | solution.py:670
  17.7 5.3 %collective-permute-start.3 = (s32[8,64]{1,0:T(8,128)}, s32[8,64]{1,0:T(8,128)S(1)}, u32[]{:S(2)}, u32[]{:S(2)}) collective-permute-start(s32[8,64]{1,0:T(8,128)} %land_hbm.1), channel_id=1, source_target_pairs={{0,8},{4,12},{8,0},{12,4},{1,9},{5,13},{9,1},{13,5},{2,10},{6,14},... | collective-permute-start | bytes 6152 | tf_op jit(solution)/shard_map/ppermute | solution.py:670
  23.0 3.9 %collective-permute-start.4 = (s32[16,64]{1,0:T(8,128)S(1)}, s32[16,64]{1,0:T(8,128)S(1)}, u32[]{:S(2)}, u32[]{:S(2)}) collective-permute-start(s32[16,64]{1,0:T(8,128)S(1)} %shard_map.111), channel_id=1, source_target_pairs={{0,4},{4,0},{8,12},{12,8},{1,5},{5,1},{9,13},{13,9},{2,6},{6,2},{1... | collective-permute-start | bytes 12296 | tf_op jit(solution)/shard_map/ppermute | solution.py:670
  28.5 3.0 %collective-permute-start.5 = (f32[8,128]{1,0:T(8,128)S(1)}, f32[8,128]{1,0:T(8,128)S(1)}, u32[]{:S(2)}, u32[]{:S(2)}) collective-permute-start(f32[8,128]{1,0:T(8,128)S(1)} %get-tuple-element.42), channel_id=1, source_target_pairs={{0,1},{1,0},{2,3},{3,2},{4,5},{5,4},{6,7},{7,6},{8,9},{9,8},{10,11... | collective-permute-start | bytes 12296 | tf_op jit(solution)/shard_map/ppermute | solution.py:308
  28.5 3.7 %collective-permute-start.6 = (f32[8,128]{1,0:T(8,128)S(1)}, f32[8,128]{1,0:T(8,128)S(1)}, u32[]{:S(2)}, u32[]{:S(2)}) collective-permute-start(f32[8,128]{1,0:T(8,128)S(1)} %get-tuple-element.42), channel_id=1, source_target_pairs={{0,2},{1,3},{2,0},{3,1},{4,6},{5,7},{6,4},{7,5},{8,10},{9,11},{10,... | collective-permute-start | bytes 12296 | tf_op jit(solution)/shard_map/ppermute | solution.py:310
  30.1 3.0 %collective-permute-start.7 = (f32[8,128]{1,0:T(8,128)S(1)}, f32[8,128]{1,0:T(8,128)S(1)}, u32[]{:S(2)}, u32[]{:S(2)}) collective-permute-start(f32[8,128]{1,0:T(8,128)S(1)} %get-tuple-element.42), channel_id=1, source_target_pairs={{0,3},{1,2},{2,1},{3,0},{4,7},{5,6},{6,5},{7,4},{8,11},{9,10},{10,... | collective-permute-start | bytes 12296 | tf_op jit(solution)/shard_map/ppermute | solution.py:311
  34.4 3.4 %collective-permute-start.11 = (f32[8,128]{1,0:T(8,128)S(1)}, f32[8,128]{1,0:T(8,128)S(1)}, u32[]{:S(2)}, u32[]{:S(2)}) collective-permute-start(f32[8,128]{1,0:T(8,128)S(1)} %get-tuple-element.50), channel_id=1, source_target_pairs={{0,1},{1,0},{2,3},{3,2},{4,5},{5,4},{6,7},{7,6},{8,9},{9,8},{10,11... | collective-permute-start | bytes 12296 | tf_op jit(solution)/shard_map/ppermute | solution.py:308
  34.6 3.6 %collective-permute-start.12 = (f32[8,128]{1,0:T(8,128)S(1)}, f32[8,128]{1,0:T(8,128)S(1)}, u32[]{:S(2)}, u32[]{:S(2)}) collective-permute-start(f32[8,128]{1,0:T(8,128)S(1)} %get-tuple-element.50), channel_id=1, source_target_pairs={{0,2},{1,3},{2,0},{3,1},{4,6},{5,7},{6,4},{7,5},{8,10},{9,11},{10,... | collective-permute-start | bytes 12296 | tf_op jit(solution)/shard_map/ppermute | solution.py:310
  35.1 3.1 %collective-permute-start.13 = (f32[8,128]{1,0:T(8,128)S(1)}, f32[8,128]{1,0:T(8,128)S(1)}, u32[]{:S(2)}, u32[]{:S(2)}) collective-permute-start(f32[8,128]{1,0:T(8,128)S(1)} %get-tuple-element.50), channel_id=1, source_target_pairs={{0,3},{1,2},{2,1},{3,0},{4,7},{5,6},{6,5},{7,4},{8,11},{9,10},{10,... | collective-permute-start | bytes 12296 | tf_op jit(solution)/shard_map/ppermute | solution.py:311
  37.3 2.2 %collective-permute-start.16 = (bf16[2,9,32,128]{3,2,1,0:T(8,128)(2,1)S(1)}, bf16[2,9,32,128]{3,2,1,0:T(8,128)(2,1)S(1)}, u32[]{:S(2)}, u32[]{:S(2)}) collective-permute-start(bf16[2,9,32,128]{3,2,1,0:T(8,128)(2,1)S(1)} %get-tuple-element.60), channel_id=1, source_target_pairs={{0,1},{1,0},{2,3},{3,2},{4,5},{5,4},{6,7},{7,6},{8,9},{9,8},{10,11... | collective-permute-start | bytes 442376 | tf_op jit(solution)/shard_map/ppermute | solution.py:523
  39.3 1.7 %collective-permute-start.14 = (bf16[2,9,32,128]{3,2,1,0:T(8,128)(2,1)S(1)}, bf16[2,9,32,128]{3,2,1,0:T(8,128)(2,1)S(1)}, u32[]{:S(2)}, u32[]{:S(2)}) collective-permute-start(bf16[2,9,32,128]{3,2,1,0:T(8,128)(2,1)S(1)} %get-tuple-element.54), channel_id=1, source_target_pairs={{0,1},{1,0},{2,3},{3,2},{4,5},{5,4},{6,7},{7,6},{8,9},{9,8},{10,11... | collective-permute-start | bytes 442376 | tf_op jit(solution)/shard_map/ppermute | solution.py:523
  39.5 5.0 %collective-permute-start.17 = (bf16[1,9,32,128]{3,2,1,0:T(8,128)(2,1)S(1)}, bf16[1,9,32,128]{3,2,1,0:T(8,128)(2,1)S(1)}, u32[]{:S(2)}, u32[]{:S(2)}) collective-permute-start(bf16[1,9,32,128]{3,2,1,0:T(8,128)(2,1)S(1)} %get-tuple-element.62), channel_id=1, source_target_pairs={{0,2},{1,3},{2,0},{3,1},{4,6},{5,7},{6,4},{7,5},{8,10},{9,11},{10,... | collective-permute-start | bytes 221192 | tf_op jit(solution)/shard_map/ppermute | solution.py:523
  41.1 4.7 %collective-permute-start.15 = (bf16[1,9,32,128]{3,2,1,0:T(8,128)(2,1)S(1)}, bf16[1,9,32,128]{3,2,1,0:T(8,128)(2,1)S(1)}, u32[]{:S(2)}, u32[]{:S(2)}) collective-permute-start(bf16[1,9,32,128]{3,2,1,0:T(8,128)(2,1)S(1)} %get-tuple-element.57), channel_id=1, source_target_pairs={{0,2},{1,3},{2,0},{3,1},{4,6},{5,7},{6,4},{7,5},{8,10},{9,11},{10,... | collective-permute-start | bytes 221192 | tf_op jit(solution)/shard_map/ppermute | solution.py:523

commit v5 on v4

--- a/solution.py
+++ b/solution.py
@@ -360,7 +360,7 @@
 def sample_prep(
     lon, lat, chans, tiles,
     f_hbm, t_hbm, land_hbm, win_hbm, wout_hbm, gain_hbm, offset_hbm,
-    ss_ref, tt_ref, mask_ref, target_ref, land_ref, win_ref, wout_ref, wt_ref, bn_ref,
+    ss_ref, tt_ref, mask_ref, land_ref, win_ref, wout_ref, wt_ref, bn_ref,
     f_ref, t_ref, wraw_ref, sems,
 ):
     pairs = [
@@ -379,7 +379,6 @@
         mask_ref[first + i] = mask.astype(BF16)
         put_shifted(ss_ref, first + i + 1, f_ref[0, i].astype(F32) * mask, 1)
         target = t_ref[0, i].astype(F32) * mask
-        target_ref[0, i] = target.astype(BF16)
         put_shifted(tt_ref, first + i + 1, target, -1)
     for c in copies[3:]:
         c.wait()
@@ -442,12 +441,12 @@
     stat_ref[...] = jnp.concatenate(rows + [jnp.zeros((5, chans), F32)], axis=0)
 
 
-def sample_place(lon, t1_ref, t2_ref, tt_in, tt_ref):
+def sample_place(lon, t1_ref, t2_ref, mask_ref, tt_in, tt_ref):
     me = lax.axis_index("space")
     for k, t_ref in ((1, t1_ref), (2, t2_ref)):
         start = jnp.bitwise_xor(me, k) * lon
         for i in range(lon):
-            put_shifted(tt_ref, start + i + 1, t_ref[0, i].astype(F32), -1)
+            put_shifted(tt_ref, start + i + 1, t_ref[0, i].astype(F32) * mask_ref[start + i].astype(F32), -1)
 
 
 def sample_adjoint(lon, lat, chans, t3_ref, mask_ref, wt_ref, tt_in, tt_ref, dact_ref):
@@ -456,7 +455,7 @@
     for k, t_ref in ((3, t3_ref),):
         start = jnp.bitwise_xor(me, k) * lon
         for i in range(lon):
-            put_shifted(tt_ref, start + i + 1, t_ref[0, i].astype(F32), -1)
+            put_shifted(tt_ref, start + i + 1, t_ref[0, i].astype(F32) * mask_ref[start + i].astype(F32), -1)
     tt_ref[0] = tt_ref[nx]
     tt_ref[nx + 1] = tt_ref[1]
     top = [tt_ref[i + 1, lat - 8 :, chans : 2 * chans].astype(F32)[7:8] for i in range(nx)]
@@ -686,9 +685,9 @@
     sums = sds((8, chans), F32)
     work = 2 * nx * lat * 9 * chans * chans
     double = sds((12 * chans, 2 * chans), BF16)
-    ss, tt, mask, target, land_own, win, wout, wt, bn = run(
+    ss, tt, mask, land_own, win, wout, wt, bn = run(
         functools.partial(sample_prep, *sizes, tiles),
-        [shifted, shifted, cells, sds(target_grad.shape, BF16), sds(land.shape, jnp.int32), double, sds(conv_out.shape, BF16), double, sums],
+        [shifted, shifted, cells, sds(land.shape, jnp.int32), double, sds(conv_out.shape, BF16), double, sums],
         params,
         scratch=[
             pltpu.VMEM(fields.shape, BF16), pltpu.VMEM(fields.shape, BF16), pltpu.VMEM(conv_in.shape, BF16), pltpu.SemaphoreType.DMA((7,)),
@@ -700,14 +699,14 @@
     ss, mask = run(
         functools.partial(sample_build, *sizes), [shifted, cells], [f1, f2, l2, l13, ss, mask], alias={4: 0, 5: 1}
     )
-    t2 = move(target, across)
-    t1 = move(target, near)
+    t2 = move(target_grad, across)
+    t1 = move(target_grad, near)
     t3 = move(t2, near)
     ss, first, stat = run(
         functools.partial(sample_conv, *sizes), [shifted, cells, sums], [f3, ss, mask, win], flops=work, alias={1: 0}
     )
     stat = all_sum(stat, "batch")
-    (tt,) = run(functools.partial(sample_place, lon), [shifted], [t1, t2, tt], alias={2: 0})
+    (tt,) = run(functools.partial(sample_place, lon), [shifted], [t1, t2, mask, tt], alias={3: 0})
     tt, dact = run(
         functools.partial(sample_adjoint, *sizes), [shifted, cells_f], [t3, mask, wt, tt], flops=work, alias={3: 0}
     )

time: 46.6 us -> 46.6 us (level)
    ppermute x8, starting transfers between devices: 12.7 us -> 12.2 us  [sample_body(): move = lambda x, pairs: lax.ppermute(x, 'space', pairs)]
where the time goes in v5:
time: 46.6 us; the launch traced here: 46.4 us
  starting transfers between devices  19.5 us (42%)
  waiting for transfers between devices  15.9 us (34%)
  Pallas kernels  8.94 us (19%)
  other arithmetic  1.37 us (3%)
  between operations  0.73 us (2%)
    ppermute x8, waiting for transfers between devices, sample_body(): move = lambda x, pairs: lax.ppermute(x, 'space', pairs)  12.2 us
    ppermute x8, starting transfers between devices, sample_body(): move = lambda x, pairs: lax.ppermute(x, 'space', pairs)  12.2 us
    pallas_call x12, Pallas kernels, run(): pl.pallas_call(body, out_shape=list(outs), in_specs=[space] * len(args),...  8.94 us
    ppermute x4, starting transfers between devices, exchange_sum(): got = lax.ppermute(send, 'batch', xor_pairs(size, bit))  3.5 us
    ppermute x2, starting transfers between devices, all_sum(): far = lax.ppermute(x, axis, xor_pairs(size, 2 * bit))  2.12 us
    ppermute x4, waiting for transfers between devices, exchange_sum(): got = lax.ppermute(send, 'batch', xor_pairs(size, bit))  1.56 us
    ppermute x2, starting transfers between devices, all_sum(): both = lax.ppermute(x, axis, xor_pairs(size, 3 * bit))  1.44 us
    transpose x2, other arithmetic, exchange_sum(): return (jnp.swapaxes(keep[0].astype(F32) + got[0].astype(F32), 1, 2), keep)  1.36 us
  transfers between devices with their start and end apart: 18, of which 9 were waited for; matrix products, arithmetic and copies ran while one was open for 1% of the time, Pallas kernels for 17%

profile of v5, /device:TPU:0, one launch (start us, length us, event | category | flops | bytes accessed | tf_op | source)
XLA Modules:
  0.0 46.4 jit_solution(4378646297316958721)
XLA Ops:
  0.6 4.1 %collective-permute-start = (bf16[1,8,64,128]{3,2,1,0:T(8,128)(2,1)}, bf16[1,8,64,128]{3,2,1,0:T(8,128)(2,1)S(1)}, u32[]{:S(2)}, u32[]{:S(2)}) collective-permute-start(bf16[1,8,64,128]{3,2,1,0:T(8,128)(2,1)} %f_hbm.1), channel_id=1, source_target_pairs={{0,8},{4,12},{8,0},{12,4},{1,9},{5,13},{9,1},{13,5},{2,10},{6,14},... | collective-permute-start | bytes 393224 | tf_op jit(solution)/shard_map/ppermute | solution.py:669
  4.8 1.8 %collective-permute-start.2 = (bf16[1,8,64,128]{3,2,1,0:T(8,128)(2,1)}, bf16[1,8,64,128]{3,2,1,0:T(8,128)(2,1)S(1)}, u32[]{:S(2)}, u32[]{:S(2)}) collective-permute-start(bf16[1,8,64,128]{3,2,1,0:T(8,128)(2,1)} %f_hbm.1), channel_id=1, source_target_pairs={{0,4},{4,0},{8,12},{12,8},{1,5},{5,1},{9,13},{13,9},{2,6},{6,2},{1... | collective-permute-start | bytes 393224 | tf_op jit(solution)/shard_map/ppermute | solution.py:669
  6.9 8.2 %collective-permute-done.f2_ref = bf16[1,8,64,128]{3,2,1,0:T(8,128)(2,1)S(1)} collective-permute-done((bf16[1,8,64,128]{3,2,1,0:T(8,128)(2,1)}, bf16[1,8,64,128]{3,2,1,0:T(8,128)(2,1)S(1)}, u32[]{:S(2)}, u32[]{:S(2)}) %collective-permute-start) | collective-permute-done | bytes 131104 | tf_op jit(solution)/shard_map/ppermute | solution.py:669
  15.1 1.9 %collective-permute-done.8.t2_ref = bf16[1,8,64,128]{3,2,1,0:T(8,128)(2,1)S(1)} collective-permute-done((bf16[1,8,64,128]{3,2,1,0:T(8,128)(2,1)}, bf16[1,8,64,128]{3,2,1,0:T(8,128)(2,1)S(1)}, u32[]{:S(2)}, u32[]{:S(2)}) %collective-permute-start.8) | collective-permute-done | bytes 131104 | tf_op jit(solution)/shard_map/ppermute | solution.py:669
  17.0 0.8 %collective-permute-start.9 = (bf16[1,8,64,128]{3,2,1,0:T(8,128)(2,1)S(1)}, bf16[1,8,64,128]{3,2,1,0:T(8,128)(2,1)S(1)}, u32[]{:S(2)}, u32[]{:S(2)}) collective-permute-start(bf16[1,8,64,128]{3,2,1,0:T(8,128)(2,1)S(1)} %collective-permute-done.8.t2_ref), channel_id=1, source_target_pairs={{0,4},{4,0},{8,12},{12,8},{1,5},{5,1},{9,13},{13,9},{2,6},{6,2},{1... | collective-permute-start | bytes 393224 | tf_op jit(solution)/shard_map/ppermute | solution.py:669
  17.8 3.3 %collective-permute-start.3 = (s32[8,64]{1,0:T(8,128)}, s32[8,64]{1,0:T(8,128)S(1)}, u32[]{:S(2)}, u32[]{:S(2)}) collective-permute-start(s32[8,64]{1,0:T(8,128)} %land_hbm.1), channel_id=1, source_target_pairs={{0,8},{4,12},{8,0},{12,4},{1,9},{5,13},{9,1},{13,5},{2,10},{6,14},... | collective-permute-start | bytes 6152 | tf_op jit(solution)/shard_map/ppermute | solution.py:669
  21.1 1.6 %shard_map.110 = (bf16[34,64,384]{2,1,0:T(8,128)(2,1)S(1)}, bf16[34,64,384]{2,1,0:T(8,128)(2,1)S(1)}, bf16[32,64,128]{2,1,0:T(8,128)(2,1)S(1)}, s32[8,64]{1,0:T(...) custom-call(bf16[1,8,64,128]{3,2,1,0:T(8,128)(2,1)} %f_hbm.1, ...), custom_call_target="tpu_custom_call" | custom-call | bytes 6595584 | tf_op jit(solution)/shard_map/pallas_call | solution.py:19
  22.7 0.3 collective-permute-done.3.b_ref.l2_ref
  23.0 1.8 %collective-permute-start.4 = (s32[16,64]{1,0:T(8,128)S(1)}, s32[16,64]{1,0:T(8,128)S(1)}, u32[]{:S(2)}, u32[]{:S(2)}) collective-permute-start(s32[16,64]{1,0:T(8,128)S(1)} %shard_map.111), channel_id=1, source_target_pairs={{0,4},{4,0},{8,12},{12,8},{1,5},{5,1},{9,13},{13,9},{2,6},{6,2},{1... | collective-permute-start | bytes 12296 | tf_op jit(solution)/shard_map/ppermute | solution.py:669
  24.8 1.8 %collective-permute-done.4.l13_ref = s32[16,64]{1,0:T(8,128)S(1)} collective-permute-done((s32[16,64]{1,0:T(8,128)S(1)}, s32[16,64]{1,0:T(8,128)S(1)}, u32[]{:S(2)}, u32[]{:S(2)}) %collective-permute-start.4) | collective-permute-done | bytes 4128 | tf_op jit(solution)/shard_map/ppermute | solution.py:669
  26.6 0.3 shard_map.112
  27.2 1.2 %shard_map.113 = (bf16[34,64,384]{2,1,0:T(8,128)(2,1)S(1)}, bf16[32,64,128]{2,1,0:T(8,128)(2,1)S(1)}, f32[8,128]{1,0:T(8,128)S(1)}) custom-call(bf16[1,8,64,128]{3,2,1,0:T(8,128)(2,1)S(1)} %collective-permute-done.1.f3_ref, bf16[34,64,384]{2,1,0:T(8,128)(2,1)S(1)} %get-tuple-element.37.ss_in, ...), custom_call_target="tpu_custom_call", output_to_operand_aliasing={{0}: (1, {})} | custom-call | flops 603979776 | bytes 5312512 | tf_op jit(solution)/shard_map/pallas_call | solution.py:19
  28.5 1.6 %collective-permute-start.6 = (f32[8,128]{1,0:T(8,128)S(1)}, f32[8,128]{1,0:T(8,128)S(1)}, u32[]{:S(2)}, u32[]{:S(2)}) collective-permute-start(f32[8,128]{1,0:T(8,128)S(1)} %get-tuple-element.41), channel_id=1, source_target_pairs={{0,2},{1,3},{2,0},{3,1},{4,6},{5,7},{6,4},{7,5},{8,10},{9,11},{10,... | collective-permute-start | bytes 12296 | tf_op jit(solution)/shard_map/ppermute | solution.py:310
  30.1 0.3 collective-permute-start.7
  30.4 1.1 %shard_map.115 = (bf16[34,64,384]{2,1,0:T(8,128)(2,1)S(1)}, f32[32,64,128]{2,1,0:T(8,128)S(1)}) custom-call(bf16[1,8,64,128]{3,2,1,0:T(8,128)(2,1)S(1)} %collective-permute-done.9.t3_ref, bf16[32,64,128]{2,1,0:T(8,128)(2,1)S(1)} %get-tuple-element.38.mask_ref, bf16[1536,256]{1,0:T(8,128)(2,1)S(1)} %get-tuple-element.43.wt_ref, ...), custom_call_target="tpu_custom_call", output_to_operand_aliasing={{0}: (3, {})} | custom-call | flops 603979776 | bytes 5832704 | tf_op jit(solution)/shard_map/pallas_call | solution.py:19
  31.5 0.7 %collective-permute-done.6 = f32[8,128]{1,0:T(8,128)S(1)} collective-permute-done((f32[8,128]{1,0:T(8,128)S(1)}, f32[8,128]{1,0:T(8,128)S(1)}, u32[]{:S(2)}, u32[]{:S(2)}) %collective-permute-start.6) | collective-permute-done | bytes 4128 | tf_op jit(solution)/shard_map/ppermute | solution.py:310
  32.2 0.9 %collective-permute-done.7 = f32[8,128]{1,0:T(8,128)S(1)} collective-permute-done((f32[8,128]{1,0:T(8,128)S(1)}, f32[8,128]{1,0:T(8,128)S(1)}, u32[]{:S(2)}, u32[]{:S(2)}) %collective-permute-start.7) | collective-permute-done | bytes 4128 | tf_op jit(solution)/shard_map/ppermute | solution.py:311
  33.1 1.2 %shard_map.116 = (f32[8,128]{1,0:T(8,128)S(1)}, f32[32,64,128]{2,1,0:T(8,128)S(1)}, bf16[34,64,384]{2,1,0:T(8,128)(2,1)S(1)}) custom-call(bf16[32,64,128]{2,1,0:T(8,128)(2,1)S(1)} %get-tuple-element.40.first_ref, bf16[32,64,128]{2,1,0:T(8,128)(2,1)S(1)} %get-tuple-element.38.mask_ref, f32[8,128]{1,0:T(8,128)S(1)} %add_add_fusion.1.stat_ref, ...), custom_call_target="tpu_custom_call" | custom-call | bytes 4829184 | tf_op jit(solution)/shard_map/pallas_call | solution.py:19
  34.4 0.2 collective-permute-start.11
  34.6 0.5 %collective-permute-start.12 = (f32[8,128]{1,0:T(8,128)S(1)}, f32[8,128]{1,0:T(8,128)S(1)}, u32[]{:S(2)}, u32[]{:S(2)}) collective-permute-start(f32[8,128]{1,0:T(8,128)S(1)} %get-tuple-element.48), channel_id=1, source_target_pairs={{0,2},{1,3},{2,0},{3,1},{4,6},{5,7},{6,4},{7,5},{8,10},{9,11},{10,... | collective-permute-start | bytes 12296 | tf_op jit(solution)/shard_map/ppermute | solution.py:310
  35.1 1.2 %collective-permute-start.13 = (f32[8,128]{1,0:T(8,128)S(1)}, f32[8,128]{1,0:T(8,128)S(1)}, u32[]{:S(2)}, u32[]{:S(2)}) collective-permute-start(f32[8,128]{1,0:T(8,128)S(1)} %get-tuple-element.48), channel_id=1, source_target_pairs={{0,3},{1,2},{2,1},{3,0},{4,7},{5,6},{6,5},{7,4},{8,11},{9,10},{10,... | collective-permute-start | bytes 12296 | tf_op jit(solution)/shard_map/ppermute | solution.py:311
  36.3 0.9 %shard_map.120 = (bf16[2,9,32,128]{3,2,1,0:T(8,128)(2,1)S(1)}, bf16[2,9,32,128]{3,2,1,0:T(8,128)(2,1)S(1)}) custom-call(bf16[34,64,384]{2,1,0:T(8,128)(2,1)S(1)} %get-tuple-element.46.aa_ref, bf16[34,64,384]{2,1,0:T(8,128)(2,1)S(1)} %get-tuple-element.56.tt_ref, f32[8,128]{1,0:T(8,128)S(1)} %add_add_fusion.1.stat_ref), custom_call_target="tpu_custom_call" | custom-call | flops 603979776 | bytes 3641344 | tf_op jit(solution)/shard_map/pallas_call | solution.py:19
  37.2 0.5 %collective-permute-start.16 = (bf16[2,9,32,128]{3,2,1,0:T(8,128)(2,1)S(1)}, bf16[2,9,32,128]{3,2,1,0:T(8,128)(2,1)S(1)}, u32[]{:S(2)}, u32[]{:S(2)}) collective-permute-start(bf16[2,9,32,128]{3,2,1,0:T(8,128)(2,1)S(1)} %get-tuple-element.58), channel_id=1, source_target_pairs={{0,1},{1,0},{2,3},{3,2},{4,5},{5,4},{6,7},{7,6},{8,9},{9,8},{10,11... | collective-permute-start | bytes 442376 | tf_op jit(solution)/shard_map/ppermute | solution.py:522
  37.8 0.4 collective-permute-done.12
  38.2 1.1 %shard_map.117 = (bf16[2,9,32,128]{3,2,1,0:T(8,128)(2,1)S(1)}, bf16[2,9,32,128]{3,2,1,0:T(8,128)(2,1)S(1)}) custom-call(bf16[32,64,128]{2,1,0:T(8,128)(2,1)S(1)} %get-tuple-element.40.first_ref, bf16[32,64,128]{2,1,0:T(8,128)(2,1)S(1)} %get-tuple-element.38.mask_ref, f32[8,128]{1,0:T(8,128)S(1)} %add_add_fusion.1.stat_ref, ...), custom_call_target="tpu_custom_call" | custom-call | flops 603979776 | bytes 4075520 | tf_op jit(solution)/shard_map/pallas_call | solution.py:19
  39.5 1.5 %collective-permute-start.17 = (bf16[1,9,32,128]{3,2,1,0:T(8,128)(2,1)S(1)}, bf16[1,9,32,128]{3,2,1,0:T(8,128)(2,1)S(1)}, u32[]{:S(2)}, u32[]{:S(2)}) collective-permute-start(bf16[1,9,32,128]{3,2,1,0:T(8,128)(2,1)S(1)} %get-tuple-element.60), channel_id=1, source_target_pairs={{0,2},{1,3},{2,0},{3,1},{4,6},{5,7},{6,4},{7,5},{8,10},{9,11},{10,... | collective-permute-start | bytes 221192 | tf_op jit(solution)/shard_map/ppermute | solution.py:522
  41.1 1.3 %collective-permute-start.15 = (bf16[1,9,32,128]{3,2,1,0:T(8,128)(2,1)S(1)}, bf16[1,9,32,128]{3,2,1,0:T(8,128)(2,1)S(1)}, u32[]{:S(2)}, u32[]{:S(2)}) collective-permute-start(bf16[1,9,32,128]{3,2,1,0:T(8,128)(2,1)S(1)} %get-tuple-element.55), channel_id=1, source_target_pairs={{0,2},{1,3},{2,0},{3,1},{4,6},{5,7},{6,4},{7,5},{8,10},{9,11},{10,... | collective-permute-start | bytes 221192 | tf_op jit(solution)/shard_map/ppermute | solution.py:522
  42.4 1.1 %shard_map.119 = (bf16[1,8,64,128]{3,2,1,0:T(8,128)(2,1)}, f32[1,128]{1,0:T(1,128)}, f32[1,128]{1,0:T(1,128)}) custom-call(bf16[34,64,384]{2,1,0:T(8,128)(2,1)S(1)} %get-tuple-element.46.aa_ref, bf16[32,64,128]{2,1,0:T(8,128)(2,1)S(1)} %get-tuple-element.38.mask_ref, bf16[9,128,128]{2,1,0:T(8,128)(2,1)S(1)} %get-tuple-element.47.w_ref, ...), custom_call_target="tpu_custom_call" | custom-call | flops 150994944 | bytes 2700288 | tf_op jit(solution)/shard_map/pallas_call | solution.py:19
  43.5 0.9 %collective-permute-done.17 = bf16[1,9,32,128]{3,2,1,0:T(8,128)(2,1)S(1)} collective-permute-done((bf16[1,9,32,128]{3,2,1,0:T(8,128)(2,1)S(1)}, bf16[1,9,32,128]{3,2,1,0:T(8,128)(2,1)S(1)}, u32[]{:S(2)}, u32[]{:S(2)}) %collective-permute-start.17) | collective-permute-done | bytes 73760 | tf_op jit(solution)/shard_map/ppermute | solution.py:522
  44.4 0.7 %add_bitcast_fusion = f32[9,128,32]{1,2,0:T(8,128)} fusion(bf16[1,9,32,128]{3,2,1,0:T(8,128)(2,1)S(1)} %collective-permute-done.17, bf16[1,9,32,128]{3,2,1,0:T(8,128)(2,1)S(1)} %get-tuple-element.59), kind=kLoop, calls=%fused_computation | loop fusion | flops 110592 | bytes 294912 | tf_op jit(solution)/shard_map/transpose | solution.py:525
  45.0 0.7 %collective-permute-done.15 = bf16[1,9,32,128]{3,2,1,0:T(8,128)(2,1)S(1)} collective-permute-done((bf16[1,9,32,128]{3,2,1,0:T(8,128)(2,1)S(1)}, bf16[1,9,32,128]{3,2,1,0:T(8,128)(2,1)S(1)}, u32[]{:S(2)}, u32[]{:S(2)}) %collective-permute-start.15) | collective-permute-done | bytes 73760 | tf_op jit(solution)/shard_map/ppermute | solution.py:522
  45.7 0.7 %add_bitcast_fusion.1 = f32[9,128,32]{1,2,0:T(8,128)} fusion(bf16[1,9,32,128]{3,2,1,0:T(8,128)(2,1)S(1)} %collective-permute-done.15, bf16[1,9,32,128]{3,2,1,0:T(8,128)(2,1)S(1)} %get-tuple-element.53.after_ref), kind=kLoop, calls=%fused_computation.1 | loop fusion | flops 110592 | bytes 294912 | tf_op jit(solution)/shard_map/transpose | solution.py:525
  (20 shorter events, 0.9 us)
Async XLA Ops:
  0.6 14.4 %collective-permute-start = (bf16[1,8,64,128]{3,2,1,0:T(8,128)(2,1)}, bf16[1,8,64,128]{3,2,1,0:T(8,128)(2,1)S(1)}, u32[]{:S(2)}, u32[]{:S(2)}) collective-permute-start(bf16[1,8,64,128]{3,2,1,0:T(8,128)(2,1)} %f_hbm.1), channel_id=1, source_target_pairs={{0,8},{4,12},{8,0},{12,4},{1,9},{5,13},{9,1},{13,5},{2,10},{6,14},... | collective-permute-start | bytes 393224 | tf_op jit(solution)/shard_map/ppermute | solution.py:669
  4.8 12.2 %collective-permute-start.8 = (bf16[1,8,64,128]{3,2,1,0:T(8,128)(2,1)}, bf16[1,8,64,128]{3,2,1,0:T(8,128)(2,1)S(1)}, u32[]{:S(2)}, u32[]{:S(2)}) collective-permute-start(bf16[1,8,64,128]{3,2,1,0:T(8,128)(2,1)} %t_hbm.1), channel_id=1, source_target_pairs={{0,8},{4,12},{8,0},{12,4},{1,9},{5,13},{9,1},{13,5},{2,10},{6,14},... | collective-permute-start | bytes 393224 | tf_op jit(solution)/shard_map/ppermute | solution.py:669
  4.8 21.8 %collective-permute-start.2 = (bf16[1,8,64,128]{3,2,1,0:T(8,128)(2,1)}, bf16[1,8,64,128]{3,2,1,0:T(8,128)(2,1)S(1)}, u32[]{:S(2)}, u32[]{:S(2)}) collective-permute-start(bf16[1,8,64,128]{3,2,1,0:T(8,128)(2,1)} %f_hbm.1), channel_id=1, source_target_pairs={{0,4},{4,0},{8,12},{12,8},{1,5},{5,1},{9,13},{13,9},{2,6},{6,2},{1... | collective-permute-start | bytes 393224 | tf_op jit(solution)/shard_map/ppermute | solution.py:669
  6.7 20.3 %collective-permute-start.10 = (bf16[1,8,64,128]{3,2,1,0:T(8,128)(2,1)}, bf16[1,8,64,128]{3,2,1,0:T(8,128)(2,1)S(1)}, u32[]{:S(2)}, u32[]{:S(2)}) collective-permute-start(bf16[1,8,64,128]{3,2,1,0:T(8,128)(2,1)} %t_hbm.1), channel_id=1, source_target_pairs={{0,4},{4,0},{8,12},{12,8},{1,5},{5,1},{9,13},{13,9},{2,6},{6,2},{1... | collective-permute-start | bytes 393224 | tf_op jit(solution)/shard_map/ppermute | solution.py:669
  15.0 12.2 %collective-permute-start.1 = (bf16[1,8,64,128]{3,2,1,0:T(8,128)(2,1)S(1)}, bf16[1,8,64,128]{3,2,1,0:T(8,128)(2,1)S(1)}, u32[]{:S(2)}, u32[]{:S(2)}) collective-permute-start(bf16[1,8,64,128]{3,2,1,0:T(8,128)(2,1)S(1)} %collective-permute-done.f2_ref), channel_id=1, source_target_pairs={{0,4},{4,0},{8,12},{12,8},{1,5},{5,1},{9,13},{13,9},{2,6},{6,2},{1... | collective-permute-start | bytes 393224 | tf_op jit(solution)/shard_map/ppermute | solution.py:669
  17.0 13.4 %collective-permute-start.9 = (bf16[1,8,64,128]{3,2,1,0:T(8,128)(2,1)S(1)}, bf16[1,8,64,128]{3,2,1,0:T(8,128)(2,1)S(1)}, u32[]{:S(2)}, u32[]{:S(2)}) collective-permute-start(bf16[1,8,64,128]{3,2,1,0:T(8,128)(2,1)S(1)} %collective-permute-done.8.t2_ref), channel_id=1, source_target_pairs={{0,4},{4,0},{8,12},{12,8},{1,5},{5,1},{9,13},{13,9},{2,6},{6,2},{1... | collective-permute-start | bytes 393224 | tf_op jit(solution)/shard_map/ppermute | solution.py:669
  17.8 5.2 %collective-permute-start.3 = (s32[8,64]{1,0:T(8,128)}, s32[8,64]{1,0:T(8,128)S(1)}, u32[]{:S(2)}, u32[]{:S(2)}) collective-permute-start(s32[8,64]{1,0:T(8,128)} %land_hbm.1), channel_id=1, source_target_pairs={{0,8},{4,12},{8,0},{12,4},{1,9},{5,13},{9,1},{13,5},{2,10},{6,14},... | collective-permute-start | bytes 6152 | tf_op jit(solution)/shard_map/ppermute | solution.py:669
  23.0 3.7 %collective-permute-start.4 = (s32[16,64]{1,0:T(8,128)S(1)}, s32[16,64]{1,0:T(8,128)S(1)}, u32[]{:S(2)}, u32[]{:S(2)}) collective-permute-start(s32[16,64]{1,0:T(8,128)S(1)} %shard_map.111), channel_id=1, source_target_pairs={{0,4},{4,0},{8,12},{12,8},{1,5},{5,1},{9,13},{13,9},{2,6},{6,2},{1... | collective-permute-start | bytes 12296 | tf_op jit(solution)/shard_map/ppermute | solution.py:669
  28.4 3.0 %collective-permute-start.5 = (f32[8,128]{1,0:T(8,128)S(1)}, f32[8,128]{1,0:T(8,128)S(1)}, u32[]{:S(2)}, u32[]{:S(2)}) collective-permute-start(f32[8,128]{1,0:T(8,128)S(1)} %get-tuple-element.41), channel_id=1, source_target_pairs={{0,1},{1,0},{2,3},{3,2},{4,5},{5,4},{6,7},{7,6},{8,9},{9,8},{10,11... | collective-permute-start | bytes 12296 | tf_op jit(solution)/shard_map/ppermute | solution.py:308
  28.5 3.7 %collective-permute-start.6 = (f32[8,128]{1,0:T(8,128)S(1)}, f32[8,128]{1,0:T(8,128)S(1)}, u32[]{:S(2)}, u32[]{:S(2)}) collective-permute-start(f32[8,128]{1,0:T(8,128)S(1)} %get-tuple-element.41), channel_id=1, source_target_pairs={{0,2},{1,3},{2,0},{3,1},{4,6},{5,7},{6,4},{7,5},{8,10},{9,11},{10,... | collective-permute-start | bytes 12296 | tf_op jit(solution)/shard_map/ppermute | solution.py:310
  30.1 3.0 %collective-permute-start.7 = (f32[8,128]{1,0:T(8,128)S(1)}, f32[8,128]{1,0:T(8,128)S(1)}, u32[]{:S(2)}, u32[]{:S(2)}) collective-permute-start(f32[8,128]{1,0:T(8,128)S(1)} %get-tuple-element.41), channel_id=1, source_target_pairs={{0,3},{1,2},{2,1},{3,0},{4,7},{5,6},{6,5},{7,4},{8,11},{9,10},{10,... | collective-permute-start | bytes 12296 | tf_op jit(solution)/shard_map/ppermute | solution.py:311
  34.4 3.4 %collective-permute-start.11 = (f32[8,128]{1,0:T(8,128)S(1)}, f32[8,128]{1,0:T(8,128)S(1)}, u32[]{:S(2)}, u32[]{:S(2)}) collective-permute-start(f32[8,128]{1,0:T(8,128)S(1)} %get-tuple-element.48), channel_id=1, source_target_pairs={{0,1},{1,0},{2,3},{3,2},{4,5},{5,4},{6,7},{7,6},{8,9},{9,8},{10,11... | collective-permute-start | bytes 12296 | tf_op jit(solution)/shard_map/ppermute | solution.py:308
  34.6 3.6 %collective-permute-start.12 = (f32[8,128]{1,0:T(8,128)S(1)}, f32[8,128]{1,0:T(8,128)S(1)}, u32[]{:S(2)}, u32[]{:S(2)}) collective-permute-start(f32[8,128]{1,0:T(8,128)S(1)} %get-tuple-element.48), channel_id=1, source_target_pairs={{0,2},{1,3},{2,0},{3,1},{4,6},{5,7},{6,4},{7,5},{8,10},{9,11},{10,... | collective-permute-start | bytes 12296 | tf_op jit(solution)/shard_map/ppermute | solution.py:310
  35.1 3.1 %collective-permute-start.13 = (f32[8,128]{1,0:T(8,128)S(1)}, f32[8,128]{1,0:T(8,128)S(1)}, u32[]{:S(2)}, u32[]{:S(2)}) collective-permute-start(f32[8,128]{1,0:T(8,128)S(1)} %get-tuple-element.48), channel_id=1, source_target_pairs={{0,3},{1,2},{2,1},{3,0},{4,7},{5,6},{6,5},{7,4},{8,11},{9,10},{10,... | collective-permute-start | bytes 12296 | tf_op jit(solution)/shard_map/ppermute | solution.py:311
  37.2 2.2 %collective-permute-start.16 = (bf16[2,9,32,128]{3,2,1,0:T(8,128)(2,1)S(1)}, bf16[2,9,32,128]{3,2,1,0:T(8,128)(2,1)S(1)}, u32[]{:S(2)}, u32[]{:S(2)}) collective-permute-start(bf16[2,9,32,128]{3,2,1,0:T(8,128)(2,1)S(1)} %get-tuple-element.58), channel_id=1, source_target_pairs={{0,1},{1,0},{2,3},{3,2},{4,5},{5,4},{6,7},{7,6},{8,9},{9,8},{10,11... | collective-permute-start | bytes 442376 | tf_op jit(solution)/shard_map/ppermute | solution.py:522
  39.3 1.8 %collective-permute-start.14 = (bf16[2,9,32,128]{3,2,1,0:T(8,128)(2,1)S(1)}, bf16[2,9,32,128]{3,2,1,0:T(8,128)(2,1)S(1)}, u32[]{:S(2)}, u32[]{:S(2)}) collective-permute-start(bf16[2,9,32,128]{3,2,1,0:T(8,128)(2,1)S(1)} %get-tuple-element.52), channel_id=1, source_target_pairs={{0,1},{1,0},{2,3},{3,2},{4,5},{5,4},{6,7},{7,6},{8,9},{9,8},{10,11... | collective-permute-start | bytes 442376 | tf_op jit(solution)/shard_map/ppermute | solution.py:522
  39.5 4.8 %collective-permute-start.17 = (bf16[1,9,32,128]{3,2,1,0:T(8,128)(2,1)S(1)}, bf16[1,9,32,128]{3,2,1,0:T(8,128)(2,1)S(1)}, u32[]{:S(2)}, u32[]{:S(2)}) collective-permute-start(bf16[1,9,32,128]{3,2,1,0:T(8,128)(2,1)S(1)} %get-tuple-element.60), channel_id=1, source_target_pairs={{0,2},{1,3},{2,0},{3,1},{4,6},{5,7},{6,4},{7,5},{8,10},{9,11},{10,... | collective-permute-start | bytes 221192 | tf_op jit(solution)/shard_map/ppermute | solution.py:522
  41.1 4.6 %collective-permute-start.15 = (bf16[1,9,32,128]{3,2,1,0:T(8,128)(2,1)S(1)}, bf16[1,9,32,128]{3,2,1,0:T(8,128)(2,1)S(1)}, u32[]{:S(2)}, u32[]{:S(2)}) collective-permute-start(bf16[1,9,32,128]{3,2,1,0:T(8,128)(2,1)S(1)} %get-tuple-element.55), channel_id=1, source_target_pairs={{0,2},{1,3},{2,0},{3,1},{4,6},{5,7},{6,4},{7,5},{8,10},{9,11},{10,... | collective-permute-start | bytes 221192 | tf_op jit(solution)/shard_map/ppermute | solution.py:522

commit v6 on v4

--- a/solution.py
+++ b/solution.py
@@ -351,17 +351,11 @@
     ref[k, :, 2 * chans :] = shift_rows(x, step, zero).astype(BF16)
 
 
-def join_kernel(a_ref, b_ref, out_ref):
-    rows = a_ref.shape[0]
-    out_ref[0:rows] = a_ref[...]
-    out_ref[rows:] = b_ref[...]
-
-
 def sample_prep(
     lon, lat, chans, tiles,
     f_hbm, t_hbm, land_hbm, win_hbm, wout_hbm, gain_hbm, offset_hbm,
-    ss_ref, tt_ref, mask_ref, target_ref, land_ref, win_ref, wout_ref, wt_ref, bn_ref,
-    f_ref, t_ref, wraw_ref, sems,
+    ss_ref, tt_ref, mask_ref, target_ref, win_ref, wout_ref, wt_ref, bn_ref,
+    f_ref, t_ref, land_ref, wraw_ref, sems,
 ):
     pairs = [
         (land_hbm, land_ref), (f_hbm, f_ref), (t_hbm, t_ref), (wout_hbm, wout_ref), (win_hbm, wraw_ref),
@@ -401,11 +395,11 @@
     return jnp.concatenate(columns, axis=1)
 
 
-def sample_build(lon, lat, chans, f1_ref, f2_ref, l2_ref, l13_ref, ss_in, mask_in, ss_ref, mask_ref):
+def sample_build(lon, lat, chans, f1_ref, f2_ref, l1_ref, l2_ref, l3_ref, ss_in, mask_in, ss_ref, mask_ref):
     me = lax.axis_index("space")
-    for k, f_ref, land_ref in ((1, f1_ref, l13_ref), (2, f2_ref, l2_ref), (3, None, l13_ref)):
+    for k, f_ref, land_ref in ((1, f1_ref, l1_ref), (2, f2_ref, l2_ref), (3, None, l3_ref)):
         first = jnp.bitwise_xor(me, k) * lon
-        lines = land_ref[lon if k == 3 else 0 : 2 * lon if k == 3 else lon].astype(F32)
+        lines = land_ref[...].astype(F32)
         for i in range(lon):
             mask = spread(lines[i : i + 1], lat, chans)
             mask_ref[first + i] = mask.astype(BF16)
@@ -671,6 +665,8 @@
     f2 = move(fields, across)
     l2 = move(land, across)
     f1 = move(fields, near)
+    l1 = move(land, near)
+    l3 = move(land, xor_pairs(tiles, 3))
     f3 = move(f2, near)
     gain, offset = batchnorm_gain[None, :], batchnorm_offset[None, :]
     params = [
@@ -686,19 +682,18 @@
     sums = sds((8, chans), F32)
     work = 2 * nx * lat * 9 * chans * chans
     double = sds((12 * chans, 2 * chans), BF16)
-    ss, tt, mask, target, land_own, win, wout, wt, bn = run(
+    ss, tt, mask, target, win, wout, wt, bn = run(
         functools.partial(sample_prep, *sizes, tiles),
-        [shifted, shifted, cells, sds(target_grad.shape, BF16), sds(land.shape, jnp.int32), double, sds(conv_out.shape, BF16), double, sums],
+        [shifted, shifted, cells, sds(target_grad.shape, BF16), double, sds(conv_out.shape, BF16), double, sums],
         params,
         scratch=[
-            pltpu.VMEM(fields.shape, BF16), pltpu.VMEM(fields.shape, BF16), pltpu.VMEM(conv_in.shape, BF16), pltpu.SemaphoreType.DMA((7,)),
+            pltpu.VMEM(fields.shape, BF16), pltpu.VMEM(fields.shape, BF16), pltpu.VMEM(land.shape, jnp.int32),
+            pltpu.VMEM(conv_in.shape, BF16), pltpu.SemaphoreType.DMA((7,)),
         ],
         space=pl.BlockSpec(memory_space=pltpu.HBM),
     )
-    (both,) = run(join_kernel, [sds((2 * lon, lat), jnp.int32)], [land_own, l2])
-    l13 = move(both, near)
     ss, mask = run(
-        functools.partial(sample_build, *sizes), [shifted, cells], [f1, f2, l2, l13, ss, mask], alias={4: 0, 5: 1}
+        functools.partial(sample_build, *sizes), [shifted, cells], [f1, f2, l1, l2, l3, ss, mask], alias={5: 0, 6: 1}
     )
     t2 = move(target, across)
     t1 = move(target, near)

time: 46.6 us -> 52.5 us (1.13)
  waiting for transfers between devices: 15.5 us -> 21.1 us
    ppermute x8 -> x9, waiting for transfers between devices: 11.8 us -> 17.4 us  [sample_body(): move = lambda x, pairs: lax.ppermute(x, 'space', pairs)]
    ppermute x8 -> x9, starting transfers between devices: 12.7 us -> 13 us  [sample_body(): move = lambda x, pairs: lax.ppermute(x, 'space', pairs)]
    pallas_call x12 -> x11, Pallas kernels: 8.9 us -> 8.9 us  [run(): pl.pallas_call(body, out_shape=list(outs), in_specs=[space] * len(args),...]
  transfers between devices with their start and end apart: 18 -> 19, of which waited for: 9 -> 9; matrix products, arithmetic and copies ran while one was open for 1% -> 1% of each run, Pallas kernels for 17% -> 15%
where the time goes in v6:
time: 52.5 us; the launch traced here: 52.3 us
  waiting for transfers between devices  21.1 us (40%)
  starting transfers between devices  20.2 us (38%)
  Pallas kernels  8.9 us (17%)
  other arithmetic  1.37 us (3%)
  between operations  0.72 us (1%)
    ppermute x9, waiting for transfers between devices, sample_body(): move = lambda x, pairs: lax.ppermute(x, 'space', pairs)  17.4 us
    ppermute x9, starting transfers between devices, sample_body(): move = lambda x, pairs: lax.ppermute(x, 'space', pairs)  13 us
    pallas_call x11, Pallas kernels, run(): pl.pallas_call(body, out_shape=list(outs), in_specs=[space] * len(args),...  8.9 us
    ppermute x4, starting transfers between devices, exchange_sum(): got = lax.ppermute(send, 'batch', xor_pairs(size, bit))  3.4 us
    ppermute x2, starting transfers between devices, all_sum(): far = lax.ppermute(x, axis, xor_pairs(size, 2 * bit))  2.1 us
    ppermute x4, waiting for transfers between devices, exchange_sum(): got = lax.ppermute(send, 'batch', xor_pairs(size, bit))  1.66 us
    ppermute x2, starting transfers between devices, all_sum(): both = lax.ppermute(x, axis, xor_pairs(size, 3 * bit))  1.46 us
    transpose x2, other arithmetic, exchange_sum(): return (jnp.swapaxes(keep[0].astype(F32) + got[0].astype(F32), 1, 2), keep)  1.36 us
  transfers between devices with their start and end apart: 19, of which 9 were waited for; matrix products, arithmetic and copies ran while one was open for 1% of the time, Pallas kernels for 15%

profile of v6, /device:TPU:0, one launch (start us, length us, event | category | flops | bytes accessed | tf_op | source)
XLA Modules:
  0.0 52.3 jit_solution(13760675011640508369)
XLA Ops:
  0.6 4.1 %collective-permute-start = (bf16[1,8,64,128]{3,2,1,0:T(8,128)(2,1)}, bf16[1,8,64,128]{3,2,1,0:T(8,128)(2,1)S(1)}, u32[]{:S(2)}, u32[]{:S(2)}) collective-permute-start(bf16[1,8,64,128]{3,2,1,0:T(8,128)(2,1)} %f_hbm.1), channel_id=1, source_target_pairs={{0,8},{4,12},{8,0},{12,4},{1,9},{5,13},{9,1},{13,5},{2,10},{6,14},... | collective-permute-start | bytes 393224 | tf_op jit(solution)/shard_map/ppermute | solution.py:664
  4.8 1.6 %shard_map.110 = (bf16[34,64,384]{2,1,0:T(8,128)(2,1)S(1)}, bf16[34,64,384]{2,1,0:T(8,128)(2,1)S(1)}, bf16[32,64,128]{2,1,0:T(8,128)(2,1)S(1)}, bf16[1,8,64,128]...) custom-call(bf16[1,8,64,128]{3,2,1,0:T(8,128)(2,1)} %f_hbm.1, ...), custom_call_target="tpu_custom_call" | custom-call | bytes 6724608 | tf_op jit(solution)/shard_map/pallas_call | solution.py:19
  6.5 1.9 %collective-permute-start.11 = (bf16[1,8,64,128]{3,2,1,0:T(8,128)(2,1)S(1)}, bf16[1,8,64,128]{3,2,1,0:T(8,128)(2,1)S(1)}, u32[]{:S(2)}, u32[]{:S(2)}) collective-permute-start(bf16[1,8,64,128]{3,2,1,0:T(8,128)(2,1)S(1)} %get-tuple-element.42), channel_id=1, source_target_pairs={{0,4},{4,0},{8,12},{12,8},{1,5},{5,1},{9,13},{13,9},{2,6},{6,2},{1... | collective-permute-start | bytes 393224 | tf_op jit(solution)/shard_map/ppermute | solution.py:664
  8.5 6.5 %collective-permute-done.f2_ref = bf16[1,8,64,128]{3,2,1,0:T(8,128)(2,1)S(1)} collective-permute-done((bf16[1,8,64,128]{3,2,1,0:T(8,128)(2,1)}, bf16[1,8,64,128]{3,2,1,0:T(8,128)(2,1)S(1)}, u32[]{:S(2)}, u32[]{:S(2)}) %collective-permute-start) | collective-permute-done | bytes 131104 | tf_op jit(solution)/shard_map/ppermute | solution.py:664
  15.1 1.9 %collective-permute-done.9.t2_ref = bf16[1,8,64,128]{3,2,1,0:T(8,128)(2,1)S(1)} collective-permute-done((bf16[1,8,64,128]{3,2,1,0:T(8,128)(2,1)S(1)}, bf16[1,8,64,128]{3,2,1,0:T(8,128)(2,1)S(1)}, u32[]{:S(2)}, u32[]{:S(2)}) %collective-permute-start.9) | collective-permute-done | bytes 131104 | tf_op jit(solution)/shard_map/ppermute | solution.py:664
  17.0 0.7 %collective-permute-start.10 = (bf16[1,8,64,128]{3,2,1,0:T(8,128)(2,1)S(1)}, bf16[1,8,64,128]{3,2,1,0:T(8,128)(2,1)S(1)}, u32[]{:S(2)}, u32[]{:S(2)}) collective-permute-start(bf16[1,8,64,128]{3,2,1,0:T(8,128)(2,1)S(1)} %collective-permute-done.9.t2_ref), channel_id=1, source_target_pairs={{0,4},{4,0},{8,12},{12,8},{1,5},{5,1},{9,13},{13,9},{2,6},{6,2},{1... | collective-permute-start | bytes 393224 | tf_op jit(solution)/shard_map/ppermute | solution.py:664
  17.7 1.4 %collective-permute-start.3 = (s32[8,64]{1,0:T(8,128)}, s32[8,64]{1,0:T(8,128)S(1)}, u32[]{:S(2)}, u32[]{:S(2)}) collective-permute-start(s32[8,64]{1,0:T(8,128)} %land_hbm.1), channel_id=1, source_target_pairs={{0,4},{4,0},{8,12},{12,8},{1,5},{5,1},{9,13},{13,9},{2,6},{6,2},{1... | collective-permute-start | bytes 6152 | tf_op jit(solution)/shard_map/ppermute | solution.py:664
  19.0 5.4 %collective-permute-done.3.l1_ref = s32[8,64]{1,0:T(8,128)S(1)} collective-permute-done((s32[8,64]{1,0:T(8,128)}, s32[8,64]{1,0:T(8,128)S(1)}, u32[]{:S(2)}, u32[]{:S(2)}) %collective-permute-start.3) | collective-permute-done | bytes 2080 | tf_op jit(solution)/shard_map/ppermute | solution.py:664
  24.4 2.7 %collective-permute-start.4 = (s32[8,64]{1,0:T(8,128)}, s32[8,64]{1,0:T(8,128)S(1)}, u32[]{:S(2)}, u32[]{:S(2)}) collective-permute-start(s32[8,64]{1,0:T(8,128)} %land_hbm.1), channel_id=1, source_target_pairs={{0,8},{4,12},{8,0},{12,4},{1,9},{5,13},{9,1},{13,5},{2,10},{6,14},... | collective-permute-start | bytes 6152 | tf_op jit(solution)/shard_map/ppermute | solution.py:664
  27.2 1.9 %collective-permute-start.5 = (s32[8,64]{1,0:T(8,128)}, s32[8,64]{1,0:T(8,128)S(1)}, u32[]{:S(2)}, u32[]{:S(2)}) collective-permute-start(s32[8,64]{1,0:T(8,128)} %land_hbm.1), channel_id=1, source_target_pairs={{0,12},{4,8},{8,4},{12,0},{1,13},{5,9},{9,5},{13,1},{2,14},{6,10},... | collective-permute-start | bytes 6152 | tf_op jit(solution)/shard_map/ppermute | solution.py:664
  29.3 3.5 %collective-permute-done.5.l3_ref = s32[8,64]{1,0:T(8,128)S(1)} collective-permute-done((s32[8,64]{1,0:T(8,128)}, s32[8,64]{1,0:T(8,128)S(1)}, u32[]{:S(2)}, u32[]{:S(2)}) %collective-permute-start.5) | collective-permute-done | bytes 2080 | tf_op jit(solution)/shard_map/ppermute | solution.py:664
  32.8 0.3 shard_map.111
  33.2 1.2 %shard_map.112 = (bf16[34,64,384]{2,1,0:T(8,128)(2,1)S(1)}, bf16[32,64,128]{2,1,0:T(8,128)(2,1)S(1)}, f32[8,128]{1,0:T(8,128)S(1)}) custom-call(bf16[1,8,64,128]{3,2,1,0:T(8,128)(2,1)S(1)} %collective-permute-done.1.f3_ref, bf16[34,64,384]{2,1,0:T(8,128)(2,1)S(1)} %get-tuple-element.36.ss_in, ...), custom_call_target="tpu_custom_call", output_to_operand_aliasing={{0}: (1, {})} | custom-call | flops 603979776 | bytes 5312512 | tf_op jit(solution)/shard_map/pallas_call | solution.py:19
  34.5 1.5 %collective-permute-start.7 = (f32[8,128]{1,0:T(8,128)S(1)}, f32[8,128]{1,0:T(8,128)S(1)}, u32[]{:S(2)}, u32[]{:S(2)}) collective-permute-start(f32[8,128]{1,0:T(8,128)S(1)} %get-tuple-element.40), channel_id=1, source_target_pairs={{0,2},{1,3},{2,0},{3,1},{4,6},{5,7},{6,4},{7,5},{8,10},{9,11},{10,... | collective-permute-start | bytes 12296 | tf_op jit(solution)/shard_map/ppermute | solution.py:310
  36.0 0.3 collective-permute-start.8
  36.3 1.1 %shard_map.114 = (bf16[34,64,384]{2,1,0:T(8,128)(2,1)S(1)}, f32[32,64,128]{2,1,0:T(8,128)S(1)}) custom-call(bf16[1,8,64,128]{3,2,1,0:T(8,128)(2,1)S(1)} %collective-permute-done.10.t3_ref, bf16[32,64,128]{2,1,0:T(8,128)(2,1)S(1)} %get-tuple-element.37.mask_ref, bf16[1536,256]{1,0:T(8,128)(2,1)S(1)} %get-tuple-element.43.wt_ref, ...), custom_call_target="tpu_custom_call", output_to_operand_aliasing={{0}: (3, {})} | custom-call | flops 603979776 | bytes 5832704 | tf_op jit(solution)/shard_map/pallas_call | solution.py:19
  37.4 0.7 %collective-permute-done.7 = f32[8,128]{1,0:T(8,128)S(1)} collective-permute-done((f32[8,128]{1,0:T(8,128)S(1)}, f32[8,128]{1,0:T(8,128)S(1)}, u32[]{:S(2)}, u32[]{:S(2)}) %collective-permute-start.7) | collective-permute-done | bytes 4128 | tf_op jit(solution)/shard_map/ppermute | solution.py:310
  38.1 0.9 %collective-permute-done.8 = f32[8,128]{1,0:T(8,128)S(1)} collective-permute-done((f32[8,128]{1,0:T(8,128)S(1)}, f32[8,128]{1,0:T(8,128)S(1)}, u32[]{:S(2)}, u32[]{:S(2)}) %collective-permute-start.8) | collective-permute-done | bytes 4128 | tf_op jit(solution)/shard_map/ppermute | solution.py:311
  39.0 1.2 %shard_map.115 = (f32[8,128]{1,0:T(8,128)S(1)}, f32[32,64,128]{2,1,0:T(8,128)S(1)}, bf16[34,64,384]{2,1,0:T(8,128)(2,1)S(1)}) custom-call(bf16[32,64,128]{2,1,0:T(8,128)(2,1)S(1)} %get-tuple-element.39.first_ref, bf16[32,64,128]{2,1,0:T(8,128)(2,1)S(1)} %get-tuple-element.37.mask_ref, f32[8,128]{1,0:T(8,128)S(1)} %add_add_fusion.1.stat_ref, ...), custom_call_target="tpu_custom_call" | custom-call | bytes 4829184 | tf_op jit(solution)/shard_map/pallas_call | solution.py:19
  40.5 0.5 %collective-permute-start.13 = (f32[8,128]{1,0:T(8,128)S(1)}, f32[8,128]{1,0:T(8,128)S(1)}, u32[]{:S(2)}, u32[]{:S(2)}) collective-permute-start(f32[8,128]{1,0:T(8,128)S(1)} %get-tuple-element.48), channel_id=1, source_target_pairs={{0,2},{1,3},{2,0},{3,1},{4,6},{5,7},{6,4},{7,5},{8,10},{9,11},{10,... | collective-permute-start | bytes 12296 | tf_op jit(solution)/shard_map/ppermute | solution.py:310
  41.0 1.2 %collective-permute-start.14 = (f32[8,128]{1,0:T(8,128)S(1)}, f32[8,128]{1,0:T(8,128)S(1)}, u32[]{:S(2)}, u32[]{:S(2)}) collective-permute-start(f32[8,128]{1,0:T(8,128)S(1)} %get-tuple-element.48), channel_id=1, source_target_pairs={{0,3},{1,2},{2,1},{3,0},{4,7},{5,6},{6,5},{7,4},{8,11},{9,10},{10,... | collective-permute-start | bytes 12296 | tf_op jit(solution)/shard_map/ppermute | solution.py:311
  42.2 1.0 %shard_map.119 = (bf16[2,9,32,128]{3,2,1,0:T(8,128)(2,1)S(1)}, bf16[2,9,32,128]{3,2,1,0:T(8,128)(2,1)S(1)}) custom-call(bf16[34,64,384]{2,1,0:T(8,128)(2,1)S(1)} %get-tuple-element.46.aa_ref, bf16[34,64,384]{2,1,0:T(8,128)(2,1)S(1)} %get-tuple-element.56.tt_ref, f32[8,128]{1,0:T(8,128)S(1)} %add_add_fusion.1.stat_ref), custom_call_target="tpu_custom_call" | custom-call | flops 603979776 | bytes 3641344 | tf_op jit(solution)/shard_map/pallas_call | solution.py:19
  43.2 0.5 collective-permute-start.17
  43.7 0.4 collective-permute-done.13
  44.1 1.1 %shard_map.116 = (bf16[2,9,32,128]{3,2,1,0:T(8,128)(2,1)S(1)}, bf16[2,9,32,128]{3,2,1,0:T(8,128)(2,1)S(1)}) custom-call(bf16[32,64,128]{2,1,0:T(8,128)(2,1)S(1)} %get-tuple-element.39.first_ref, bf16[32,64,128]{2,1,0:T(8,128)(2,1)S(1)} %get-tuple-element.37.mask_ref, f32[8,128]{1,0:T(8,128)S(1)} %add_add_fusion.1.stat_ref, ...), custom_call_target="tpu_custom_call" | custom-call | flops 603979776 | bytes 4075520 | tf_op jit(solution)/shard_map/pallas_call | solution.py:19
  45.4 1.5 %collective-permute-start.18 = (bf16[1,9,32,128]{3,2,1,0:T(8,128)(2,1)S(1)}, bf16[1,9,32,128]{3,2,1,0:T(8,128)(2,1)S(1)}, u32[]{:S(2)}, u32[]{:S(2)}) collective-permute-start(bf16[1,9,32,128]{3,2,1,0:T(8,128)(2,1)S(1)} %get-tuple-element.60), channel_id=1, source_target_pairs={{0,2},{1,3},{2,0},{3,1},{4,6},{5,7},{6,4},{7,5},{8,10},{9,11},{10,... | collective-permute-start | bytes 221192 | tf_op jit(solution)/shard_map/ppermute | solution.py:517
  47.0 1.2 %collective-permute-start.16 = (bf16[1,9,32,128]{3,2,1,0:T(8,128)(2,1)S(1)}, bf16[1,9,32,128]{3,2,1,0:T(8,128)(2,1)S(1)}, u32[]{:S(2)}, u32[]{:S(2)}) collective-permute-start(bf16[1,9,32,128]{3,2,1,0:T(8,128)(2,1)S(1)} %get-tuple-element.55), channel_id=1, source_target_pairs={{0,2},{1,3},{2,0},{3,1},{4,6},{5,7},{6,4},{7,5},{8,10},{9,11},{10,... | collective-permute-start | bytes 221192 | tf_op jit(solution)/shard_map/ppermute | solution.py:517
  48.2 1.1 %shard_map.118 = (bf16[1,8,64,128]{3,2,1,0:T(8,128)(2,1)}, f32[1,128]{1,0:T(1,128)}, f32[1,128]{1,0:T(1,128)}) custom-call(bf16[34,64,384]{2,1,0:T(8,128)(2,1)S(1)} %get-tuple-element.46.aa_ref, bf16[32,64,128]{2,1,0:T(8,128)(2,1)S(1)} %get-tuple-element.37.mask_ref, bf16[9,128,128]{2,1,0:T(8,128)(2,1)S(1)} %get-tuple-element.47.w_ref, ...), custom_call_target="tpu_custom_call" | custom-call | flops 150994944 | bytes 2700288 | tf_op jit(solution)/shard_map/pallas_call | solution.py:19
  49.3 1.1 %collective-permute-done.18 = bf16[1,9,32,128]{3,2,1,0:T(8,128)(2,1)S(1)} collective-permute-done((bf16[1,9,32,128]{3,2,1,0:T(8,128)(2,1)S(1)}, bf16[1,9,32,128]{3,2,1,0:T(8,128)(2,1)S(1)}, u32[]{:S(2)}, u32[]{:S(2)}) %collective-permute-start.18) | collective-permute-done | bytes 73760 | tf_op jit(solution)/shard_map/ppermute | solution.py:517
  50.4 0.7 %add_bitcast_fusion = f32[9,128,32]{1,2,0:T(8,128)} fusion(bf16[1,9,32,128]{3,2,1,0:T(8,128)(2,1)S(1)} %collective-permute-done.18, bf16[1,9,32,128]{3,2,1,0:T(8,128)(2,1)S(1)} %get-tuple-element.59), kind=kLoop, calls=%fused_computation | loop fusion | flops 110592 | bytes 294912 | tf_op jit(solution)/shard_map/transpose | solution.py:520
  51.1 0.6 %collective-permute-done.16 = bf16[1,9,32,128]{3,2,1,0:T(8,128)(2,1)S(1)} collective-permute-done((bf16[1,9,32,128]{3,2,1,0:T(8,128)(2,1)S(1)}, bf16[1,9,32,128]{3,2,1,0:T(8,128)(2,1)S(1)}, u32[]{:S(2)}, u32[]{:S(2)}) %collective-permute-start.16) | collective-permute-done | bytes 73760 | tf_op jit(solution)/shard_map/ppermute | solution.py:517
  51.6 0.7 %add_bitcast_fusion.1 = f32[9,128,32]{1,2,0:T(8,128)} fusion(bf16[1,9,32,128]{3,2,1,0:T(8,128)(2,1)S(1)} %collective-permute-done.16, bf16[1,9,32,128]{3,2,1,0:T(8,128)(2,1)S(1)} %get-tuple-element.53.after_ref), kind=kLoop, calls=%fused_computation.1 | loop fusion | flops 110592 | bytes 294912 | tf_op jit(solution)/shard_map/transpose | solution.py:520
  (21 shorter events, 1.1 us)
Async XLA Ops:
  0.6 14.4 %collective-permute-start = (bf16[1,8,64,128]{3,2,1,0:T(8,128)(2,1)}, bf16[1,8,64,128]{3,2,1,0:T(8,128)(2,1)S(1)}, u32[]{:S(2)}, u32[]{:S(2)}) collective-permute-start(bf16[1,8,64,128]{3,2,1,0:T(8,128)(2,1)} %f_hbm.1), channel_id=1, source_target_pairs={{0,8},{4,12},{8,0},{12,4},{1,9},{5,13},{9,1},{13,5},{2,10},{6,14},... | collective-permute-start | bytes 393224 | tf_op jit(solution)/shard_map/ppermute | solution.py:664
  6.4 10.6 %collective-permute-start.9 = (bf16[1,8,64,128]{3,2,1,0:T(8,128)(2,1)S(1)}, bf16[1,8,64,128]{3,2,1,0:T(8,128)(2,1)S(1)}, u32[]{:S(2)}, u32[]{:S(2)}) collective-permute-start(bf16[1,8,64,128]{3,2,1,0:T(8,128)(2,1)S(1)} %get-tuple-element.42), channel_id=1, source_target_pairs={{0,8},{4,12},{8,0},{12,4},{1,9},{5,13},{9,1},{13,5},{2,10},{6,14},... | collective-permute-start | bytes 393224 | tf_op jit(solution)/shard_map/ppermute | solution.py:664
  6.5 20.7 %collective-permute-start.11 = (bf16[1,8,64,128]{3,2,1,0:T(8,128)(2,1)S(1)}, bf16[1,8,64,128]{3,2,1,0:T(8,128)(2,1)S(1)}, u32[]{:S(2)}, u32[]{:S(2)}) collective-permute-start(bf16[1,8,64,128]{3,2,1,0:T(8,128)(2,1)S(1)} %get-tuple-element.42), channel_id=1, source_target_pairs={{0,4},{4,0},{8,12},{12,8},{1,5},{5,1},{9,13},{13,9},{2,6},{6,2},{1... | collective-permute-start | bytes 393224 | tf_op jit(solution)/shard_map/ppermute | solution.py:664
  8.4 24.4 %collective-permute-start.2 = (bf16[1,8,64,128]{3,2,1,0:T(8,128)(2,1)}, bf16[1,8,64,128]{3,2,1,0:T(8,128)(2,1)S(1)}, u32[]{:S(2)}, u32[]{:S(2)}) collective-permute-start(bf16[1,8,64,128]{3,2,1,0:T(8,128)(2,1)} %f_hbm.1), channel_id=1, source_target_pairs={{0,4},{4,0},{8,12},{12,8},{1,5},{5,1},{9,13},{13,9},{2,6},{6,2},{1... | collective-permute-start | bytes 393224 | tf_op jit(solution)/shard_map/ppermute | solution.py:664
  15.0 18.1 %collective-permute-start.1 = (bf16[1,8,64,128]{3,2,1,0:T(8,128)(2,1)S(1)}, bf16[1,8,64,128]{3,2,1,0:T(8,128)(2,1)S(1)}, u32[]{:S(2)}, u32[]{:S(2)}) collective-permute-start(bf16[1,8,64,128]{3,2,1,0:T(8,128)(2,1)S(1)} %collective-permute-done.f2_ref), channel_id=1, source_target_pairs={{0,4},{4,0},{8,12},{12,8},{1,5},{5,1},{9,13},{13,9},{2,6},{6,2},{1... | collective-permute-start | bytes 393224 | tf_op jit(solution)/shard_map/ppermute | solution.py:664
  17.0 19.3 %collective-permute-start.10 = (bf16[1,8,64,128]{3,2,1,0:T(8,128)(2,1)S(1)}, bf16[1,8,64,128]{3,2,1,0:T(8,128)(2,1)S(1)}, u32[]{:S(2)}, u32[]{:S(2)}) collective-permute-start(bf16[1,8,64,128]{3,2,1,0:T(8,128)(2,1)S(1)} %collective-permute-done.9.t2_ref), channel_id=1, source_target_pairs={{0,4},{4,0},{8,12},{12,8},{1,5},{5,1},{9,13},{13,9},{2,6},{6,2},{1... | collective-permute-start | bytes 393224 | tf_op jit(solution)/shard_map/ppermute | solution.py:664
  17.7 6.8 %collective-permute-start.3 = (s32[8,64]{1,0:T(8,128)}, s32[8,64]{1,0:T(8,128)S(1)}, u32[]{:S(2)}, u32[]{:S(2)}) collective-permute-start(s32[8,64]{1,0:T(8,128)} %land_hbm.1), channel_id=1, source_target_pairs={{0,4},{4,0},{8,12},{12,8},{1,5},{5,1},{9,13},{13,9},{2,6},{6,2},{1... | collective-permute-start | bytes 6152 | tf_op jit(solution)/shard_map/ppermute | solution.py:664
  24.4 4.8 %collective-permute-start.4 = (s32[8,64]{1,0:T(8,128)}, s32[8,64]{1,0:T(8,128)S(1)}, u32[]{:S(2)}, u32[]{:S(2)}) collective-permute-start(s32[8,64]{1,0:T(8,128)} %land_hbm.1), channel_id=1, source_target_pairs={{0,8},{4,12},{8,0},{12,4},{1,9},{5,13},{9,1},{13,5},{2,10},{6,14},... | collective-permute-start | bytes 6152 | tf_op jit(solution)/shard_map/ppermute | solution.py:664
  27.2 5.6 %collective-permute-start.5 = (s32[8,64]{1,0:T(8,128)}, s32[8,64]{1,0:T(8,128)S(1)}, u32[]{:S(2)}, u32[]{:S(2)}) collective-permute-start(s32[8,64]{1,0:T(8,128)} %land_hbm.1), channel_id=1, source_target_pairs={{0,12},{4,8},{8,4},{12,0},{1,13},{5,9},{9,5},{13,1},{2,14},{6,10},... | collective-permute-start | bytes 6152 | tf_op jit(solution)/shard_map/ppermute | solution.py:664
  34.4 3.0 %collective-permute-start.6 = (f32[8,128]{1,0:T(8,128)S(1)}, f32[8,128]{1,0:T(8,128)S(1)}, u32[]{:S(2)}, u32[]{:S(2)}) collective-permute-start(f32[8,128]{1,0:T(8,128)S(1)} %get-tuple-element.40), channel_id=1, source_target_pairs={{0,1},{1,0},{2,3},{3,2},{4,5},{5,4},{6,7},{7,6},{8,9},{9,8},{10,11... | collective-permute-start | bytes 12296 | tf_op jit(solution)/shard_map/ppermute | solution.py:308
  34.5 3.7 %collective-permute-start.7 = (f32[8,128]{1,0:T(8,128)S(1)}, f32[8,128]{1,0:T(8,128)S(1)}, u32[]{:S(2)}, u32[]{:S(2)}) collective-permute-start(f32[8,128]{1,0:T(8,128)S(1)} %get-tuple-element.40), channel_id=1, source_target_pairs={{0,2},{1,3},{2,0},{3,1},{4,6},{5,7},{6,4},{7,5},{8,10},{9,11},{10,... | collective-permute-start | bytes 12296 | tf_op jit(solution)/shard_map/ppermute | solution.py:310
  36.0 3.0 %collective-permute-start.8 = (f32[8,128]{1,0:T(8,128)S(1)}, f32[8,128]{1,0:T(8,128)S(1)}, u32[]{:S(2)}, u32[]{:S(2)}) collective-permute-start(f32[8,128]{1,0:T(8,128)S(1)} %get-tuple-element.40), channel_id=1, source_target_pairs={{0,3},{1,2},{2,1},{3,0},{4,7},{5,6},{6,5},{7,4},{8,11},{9,10},{10,... | collective-permute-start | bytes 12296 | tf_op jit(solution)/shard_map/ppermute | solution.py:311
  40.3 3.4 %collective-permute-start.12 = (f32[8,128]{1,0:T(8,128)S(1)}, f32[8,128]{1,0:T(8,128)S(1)}, u32[]{:S(2)}, u32[]{:S(2)}) collective-permute-start(f32[8,128]{1,0:T(8,128)S(1)} %get-tuple-element.48), channel_id=1, source_target_pairs={{0,1},{1,0},{2,3},{3,2},{4,5},{5,4},{6,7},{7,6},{8,9},{9,8},{10,11... | collective-permute-start | bytes 12296 | tf_op jit(solution)/shard_map/ppermute | solution.py:308
  40.5 3.6 %collective-permute-start.13 = (f32[8,128]{1,0:T(8,128)S(1)}, f32[8,128]{1,0:T(8,128)S(1)}, u32[]{:S(2)}, u32[]{:S(2)}) collective-permute-start(f32[8,128]{1,0:T(8,128)S(1)} %get-tuple-element.48), channel_id=1, source_target_pairs={{0,2},{1,3},{2,0},{3,1},{4,6},{5,7},{6,4},{7,5},{8,10},{9,11},{10,... | collective-permute-start | bytes 12296 | tf_op jit(solution)/shard_map/ppermute | solution.py:310
  41.0 3.1 %collective-permute-start.14 = (f32[8,128]{1,0:T(8,128)S(1)}, f32[8,128]{1,0:T(8,128)S(1)}, u32[]{:S(2)}, u32[]{:S(2)}) collective-permute-start(f32[8,128]{1,0:T(8,128)S(1)} %get-tuple-element.48), channel_id=1, source_target_pairs={{0,3},{1,2},{2,1},{3,0},{4,7},{5,6},{6,5},{7,4},{8,11},{9,10},{10,... | collective-permute-start | bytes 12296 | tf_op jit(solution)/shard_map/ppermute | solution.py:311
  43.2 2.2 %collective-permute-start.17 = (bf16[2,9,32,128]{3,2,1,0:T(8,128)(2,1)S(1)}, bf16[2,9,32,128]{3,2,1,0:T(8,128)(2,1)S(1)}, u32[]{:S(2)}, u32[]{:S(2)}) collective-permute-start(bf16[2,9,32,128]{3,2,1,0:T(8,128)(2,1)S(1)} %get-tuple-element.58), channel_id=1, source_target_pairs={{0,1},{1,0},{2,3},{3,2},{4,5},{5,4},{6,7},{7,6},{8,9},{9,8},{10,11... | collective-permute-start | bytes 442376 | tf_op jit(solution)/shard_map/ppermute | solution.py:517
  45.2 1.7 %collective-permute-start.15 = (bf16[2,9,32,128]{3,2,1,0:T(8,128)(2,1)S(1)}, bf16[2,9,32,128]{3,2,1,0:T(8,128)(2,1)S(1)}, u32[]{:S(2)}, u32[]{:S(2)}) collective-permute-start(bf16[2,9,32,128]{3,2,1,0:T(8,128)(2,1)S(1)} %get-tuple-element.52), channel_id=1, source_target_pairs={{0,1},{1,0},{2,3},{3,2},{4,5},{5,4},{6,7},{7,6},{8,9},{9,8},{10,11... | collective-permute-start | bytes 442376 | tf_op jit(solution)/shard_map/ppermute | solution.py:517
  45.4 5.0 %collective-permute-start.18 = (bf16[1,9,32,128]{3,2,1,0:T(8,128)(2,1)S(1)}, bf16[1,9,32,128]{3,2,1,0:T(8,128)(2,1)S(1)}, u32[]{:S(2)}, u32[]{:S(2)}) collective-permute-start(bf16[1,9,32,128]{3,2,1,0:T(8,128)(2,1)S(1)} %get-tuple-element.60), channel_id=1, source_target_pairs={{0,2},{1,3},{2,0},{3,1},{4,6},{5,7},{6,4},{7,5},{8,10},{9,11},{10,... | collective-permute-start | bytes 221192 | tf_op jit(solution)/shard_map/ppermute | solution.py:517
  47.0 4.7 %collective-permute-start.16 = (bf16[1,9,32,128]{3,2,1,0:T(8,128)(2,1)S(1)}, bf16[1,9,32,128]{3,2,1,0:T(8,128)(2,1)S(1)}, u32[]{:S(2)}, u32[]{:S(2)}) collective-permute-start(bf16[1,9,32,128]{3,2,1,0:T(8,128)(2,1)S(1)} %get-tuple-element.55), channel_id=1, source_target_pairs={{0,2},{1,3},{2,0},{3,1},{4,6},{5,7},{6,4},{7,5},{8,10},{9,11},{10,... | collective-permute-start | bytes 221192 | tf_op jit(solution)/shard_map/ppermute | solution.py:517

commit v7 on v6

--- a/solution.py
+++ b/solution.py
@@ -436,18 +436,10 @@
     stat_ref[...] = jnp.concatenate(rows + [jnp.zeros((5, chans), F32)], axis=0)
 
 
-def sample_place(lon, t1_ref, t2_ref, tt_in, tt_ref):
-    me = lax.axis_index("space")
-    for k, t_ref in ((1, t1_ref), (2, t2_ref)):
-        start = jnp.bitwise_xor(me, k) * lon
-        for i in range(lon):
-            put_shifted(tt_ref, start + i + 1, t_ref[0, i].astype(F32), -1)
-
-
-def sample_adjoint(lon, lat, chans, t3_ref, mask_ref, wt_ref, tt_in, tt_ref, dact_ref):
+def sample_adjoint(lon, lat, chans, t1_ref, t2_ref, t3_ref, mask_ref, wt_ref, tt_in, tt_ref, dact_ref):
     nx = dact_ref.shape[0]
     me = lax.axis_index("space")
-    for k, t_ref in ((3, t3_ref),):
+    for k, t_ref in ((1, t1_ref), (2, t2_ref), (3, t3_ref)):
         start = jnp.bitwise_xor(me, k) * lon
         for i in range(lon):
             put_shifted(tt_ref, start + i + 1, t_ref[0, i].astype(F32), -1)
@@ -702,9 +694,8 @@
         functools.partial(sample_conv, *sizes), [shifted, cells, sums], [f3, ss, mask, win], flops=work, alias={1: 0}
     )
     stat = all_sum(stat, "batch")
-    (tt,) = run(functools.partial(sample_place, lon), [shifted], [t1, t2, tt], alias={2: 0})
     tt, dact = run(
-        functools.partial(sample_adjoint, *sizes), [shifted, cells_f], [t3, mask, wt, tt], flops=work, alias={3: 0}
+        functools.partial(sample_adjoint, *sizes), [shifted, cells_f], [t1, t2, t3, mask, wt, tt], flops=work, alias={5: 0}
     )
     gsum, dpre, aa = run(
         functools.partial(sample_act, lat, chans), [sums, cells_f, shifted], [first, mask, stat, bn, dact]

time: 52.5 us -> 54.2 us (1.032)
  starting transfers between devices: 20.2 us -> 24.7 us
  waiting for transfers between devices: 21.1 us -> 18.3 us
    ppermute x9, starting transfers between devices: 13 us -> 17.2 us  [sample_body(): move = lambda x, pairs: lax.ppermute(x, 'space', pairs)]
    ppermute x9, waiting for transfers between devices: 17.4 us -> 15.5 us  [sample_body(): move = lambda x, pairs: lax.ppermute(x, 'space', pairs)]
    ppermute x2, starting transfers between devices: 2.1 us -> 3.01 us  [all_sum(): far = lax.ppermute(x, axis, xor_pairs(size, 2 * bit))]
    ppermute x2, waiting for transfers between devices: 0.91 us -> 0.01 us  [all_sum(): both = lax.ppermute(x, axis, xor_pairs(size, 3 * bit))]
    ppermute x2, starting transfers between devices: 1.46 us -> 0.69 us  [all_sum(): both = lax.ppermute(x, axis, xor_pairs(size, 3 * bit))]
    pallas_call x11 -> x10, Pallas kernels: 8.9 us -> 8.85 us  [run(): pl.pallas_call(body, out_shape=list(outs), in_specs=[space] * len(args),...]
  transfers between devices with their start and end apart: 19 -> 19, of which waited for: 9 -> 8; matrix products, arithmetic and copies ran while one was open for 1% -> 1% of each run, Pallas kernels for 15% -> 14%
where the time goes in v7:
time: 54.2 us; the launch traced here: 54 us
  starting transfers between devices  24.7 us (46%)
  waiting for transfers between devices  18.3 us (34%)
  Pallas kernels  8.85 us (16%)
  other arithmetic  1.37 us (3%)
  between operations  0.72 us (1%)
    ppermute x9, starting transfers between devices, sample_body(): move = lambda x, pairs: lax.ppermute(x, 'space', pairs)  17.2 us
    ppermute x9, waiting for transfers between devices, sample_body(): move = lambda x, pairs: lax.ppermute(x, 'space', pairs)  15.5 us
    pallas_call x10, Pallas kernels, run(): pl.pallas_call(body, out_shape=list(outs), in_specs=[space] * len(args),...  8.85 us
    ppermute x4, starting transfers between devices, exchange_sum(): got = lax.ppermute(send, 'batch', xor_pairs(size, bit))  3.51 us
    ppermute x2, starting transfers between devices, all_sum(): far = lax.ppermute(x, axis, xor_pairs(size, 2 * bit))  3.01 us
    ppermute x4, waiting for transfers between devices, exchange_sum(): got = lax.ppermute(send, 'batch', xor_pairs(size, bit))  1.63 us
    transpose x2, other arithmetic, exchange_sum(): return (jnp.swapaxes(keep[0].astype(F32) + got[0].astype(F32), 1, 2), keep)  1.36 us
    ppermute x2, waiting for transfers between devices, all_sum(): far = lax.ppermute(x, axis, xor_pairs(size, 2 * bit))  1.17 us
  transfers between devices with their start and end apart: 19, of which 8 were waited for; matrix products, arithmetic and copies ran while one was open for 1% of the time, Pallas kernels for 14%

profile of v7, /device:TPU:0, one launch (start us, length us, event | category | flops | bytes accessed | tf_op | source)
XLA Modules:
  0.0 54.0 jit_solution(646294131690102255)
XLA Ops:
  0.6 4.1 %collective-permute-start = (bf16[1,8,64,128]{3,2,1,0:T(8,128)(2,1)}, bf16[1,8,64,128]{3,2,1,0:T(8,128)(2,1)S(1)}, u32[]{:S(2)}, u32[]{:S(2)}) collective-permute-start(bf16[1,8,64,128]{3,2,1,0:T(8,128)(2,1)} %f_hbm.1), channel_id=1, source_target_pairs={{0,8},{4,12},{8,0},{12,4},{1,9},{5,13},{9,1},{13,5},{2,10},{6,14},... | collective-permute-start | bytes 393224 | tf_op jit(solution)/shard_map/ppermute | solution.py:656
  4.8 1.6 %shard_map.110 = (bf16[34,64,384]{2,1,0:T(8,128)(2,1)S(1)}, bf16[34,64,384]{2,1,0:T(8,128)(2,1)S(1)}, bf16[32,64,128]{2,1,0:T(8,128)(2,1)S(1)}, bf16[1,8,64,128]...) custom-call(bf16[1,8,64,128]{3,2,1,0:T(8,128)(2,1)} %f_hbm.1, ...), custom_call_target="tpu_custom_call" | custom-call | bytes 6724608 | tf_op jit(solution)/shard_map/pallas_call | solution.py:19
  6.5 1.9 %collective-permute-start.2 = (bf16[1,8,64,128]{3,2,1,0:T(8,128)(2,1)}, bf16[1,8,64,128]{3,2,1,0:T(8,128)(2,1)S(1)}, u32[]{:S(2)}, u32[]{:S(2)}) collective-permute-start(bf16[1,8,64,128]{3,2,1,0:T(8,128)(2,1)} %f_hbm.1), channel_id=1, source_target_pairs={{0,4},{4,0},{8,12},{12,8},{1,5},{5,1},{9,13},{13,9},{2,6},{6,2},{1... | collective-permute-start | bytes 393224 | tf_op jit(solution)/shard_map/ppermute | solution.py:656
  8.4 6.6 %collective-permute-done.f2_ref = bf16[1,8,64,128]{3,2,1,0:T(8,128)(2,1)S(1)} collective-permute-done((bf16[1,8,64,128]{3,2,1,0:T(8,128)(2,1)}, bf16[1,8,64,128]{3,2,1,0:T(8,128)(2,1)S(1)}, u32[]{:S(2)}, u32[]{:S(2)}) %collective-permute-start) | collective-permute-done | bytes 131104 | tf_op jit(solution)/shard_map/ppermute | solution.py:656
  15.1 1.9 %collective-permute-start.9 = (bf16[1,8,64,128]{3,2,1,0:T(8,128)(2,1)S(1)}, bf16[1,8,64,128]{3,2,1,0:T(8,128)(2,1)S(1)}, u32[]{:S(2)}, u32[]{:S(2)}) collective-permute-start(bf16[1,8,64,128]{3,2,1,0:T(8,128)(2,1)S(1)} %get-tuple-element.42), channel_id=1, source_target_pairs={{0,4},{4,0},{8,12},{12,8},{1,5},{5,1},{9,13},{13,9},{2,6},{6,2},{1... | collective-permute-start | bytes 393224 | tf_op jit(solution)/shard_map/ppermute | solution.py:656
  17.0 0.7 %collective-permute-start.11 = (bf16[1,8,64,128]{3,2,1,0:T(8,128)(2,1)S(1)}, bf16[1,8,64,128]{3,2,1,0:T(8,128)(2,1)S(1)}, u32[]{:S(2)}, u32[]{:S(2)}) collective-permute-start(bf16[1,8,64,128]{3,2,1,0:T(8,128)(2,1)S(1)} %collective-permute-done.10.t2_ref), channel_id=1, source_target_pairs={{0,4},{4,0},{8,12},{12,8},{1,5},{5,1},{9,13},{13,9},{2,6},{6,2},{1... | collective-permute-start | bytes 393224 | tf_op jit(solution)/shard_map/ppermute | solution.py:656
  17.7 3.4 %collective-permute-start.4 = (s32[8,64]{1,0:T(8,128)}, s32[8,64]{1,0:T(8,128)S(1)}, u32[]{:S(2)}, u32[]{:S(2)}) collective-permute-start(s32[8,64]{1,0:T(8,128)} %land_hbm.1), channel_id=1, source_target_pairs={{0,8},{4,12},{8,0},{12,4},{1,9},{5,13},{9,1},{13,5},{2,10},{6,14},... | collective-permute-start | bytes 6152 | tf_op jit(solution)/shard_map/ppermute | solution.py:656
  21.1 2.5 %collective-permute-done.4.l2_ref = s32[8,64]{1,0:T(8,128)S(1)} collective-permute-done((s32[8,64]{1,0:T(8,128)}, s32[8,64]{1,0:T(8,128)S(1)}, u32[]{:S(2)}, u32[]{:S(2)}) %collective-permute-start.4) | collective-permute-done | bytes 2080 | tf_op jit(solution)/shard_map/ppermute | solution.py:656
  23.6 4.0 %collective-permute-start.3 = (s32[8,64]{1,0:T(8,128)}, s32[8,64]{1,0:T(8,128)S(1)}, u32[]{:S(2)}, u32[]{:S(2)}) collective-permute-start(s32[8,64]{1,0:T(8,128)} %land_hbm.1), channel_id=1, source_target_pairs={{0,4},{4,0},{8,12},{12,8},{1,5},{5,1},{9,13},{13,9},{2,6},{6,2},{1... | collective-permute-start | bytes 6152 | tf_op jit(solution)/shard_map/ppermute | solution.py:656
  27.6 1.8 %collective-permute-done.3.l1_ref = s32[8,64]{1,0:T(8,128)S(1)} collective-permute-done((s32[8,64]{1,0:T(8,128)}, s32[8,64]{1,0:T(8,128)S(1)}, u32[]{:S(2)}, u32[]{:S(2)}) %collective-permute-start.3) | collective-permute-done | bytes 2080 | tf_op jit(solution)/shard_map/ppermute | solution.py:656
  29.4 1.0 %collective-permute-start.5 = (s32[8,64]{1,0:T(8,128)}, s32[8,64]{1,0:T(8,128)S(1)}, u32[]{:S(2)}, u32[]{:S(2)}) collective-permute-start(s32[8,64]{1,0:T(8,128)} %land_hbm.1), channel_id=1, source_target_pairs={{0,12},{4,8},{8,4},{12,0},{1,13},{5,9},{9,5},{13,1},{2,14},{6,10},... | collective-permute-start | bytes 6152 | tf_op jit(solution)/shard_map/ppermute | solution.py:656
  30.4 4.6 %collective-permute-done.5.l3_ref = s32[8,64]{1,0:T(8,128)S(1)} collective-permute-done((s32[8,64]{1,0:T(8,128)}, s32[8,64]{1,0:T(8,128)S(1)}, u32[]{:S(2)}, u32[]{:S(2)}) %collective-permute-start.5) | collective-permute-done | bytes 2080 | tf_op jit(solution)/shard_map/ppermute | solution.py:656
  35.0 0.3 shard_map.111
  35.4 1.2 %shard_map.112 = (bf16[34,64,384]{2,1,0:T(8,128)(2,1)S(1)}, bf16[32,64,128]{2,1,0:T(8,128)(2,1)S(1)}, f32[8,128]{1,0:T(8,128)S(1)}) custom-call(bf16[1,8,64,128]{3,2,1,0:T(8,128)(2,1)S(1)} %collective-permute-done.1.f3_ref, bf16[34,64,384]{2,1,0:T(8,128)(2,1)S(1)} %get-tuple-element.36.ss_in, ...), custom_call_target="tpu_custom_call", output_to_operand_aliasing={{0}: (1, {})} | custom-call | flops 603979776 | bytes 5312512 | tf_op jit(solution)/shard_map/pallas_call | solution.py:19
  36.7 1.6 %collective-permute-start.7 = (f32[8,128]{1,0:T(8,128)S(1)}, f32[8,128]{1,0:T(8,128)S(1)}, u32[]{:S(2)}, u32[]{:S(2)}) collective-permute-start(f32[8,128]{1,0:T(8,128)S(1)} %get-tuple-element.40), channel_id=1, source_target_pairs={{0,2},{1,3},{2,0},{3,1},{4,6},{5,7},{6,4},{7,5},{8,10},{9,11},{10,... | collective-permute-start | bytes 12296 | tf_op jit(solution)/shard_map/ppermute | solution.py:310
  38.2 0.3 collective-permute-start.6
  38.5 1.2 %shard_map.113 = (bf16[34,64,384]{2,1,0:T(8,128)(2,1)S(1)}, f32[32,64,128]{2,1,0:T(8,128)S(1)}) custom-call(bf16[1,8,64,128]{3,2,1,0:T(8,128)(2,1)S(1)} %collective-permute-done.9.t1_ref, bf16[1,8,64,128]{3,2,1,0:T(8,128)(2,1)S(1)} %collective-permute-done.10.t2_ref, ...), custom_call_target="tpu_custom_call", output_to_operand_aliasing={{0}: (5, {})} | custom-call | flops 603979776 | bytes 6094848 | tf_op jit(solution)/shard_map/pallas_call | solution.py:19
  39.8 0.6 %collective-permute-done.7 = f32[8,128]{1,0:T(8,128)S(1)} collective-permute-done((f32[8,128]{1,0:T(8,128)S(1)}, f32[8,128]{1,0:T(8,128)S(1)}, u32[]{:S(2)}, u32[]{:S(2)}) %collective-permute-start.7) | collective-permute-done | bytes 4128 | tf_op jit(solution)/shard_map/ppermute | solution.py:310
  40.4 1.2 %shard_map.114 = (f32[8,128]{1,0:T(8,128)S(1)}, f32[32,64,128]{2,1,0:T(8,128)S(1)}, bf16[34,64,384]{2,1,0:T(8,128)(2,1)S(1)}) custom-call(bf16[32,64,128]{2,1,0:T(8,128)(2,1)S(1)} %get-tuple-element.39.first_ref, bf16[32,64,128]{2,1,0:T(8,128)(2,1)S(1)} %get-tuple-element.37.mask_ref, f32[8,128]{1,0:T(8,128)S(1)} %add_add_fusion.1.stat_ref, ...), custom_call_target="tpu_custom_call" | custom-call | bytes 4829184 | tf_op jit(solution)/shard_map/pallas_call | solution.py:19
  41.6 0.6 %collective-permute-start.14 = (f32[8,128]{1,0:T(8,128)S(1)}, f32[8,128]{1,0:T(8,128)S(1)}, u32[]{:S(2)}, u32[]{:S(2)}) collective-permute-start(f32[8,128]{1,0:T(8,128)S(1)} %get-tuple-element.48), channel_id=1, source_target_pairs={{0,3},{1,2},{2,1},{3,0},{4,7},{5,6},{6,5},{7,4},{8,11},{9,10},{10,... | collective-permute-start | bytes 12296 | tf_op jit(solution)/shard_map/ppermute | solution.py:311
  42.2 1.5 %collective-permute-start.13 = (f32[8,128]{1,0:T(8,128)S(1)}, f32[8,128]{1,0:T(8,128)S(1)}, u32[]{:S(2)}, u32[]{:S(2)}) collective-permute-start(f32[8,128]{1,0:T(8,128)S(1)} %get-tuple-element.48), channel_id=1, source_target_pairs={{0,2},{1,3},{2,0},{3,1},{4,6},{5,7},{6,4},{7,5},{8,10},{9,11},{10,... | collective-permute-start | bytes 12296 | tf_op jit(solution)/shard_map/ppermute | solution.py:310
  43.7 1.0 %shard_map.118 = (bf16[2,9,32,128]{3,2,1,0:T(8,128)(2,1)S(1)}, bf16[2,9,32,128]{3,2,1,0:T(8,128)(2,1)S(1)}) custom-call(bf16[34,64,384]{2,1,0:T(8,128)(2,1)S(1)} %get-tuple-element.46.aa_ref, bf16[34,64,384]{2,1,0:T(8,128)(2,1)S(1)} %get-tuple-element.56.tt_ref, f32[8,128]{1,0:T(8,128)S(1)} %add_add_fusion.1.stat_ref), custom_call_target="tpu_custom_call" | custom-call | flops 603979776 | bytes 3641344 | tf_op jit(solution)/shard_map/pallas_call | solution.py:19
  44.6 0.6 %collective-permute-start.17 = (bf16[2,9,32,128]{3,2,1,0:T(8,128)(2,1)S(1)}, bf16[2,9,32,128]{3,2,1,0:T(8,128)(2,1)S(1)}, u32[]{:S(2)}, u32[]{:S(2)}) collective-permute-start(bf16[2,9,32,128]{3,2,1,0:T(8,128)(2,1)S(1)} %get-tuple-element.58), channel_id=1, source_target_pairs={{0,1},{1,0},{2,3},{3,2},{4,5},{5,4},{6,7},{7,6},{8,9},{9,8},{10,11... | collective-permute-start | bytes 442376 | tf_op jit(solution)/shard_map/ppermute | solution.py:509
  45.2 0.6 %collective-permute-done.13 = f32[8,128]{1,0:T(8,128)S(1)} collective-permute-done((f32[8,128]{1,0:T(8,128)S(1)}, f32[8,128]{1,0:T(8,128)S(1)}, u32[]{:S(2)}, u32[]{:S(2)}) %collective-permute-start.13) | collective-permute-done | bytes 4128 | tf_op jit(solution)/shard_map/ppermute | solution.py:310
  45.8 1.1 %shard_map.115 = (bf16[2,9,32,128]{3,2,1,0:T(8,128)(2,1)S(1)}, bf16[2,9,32,128]{3,2,1,0:T(8,128)(2,1)S(1)}) custom-call(bf16[32,64,128]{2,1,0:T(8,128)(2,1)S(1)} %get-tuple-element.39.first_ref, bf16[32,64,128]{2,1,0:T(8,128)(2,1)S(1)} %get-tuple-element.37.mask_ref, f32[8,128]{1,0:T(8,128)S(1)} %add_add_fusion.1.stat_ref, ...), custom_call_target="tpu_custom_call" | custom-call | flops 603979776 | bytes 4075520 | tf_op jit(solution)/shard_map/pallas_call | solution.py:19
  47.1 1.5 %collective-permute-start.18 = (bf16[1,9,32,128]{3,2,1,0:T(8,128)(2,1)S(1)}, bf16[1,9,32,128]{3,2,1,0:T(8,128)(2,1)S(1)}, u32[]{:S(2)}, u32[]{:S(2)}) collective-permute-start(bf16[1,9,32,128]{3,2,1,0:T(8,128)(2,1)S(1)} %get-tuple-element.60), channel_id=1, source_target_pairs={{0,2},{1,3},{2,0},{3,1},{4,6},{5,7},{6,4},{7,5},{8,10},{9,11},{10,... | collective-permute-start | bytes 221192 | tf_op jit(solution)/shard_map/ppermute | solution.py:509
  48.6 1.3 %collective-permute-start.16 = (bf16[1,9,32,128]{3,2,1,0:T(8,128)(2,1)S(1)}, bf16[1,9,32,128]{3,2,1,0:T(8,128)(2,1)S(1)}, u32[]{:S(2)}, u32[]{:S(2)}) collective-permute-start(bf16[1,9,32,128]{3,2,1,0:T(8,128)(2,1)S(1)} %get-tuple-element.55), channel_id=1, source_target_pairs={{0,2},{1,3},{2,0},{3,1},{4,6},{5,7},{6,4},{7,5},{8,10},{9,11},{10,... | collective-permute-start | bytes 221192 | tf_op jit(solution)/shard_map/ppermute | solution.py:509
  49.9 1.1 %shard_map.117 = (bf16[1,8,64,128]{3,2,1,0:T(8,128)(2,1)}, f32[1,128]{1,0:T(1,128)}, f32[1,128]{1,0:T(1,128)}) custom-call(bf16[34,64,384]{2,1,0:T(8,128)(2,1)S(1)} %get-tuple-element.46.aa_ref, bf16[32,64,128]{2,1,0:T(8,128)(2,1)S(1)} %get-tuple-element.37.mask_ref, bf16[9,128,128]{2,1,0:T(8,128)(2,1)S(1)} %get-tuple-element.47.w_ref, ...), custom_call_target="tpu_custom_call" | custom-call | flops 150994944 | bytes 2700288 | tf_op jit(solution)/shard_map/pallas_call | solution.py:19
  51.0 1.0 %collective-permute-done.18 = bf16[1,9,32,128]{3,2,1,0:T(8,128)(2,1)S(1)} collective-permute-done((bf16[1,9,32,128]{3,2,1,0:T(8,128)(2,1)S(1)}, bf16[1,9,32,128]{3,2,1,0:T(8,128)(2,1)S(1)}, u32[]{:S(2)}, u32[]{:S(2)}) %collective-permute-start.18) | collective-permute-done | bytes 73760 | tf_op jit(solution)/shard_map/ppermute | solution.py:509
  52.1 0.7 %add_bitcast_fusion = f32[9,128,32]{1,2,0:T(8,128)} fusion(bf16[1,9,32,128]{3,2,1,0:T(8,128)(2,1)S(1)} %collective-permute-done.18, bf16[1,9,32,128]{3,2,1,0:T(8,128)(2,1)S(1)} %get-tuple-element.59), kind=kLoop, calls=%fused_computation | loop fusion | flops 110592 | bytes 294912 | tf_op jit(solution)/shard_map/transpose | solution.py:512
  52.7 0.6 %collective-permute-done.16 = bf16[1,9,32,128]{3,2,1,0:T(8,128)(2,1)S(1)} collective-permute-done((bf16[1,9,32,128]{3,2,1,0:T(8,128)(2,1)S(1)}, bf16[1,9,32,128]{3,2,1,0:T(8,128)(2,1)S(1)}, u32[]{:S(2)}, u32[]{:S(2)}) %collective-permute-start.16) | collective-permute-done | bytes 73760 | tf_op jit(solution)/shard_map/ppermute | solution.py:509
  53.4 0.7 %add_bitcast_fusion.1 = f32[9,128,32]{1,2,0:T(8,128)} fusion(bf16[1,9,32,128]{3,2,1,0:T(8,128)(2,1)S(1)} %collective-permute-done.16, bf16[1,9,32,128]{3,2,1,0:T(8,128)(2,1)S(1)} %get-tuple-element.53.after_ref), kind=kLoop, calls=%fused_computation.1 | loop fusion | flops 110592 | bytes 294912 | tf_op jit(solution)/shard_map/transpose | solution.py:512
  (20 shorter events, 0.6 us)
Async XLA Ops:
  0.6 14.3 %collective-permute-start = (bf16[1,8,64,128]{3,2,1,0:T(8,128)(2,1)}, bf16[1,8,64,128]{3,2,1,0:T(8,128)(2,1)S(1)}, u32[]{:S(2)}, u32[]{:S(2)}) collective-permute-start(bf16[1,8,64,128]{3,2,1,0:T(8,128)(2,1)} %f_hbm.1), channel_id=1, source_target_pairs={{0,8},{4,12},{8,0},{12,4},{1,9},{5,13},{9,1},{13,5},{2,10},{6,14},... | collective-permute-start | bytes 393224 | tf_op jit(solution)/shard_map/ppermute | solution.py:656
  6.4 10.6 %collective-permute-start.10 = (bf16[1,8,64,128]{3,2,1,0:T(8,128)(2,1)S(1)}, bf16[1,8,64,128]{3,2,1,0:T(8,128)(2,1)S(1)}, u32[]{:S(2)}, u32[]{:S(2)}) collective-permute-start(bf16[1,8,64,128]{3,2,1,0:T(8,128)(2,1)S(1)} %get-tuple-element.42), channel_id=1, source_target_pairs={{0,8},{4,12},{8,0},{12,4},{1,9},{5,13},{9,1},{13,5},{2,10},{6,14},... | collective-permute-start | bytes 393224 | tf_op jit(solution)/shard_map/ppermute | solution.py:656
  6.5 28.6 %collective-permute-start.2 = (bf16[1,8,64,128]{3,2,1,0:T(8,128)(2,1)}, bf16[1,8,64,128]{3,2,1,0:T(8,128)(2,1)S(1)}, u32[]{:S(2)}, u32[]{:S(2)}) collective-permute-start(bf16[1,8,64,128]{3,2,1,0:T(8,128)(2,1)} %f_hbm.1), channel_id=1, source_target_pairs={{0,4},{4,0},{8,12},{12,8},{1,5},{5,1},{9,13},{13,9},{2,6},{6,2},{1... | collective-permute-start | bytes 393224 | tf_op jit(solution)/shard_map/ppermute | solution.py:656
  14.9 20.4 %collective-permute-start.1 = (bf16[1,8,64,128]{3,2,1,0:T(8,128)(2,1)S(1)}, bf16[1,8,64,128]{3,2,1,0:T(8,128)(2,1)S(1)}, u32[]{:S(2)}, u32[]{:S(2)}) collective-permute-start(bf16[1,8,64,128]{3,2,1,0:T(8,128)(2,1)S(1)} %collective-permute-done.f2_ref), channel_id=1, source_target_pairs={{0,4},{4,0},{8,12},{12,8},{1,5},{5,1},{9,13},{13,9},{2,6},{6,2},{1... | collective-permute-start | bytes 393224 | tf_op jit(solution)/shard_map/ppermute | solution.py:656
  15.1 23.5 %collective-permute-start.9 = (bf16[1,8,64,128]{3,2,1,0:T(8,128)(2,1)S(1)}, bf16[1,8,64,128]{3,2,1,0:T(8,128)(2,1)S(1)}, u32[]{:S(2)}, u32[]{:S(2)}) collective-permute-start(bf16[1,8,64,128]{3,2,1,0:T(8,128)(2,1)S(1)} %get-tuple-element.42), channel_id=1, source_target_pairs={{0,4},{4,0},{8,12},{12,8},{1,5},{5,1},{9,13},{13,9},{2,6},{6,2},{1... | collective-permute-start | bytes 393224 | tf_op jit(solution)/shard_map/ppermute | solution.py:656
  17.0 21.5 %collective-permute-start.11 = (bf16[1,8,64,128]{3,2,1,0:T(8,128)(2,1)S(1)}, bf16[1,8,64,128]{3,2,1,0:T(8,128)(2,1)S(1)}, u32[]{:S(2)}, u32[]{:S(2)}) collective-permute-start(bf16[1,8,64,128]{3,2,1,0:T(8,128)(2,1)S(1)} %collective-permute-done.10.t2_ref), channel_id=1, source_target_pairs={{0,4},{4,0},{8,12},{12,8},{1,5},{5,1},{9,13},{13,9},{2,6},{6,2},{1... | collective-permute-start | bytes 393224 | tf_op jit(solution)/shard_map/ppermute | solution.py:656
  17.7 5.9 %collective-permute-start.4 = (s32[8,64]{1,0:T(8,128)}, s32[8,64]{1,0:T(8,128)S(1)}, u32[]{:S(2)}, u32[]{:S(2)}) collective-permute-start(s32[8,64]{1,0:T(8,128)} %land_hbm.1), channel_id=1, source_target_pairs={{0,8},{4,12},{8,0},{12,4},{1,9},{5,13},{9,1},{13,5},{2,10},{6,14},... | collective-permute-start | bytes 6152 | tf_op jit(solution)/shard_map/ppermute | solution.py:656
  23.6 5.8 %collective-permute-start.3 = (s32[8,64]{1,0:T(8,128)}, s32[8,64]{1,0:T(8,128)S(1)}, u32[]{:S(2)}, u32[]{:S(2)}) collective-permute-start(s32[8,64]{1,0:T(8,128)} %land_hbm.1), channel_id=1, source_target_pairs={{0,4},{4,0},{8,12},{12,8},{1,5},{5,1},{9,13},{13,9},{2,6},{6,2},{1... | collective-permute-start | bytes 6152 | tf_op jit(solution)/shard_map/ppermute | solution.py:656
  29.4 5.6 %collective-permute-start.5 = (s32[8,64]{1,0:T(8,128)}, s32[8,64]{1,0:T(8,128)S(1)}, u32[]{:S(2)}, u32[]{:S(2)}) collective-permute-start(s32[8,64]{1,0:T(8,128)} %land_hbm.1), channel_id=1, source_target_pairs={{0,12},{4,8},{8,4},{12,0},{1,13},{5,9},{9,5},{13,1},{2,14},{6,10},... | collective-permute-start | bytes 6152 | tf_op jit(solution)/shard_map/ppermute | solution.py:656
  36.6 3.2 %collective-permute-start.8 = (f32[8,128]{1,0:T(8,128)S(1)}, f32[8,128]{1,0:T(8,128)S(1)}, u32[]{:S(2)}, u32[]{:S(2)}) collective-permute-start(f32[8,128]{1,0:T(8,128)S(1)} %get-tuple-element.40), channel_id=1, source_target_pairs={{0,3},{1,2},{2,1},{3,0},{4,7},{5,6},{6,5},{7,4},{8,11},{9,10},{10,... | collective-permute-start | bytes 12296 | tf_op jit(solution)/shard_map/ppermute | solution.py:311
  36.7 3.7 %collective-permute-start.7 = (f32[8,128]{1,0:T(8,128)S(1)}, f32[8,128]{1,0:T(8,128)S(1)}, u32[]{:S(2)}, u32[]{:S(2)}) collective-permute-start(f32[8,128]{1,0:T(8,128)S(1)} %get-tuple-element.40), channel_id=1, source_target_pairs={{0,2},{1,3},{2,0},{3,1},{4,6},{5,7},{6,4},{7,5},{8,10},{9,11},{10,... | collective-permute-start | bytes 12296 | tf_op jit(solution)/shard_map/ppermute | solution.py:310
  38.2 2.1 %collective-permute-start.6 = (f32[8,128]{1,0:T(8,128)S(1)}, f32[8,128]{1,0:T(8,128)S(1)}, u32[]{:S(2)}, u32[]{:S(2)}) collective-permute-start(f32[8,128]{1,0:T(8,128)S(1)} %get-tuple-element.40), channel_id=1, source_target_pairs={{0,1},{1,0},{2,3},{3,2},{4,5},{5,4},{6,7},{7,6},{8,9},{9,8},{10,11... | collective-permute-start | bytes 12296 | tf_op jit(solution)/shard_map/ppermute | solution.py:308
  41.6 3.6 %collective-permute-start.14 = (f32[8,128]{1,0:T(8,128)S(1)}, f32[8,128]{1,0:T(8,128)S(1)}, u32[]{:S(2)}, u32[]{:S(2)}) collective-permute-start(f32[8,128]{1,0:T(8,128)S(1)} %get-tuple-element.48), channel_id=1, source_target_pairs={{0,3},{1,2},{2,1},{3,0},{4,7},{5,6},{6,5},{7,4},{8,11},{9,10},{10,... | collective-permute-start | bytes 12296 | tf_op jit(solution)/shard_map/ppermute | solution.py:311
  42.2 3.6 %collective-permute-start.13 = (f32[8,128]{1,0:T(8,128)S(1)}, f32[8,128]{1,0:T(8,128)S(1)}, u32[]{:S(2)}, u32[]{:S(2)}) collective-permute-start(f32[8,128]{1,0:T(8,128)S(1)} %get-tuple-element.48), channel_id=1, source_target_pairs={{0,2},{1,3},{2,0},{3,1},{4,6},{5,7},{6,4},{7,5},{8,10},{9,11},{10,... | collective-permute-start | bytes 12296 | tf_op jit(solution)/shard_map/ppermute | solution.py:310
  43.7 2.2 %collective-permute-start.12 = (f32[8,128]{1,0:T(8,128)S(1)}, f32[8,128]{1,0:T(8,128)S(1)}, u32[]{:S(2)}, u32[]{:S(2)}) collective-permute-start(f32[8,128]{1,0:T(8,128)S(1)} %get-tuple-element.48), channel_id=1, source_target_pairs={{0,1},{1,0},{2,3},{3,2},{4,5},{5,4},{6,7},{7,6},{8,9},{9,8},{10,11... | collective-permute-start | bytes 12296 | tf_op jit(solution)/shard_map/ppermute | solution.py:308
  44.6 2.5 %collective-permute-start.17 = (bf16[2,9,32,128]{3,2,1,0:T(8,128)(2,1)S(1)}, bf16[2,9,32,128]{3,2,1,0:T(8,128)(2,1)S(1)}, u32[]{:S(2)}, u32[]{:S(2)}) collective-permute-start(bf16[2,9,32,128]{3,2,1,0:T(8,128)(2,1)S(1)} %get-tuple-element.58), channel_id=1, source_target_pairs={{0,1},{1,0},{2,3},{3,2},{4,5},{5,4},{6,7},{7,6},{8,9},{9,8},{10,11... | collective-permute-start | bytes 442376 | tf_op jit(solution)/shard_map/ppermute | solution.py:509
  46.9 1.7 %collective-permute-start.15 = (bf16[2,9,32,128]{3,2,1,0:T(8,128)(2,1)S(1)}, bf16[2,9,32,128]{3,2,1,0:T(8,128)(2,1)S(1)}, u32[]{:S(2)}, u32[]{:S(2)}) collective-permute-start(bf16[2,9,32,128]{3,2,1,0:T(8,128)(2,1)S(1)} %get-tuple-element.52), channel_id=1, source_target_pairs={{0,1},{1,0},{2,3},{3,2},{4,5},{5,4},{6,7},{7,6},{8,9},{9,8},{10,11... | collective-permute-start | bytes 442376 | tf_op jit(solution)/shard_map/ppermute | solution.py:509
  47.1 4.9 %collective-permute-start.18 = (bf16[1,9,32,128]{3,2,1,0:T(8,128)(2,1)S(1)}, bf16[1,9,32,128]{3,2,1,0:T(8,128)(2,1)S(1)}, u32[]{:S(2)}, u32[]{:S(2)}) collective-permute-start(bf16[1,9,32,128]{3,2,1,0:T(8,128)(2,1)S(1)} %get-tuple-element.60), channel_id=1, source_target_pairs={{0,2},{1,3},{2,0},{3,1},{4,6},{5,7},{6,4},{7,5},{8,10},{9,11},{10,... | collective-permute-start | bytes 221192 | tf_op jit(solution)/shard_map/ppermute | solution.py:509
  48.6 4.7 %collective-permute-start.16 = (bf16[1,9,32,128]{3,2,1,0:T(8,128)(2,1)S(1)}, bf16[1,9,32,128]{3,2,1,0:T(8,128)(2,1)S(1)}, u32[]{:S(2)}, u32[]{:S(2)}) collective-permute-start(bf16[1,9,32,128]{3,2,1,0:T(8,128)(2,1)S(1)} %get-tuple-element.55), channel_id=1, source_target_pairs={{0,2},{1,3},{2,0},{3,1},{4,6},{5,7},{6,4},{7,5},{8,10},{9,11},{10,... | collective-permute-start | bytes 221192 | tf_op jit(solution)/shard_map/ppermute | solution.py:509
